TPU v7x, 32 devices: a whole 2x2x4 slice. The times are simulated.
32 devices in a mesh: seq: 2 (over x), fsdp: 16 (over z, y, core).
Axes of the slice: x: 2, y: 2, z: 4, core: 2. Of those that a mesh axis runs over, the one named last changes fastest.
Arguments:
- tokens: bfloat16 [16, 2048, 768], P('fsdp', 'seq'), may hold values from -13 to 13
- lengths: int32 [16, 16], P('fsdp'), may hold values from 0 to 2048, as said below
- block_order: int32 [16, 16], P('fsdp'), may hold values from 0 to 15, each once within a row
- qkv_weight: bfloat16 [768, 2304], P(('seq', 'fsdp')), may hold values from -0.21875 to 0.21875
- query_bias: bfloat16 [768], P(('seq', 'fsdp')), may hold values from -3 to 3
- value_bias: bfloat16 [768], P(('seq', 'fsdp')), may hold values from -3 to 3
- out_weight: bfloat16 [768, 768], P(('seq', 'fsdp')), may hold values from -0.875 to 0.875
- out_bias: bfloat16 [768], P(('seq', 'fsdp')), may hold values from -3 to 3
- norm1_gain: bfloat16 [768], P(('seq', 'fsdp')), may hold values from 0.099609375 to 1.8984375
- norm1_shift: bfloat16 [768], P(('seq', 'fsdp')), may hold values from -3 to 3
- in_weight: bfloat16 [768, 3072], P(('seq', 'fsdp')), may hold values from -0.21875 to 0.21875
- in_bias: bfloat16 [3072], P(('seq', 'fsdp')), may hold values from -3 to 3
- down_weight: bfloat16 [3072, 768], P(('seq', 'fsdp')), may hold values from -0.109375 to 0.109375
- down_bias: bfloat16 [768], P(('seq', 'fsdp')), may hold values from -3 to 3
- norm2_gain: bfloat16 [768], P(('seq', 'fsdp')), may hold values from 0.099609375 to 1.8984375
- norm2_shift: bfloat16 [768], P(('seq', 'fsdp')), may hold values from -3 to 3
- cotangent: bfloat16 [16, 2048, 768], P('fsdp', 'seq'), may hold values from -6 to 6
Outputs:
- output: bfloat16 [16, 2048, 768], P('fsdp', 'seq')
- input_grad: bfloat16 [16, 2048, 768], P('fsdp', 'seq')
- qkv_weight_grad: float32 [768, 2304], P(('seq', 'fsdp'))
- query_bias_grad: float32 [768], P(('seq', 'fsdp'))
- value_bias_grad: float32 [768], P(('seq', 'fsdp'))
- out_weight_grad: float32 [768, 768], P(('seq', 'fsdp'))
- out_bias_grad: float32 [768], P(('seq', 'fsdp'))
- norm1_gain_grad: float32 [768], P(('seq', 'fsdp'))
- norm1_shift_grad: float32 [768], P(('seq', 'fsdp'))
- in_weight_grad: float32 [768, 3072], P(('seq', 'fsdp'))
- in_bias_grad: float32 [3072], P(('seq', 'fsdp'))
- down_weight_grad: float32 [3072, 768], P(('seq', 'fsdp'))
- down_bias_grad: float32 [768], P(('seq', 'fsdp'))
- norm2_gain_grad: float32 [768], P(('seq', 'fsdp'))
- norm2_shift_grad: float32 [768], P(('seq', 'fsdp'))
Inputs may be any that keep to these rules, and one draw needn't show every extreme that they name: Each row holds the lengths of one group's packed sequences in order, at most 4 of them, multiples of 128, followed by zeros, and sums to 2048; in every draw some group holds one sequence of 2048 tokens. `block_order`: each row is a permutation of the numbers 0 to 15.
All inputs are finite; a program needn't handle non-finite values.
Results may differ from a plain program's by a relative error of at most 0.015.
Values may be sent and summed in bfloat16 or wider, within the bound.
No kernel may reach another device: no remote copies, remote signals or barrier semaphores. Data moves between devices by JAX's collectives and lax.ppermute only.
A program may use at most 256 MiB of HBM per device.

v0:
```python
import jax
import jax.numpy as jnp
from jax import lax
from jax.sharding import PartitionSpec as P

D = 768
H = 12
HD = 64
UNITS = 16


norm_eps = 1e-12


def layer_norm(values, norm_gain, norm_shift):
    row_mean = jnp.mean(values, axis=-1, keepdims=True)
    centered = values - row_mean
    row_var = jnp.mean(centered * centered, axis=-1, keepdims=True)
    return centered * lax.rsqrt(row_var + norm_eps) * norm_gain + norm_shift


def exact_gelu(values):
    return jax.nn.gelu(values, approximate=False)


def segment_ids(length_row, length_all):
    seq_ends = jnp.cumsum(length_row)
    places = jnp.arange(length_all, dtype=jnp.int32)
    return jnp.sum((places[:, None] >= seq_ends[None, :]).astype(jnp.int32), axis=1)


def dot_left(left_rows, right_rows):
    return lax.dot_general(
        left_rows, right_rows, (((0,), (0,)), ((), ())), preferred_element_type=jnp.float32
    )


def dot_right(left_rows, right_rows):
    return lax.dot_general(
        left_rows, right_rows, (((1,), (1,)), ((), ())), preferred_element_type=jnp.float32
    )


def pick_blocks(whole_rows, block_ids, unit_rows):
    width = whole_rows.shape[1]
    blocks = whole_rows.reshape(whole_rows.shape[0] // unit_rows, unit_rows, width)
    return jnp.take(blocks, block_ids, axis=0).reshape(block_ids.shape[0] * unit_rows, width)


def local(
    tokens,
    lengths,
    block_order,
    qkv_weight,
    query_bias,
    value_bias,
    out_weight,
    out_bias,
    norm1_gain,
    norm1_shift,
    in_weight,
    in_bias,
    down_weight,
    down_bias,
    norm2_gain,
    norm2_shift,
    cotangent,
):
    tok_count = tokens.shape[1]
    pair_size = lax.axis_size("seq")
    seq_place = lax.axis_index("seq")
    units_dev = UNITS // pair_size
    order_row = block_order[0]
    own_order = lax.dynamic_slice_in_dim(order_row, seq_place * units_dev, units_dev)
    slot_ids = jnp.arange(UNITS, dtype=jnp.int32)
    inverse_order = jnp.sum(
        slot_ids[:, None] * (order_row[:, None] == slot_ids[None, :]).astype(jnp.int32), axis=0
    )
    own_inverse = lax.dynamic_slice_in_dim(inverse_order, seq_place * units_dev, units_dev)
    arrived_rows, arrived_back = (
        lax.all_gather(tokens[0], "seq", axis=0, tiled=True),
        lax.all_gather(cotangent[0], "seq", axis=0, tiled=True),
    )
    unit_rows = arrived_rows.shape[0] // UNITS
    tok_rows = pick_blocks(arrived_rows, own_order, unit_rows)
    back_rows = pick_blocks(arrived_back, own_order, unit_rows)
    weights_now = (
        lax.all_gather(qkv_weight, ("seq", "fsdp"), axis=0, tiled=True),
        lax.all_gather(query_bias, ("seq", "fsdp"), axis=0, tiled=True),
        lax.all_gather(value_bias, ("seq", "fsdp"), axis=0, tiled=True),
        lax.all_gather(out_weight, ("seq", "fsdp"), axis=0, tiled=True),
        lax.all_gather(out_bias, ("seq", "fsdp"), axis=0, tiled=True),
        lax.all_gather(norm1_gain, ("seq", "fsdp"), axis=0, tiled=True),
        lax.all_gather(norm1_shift, ("seq", "fsdp"), axis=0, tiled=True),
        lax.all_gather(in_weight, ("seq", "fsdp"), axis=0, tiled=True),
        lax.all_gather(in_bias, ("seq", "fsdp"), axis=0, tiled=True),
        lax.all_gather(down_weight, ("seq", "fsdp"), axis=0, tiled=True),
        lax.all_gather(down_bias, ("seq", "fsdp"), axis=0, tiled=True),
        lax.all_gather(norm2_gain, ("seq", "fsdp"), axis=0, tiled=True),
        lax.all_gather(norm2_shift, ("seq", "fsdp"), axis=0, tiled=True),
    )
    (
        qkv_full,
        query_full,
        value_full,
        out_full,
        out_bias_full,
        first_gain,
        first_shift,
        in_full,
        in_bias_full,
        down_full,
        down_bias_full,
        second_gain,
        second_shift,
    ) = weights_now
    head_local = H // pair_size
    head_width = head_local * HD
    score_scale = HD ** (-0.5)
    qkv_bias = jnp.concatenate([query_full, jnp.zeros_like(query_full), value_full]).astype(
        jnp.float32
    )
    qkv_local = (jnp.dot(tok_rows, qkv_full, preferred_element_type=jnp.float32) + qkv_bias).astype(
        jnp.bfloat16
    )
    qkv_heads = lax.all_to_all(
        qkv_local.reshape(tok_count, 3, pair_size, head_width),
        "seq",
        split_axis=2,
        concat_axis=0,
        tiled=True,
    )
    group_len = qkv_heads.shape[0]
    block_rows = min(512, group_len)
    block_count = group_len // block_rows
    query_rows = qkv_heads[:, 0, 0].reshape(group_len, head_local, HD)
    key_rows = qkv_heads[:, 1, 0].reshape(group_len, head_local, HD)
    value_rows = qkv_heads[:, 2, 0].reshape(group_len, head_local, HD)
    segment_all = segment_ids(lengths[0], group_len)
    query_blocks = query_rows.reshape(block_count, block_rows, head_local, HD)
    segment_blocks = segment_all.reshape(block_count, block_rows)

    def attend(block_items):
        query_block, segment_block = block_items
        scores = (
            jnp.einsum("qhd,khd->hqk", query_block, key_rows, preferred_element_type=jnp.float32)
            * score_scale
        )
        same_doc = (segment_block[:, None] == segment_all[None, :])[None]
        scores = jnp.where(same_doc, scores, -1e30)
        row_max = jnp.max(scores, axis=-1, keepdims=True)
        exponent = jnp.exp(scores - row_max)
        row_total = jnp.sum(exponent, axis=-1, keepdims=True)
        soft_weights = (exponent / row_total).astype(jnp.bfloat16)
        head_out = jnp.einsum(
            "hqk,khd->qhd", soft_weights, value_rows, preferred_element_type=jnp.float32
        )
        return (head_out.astype(jnp.bfloat16), (row_max + jnp.log(row_total))[:, :, 0])

    head_blocks, lse_blocks = lax.map(attend, (query_blocks, segment_blocks))
    head_rows = head_blocks.reshape(group_len, 1, head_width)
    mixed_heads = lax.all_to_all(head_rows, "seq", split_axis=0, concat_axis=1, tiled=True).reshape(
        tok_count, D
    )
    attn_out = jnp.dot(
        mixed_heads, out_full, preferred_element_type=jnp.float32
    ) + out_bias_full.astype(jnp.float32)
    resid_one = tok_rows.astype(jnp.float32) + attn_out
    hidden_one, norm_one_back = jax.vjp(
        layer_norm, resid_one, first_gain.astype(jnp.float32), first_shift.astype(jnp.float32)
    )
    hidden_low = hidden_one.astype(jnp.bfloat16)
    ffn_inner = jnp.dot(
        hidden_low, in_full, preferred_element_type=jnp.float32
    ) + in_bias_full.astype(jnp.float32)
    act_full, gelu_back = jax.vjp(exact_gelu, ffn_inner)
    ffn_act = act_full.astype(jnp.bfloat16)
    branch = jnp.dot(
        ffn_act, down_full, preferred_element_type=jnp.float32
    ) + down_bias_full.astype(jnp.float32)
    output_rows, norm_two_back = jax.vjp(
        layer_norm,
        hidden_one + branch,
        second_gain.astype(jnp.float32),
        second_shift.astype(jnp.float32),
    )
    weights_back = (
        lax.all_gather(qkv_weight, ("seq", "fsdp"), axis=0, tiled=True),
        lax.all_gather(query_bias, ("seq", "fsdp"), axis=0, tiled=True),
        lax.all_gather(value_bias, ("seq", "fsdp"), axis=0, tiled=True),
        lax.all_gather(out_weight, ("seq", "fsdp"), axis=0, tiled=True),
        lax.all_gather(out_bias, ("seq", "fsdp"), axis=0, tiled=True),
        lax.all_gather(norm1_gain, ("seq", "fsdp"), axis=0, tiled=True),
        lax.all_gather(norm1_shift, ("seq", "fsdp"), axis=0, tiled=True),
        lax.all_gather(in_weight, ("seq", "fsdp"), axis=0, tiled=True),
        lax.all_gather(in_bias, ("seq", "fsdp"), axis=0, tiled=True),
        lax.all_gather(down_weight, ("seq", "fsdp"), axis=0, tiled=True),
        lax.all_gather(down_bias, ("seq", "fsdp"), axis=0, tiled=True),
        lax.all_gather(norm2_gain, ("seq", "fsdp"), axis=0, tiled=True),
        lax.all_gather(norm2_shift, ("seq", "fsdp"), axis=0, tiled=True),
    )
    qkv_back = weights_back[0]
    out_back = weights_back[3]
    in_back = weights_back[7]
    down_back = weights_back[9]
    resid_two_grad, second_gain_grad, second_shift_grad = norm_two_back(
        back_rows.astype(jnp.float32)
    )
    branch_grad = resid_two_grad.astype(jnp.bfloat16)
    down_bias_grad = jnp.sum(branch_grad.astype(jnp.float32), axis=0)
    down_weight_grad = dot_left(ffn_act, branch_grad)
    act_grad = dot_right(branch_grad, down_back)
    (inner_full,) = gelu_back(act_grad)
    inner_grad = inner_full.astype(jnp.bfloat16)
    in_bias_grad = jnp.sum(inner_grad.astype(jnp.float32), axis=0)
    in_weight_grad = dot_left(hidden_low, inner_grad)
    hidden_grad = resid_two_grad + dot_right(inner_grad, in_back)
    resid_one_grad, first_gain_grad, first_shift_grad = norm_one_back(hidden_grad)
    attn_grad = resid_one_grad.astype(jnp.bfloat16)
    out_bias_grad = jnp.sum(attn_grad.astype(jnp.float32), axis=0)
    out_weight_grad = dot_left(mixed_heads, attn_grad)
    mixed_grad = dot_right(attn_grad, out_back).astype(jnp.bfloat16)
    head_grad = lax.all_to_all(
        mixed_grad.reshape(tok_count, pair_size, head_width),
        "seq",
        split_axis=1,
        concat_axis=0,
        tiled=True,
    )
    head_grad = head_grad.reshape(block_count, block_rows, head_local, HD)

    def attend_back(carried, block_items):
        key_grad, value_grad = carried
        query_block, segment_block, out_grad, lse_block = block_items
        scores = (
            jnp.einsum("qhd,khd->hqk", query_block, key_rows, preferred_element_type=jnp.float32)
            * score_scale
        )
        same_doc = (segment_block[:, None] == segment_all[None, :])[None]
        soft_weights = jnp.where(same_doc, jnp.exp(scores - lse_block[:, :, None]), 0.0)
        value_grad = value_grad + jnp.einsum(
            "hqk,qhd->khd",
            soft_weights.astype(jnp.bfloat16),
            out_grad,
            preferred_element_type=jnp.float32,
        )
        weight_grad = jnp.einsum(
            "qhd,khd->hqk", out_grad, value_rows, preferred_element_type=jnp.float32
        )
        row_dot = jnp.sum(soft_weights * weight_grad, axis=-1, keepdims=True)
        score_grad = (soft_weights * (weight_grad - row_dot)).astype(jnp.bfloat16)
        query_grad = (
            jnp.einsum("hqk,khd->qhd", score_grad, key_rows, preferred_element_type=jnp.float32)
            * score_scale
        )
        key_grad = (
            key_grad
            + jnp.einsum(
                "hqk,qhd->khd", score_grad, query_block, preferred_element_type=jnp.float32
            )
            * score_scale
        )
        return ((key_grad, value_grad), query_grad)

    zero_heads = jnp.zeros((group_len, head_local, HD), jnp.float32)
    (key_grad, value_grad), query_grads = lax.scan(
        attend_back, (zero_heads, zero_heads), (query_blocks, segment_blocks, head_grad, lse_blocks)
    )
    qkv_grad_heads = jnp.stack(
        [
            query_grads.reshape(group_len, head_width),
            key_grad.reshape(group_len, head_width),
            value_grad.reshape(group_len, head_width),
        ],
        axis=1,
    ).astype(jnp.bfloat16)
    qkv_grad = lax.all_to_all(
        qkv_grad_heads[:, :, None, :], "seq", split_axis=0, concat_axis=2, tiled=True
    ).reshape(tok_count, 3 * D)
    qkv_sums = jnp.sum(qkv_grad.astype(jnp.float32), axis=0)
    query_bias_grad = qkv_sums[:D]
    value_bias_grad = qkv_sums[2 * D :]
    qkv_weight_grad = dot_left(tok_rows, qkv_grad)
    packed_grad = (resid_one_grad + dot_right(qkv_grad, qkv_back)).astype(jnp.bfloat16)
    packed_out_all, packed_grad_all = (
        lax.all_gather(output_rows.astype(jnp.bfloat16), "seq", axis=0, tiled=True),
        lax.all_gather(packed_grad, "seq", axis=0, tiled=True),
    )
    output_local = pick_blocks(packed_out_all, own_inverse, unit_rows)
    input_grad = pick_blocks(packed_grad_all, own_inverse, unit_rows)
    shares = (
        lax.psum_scatter(qkv_weight_grad, ("seq", "fsdp"), scatter_dimension=0, tiled=True),
        lax.psum_scatter(query_bias_grad, ("seq", "fsdp"), scatter_dimension=0, tiled=True),
        lax.psum_scatter(value_bias_grad, ("seq", "fsdp"), scatter_dimension=0, tiled=True),
        lax.psum_scatter(out_weight_grad, ("seq", "fsdp"), scatter_dimension=0, tiled=True),
        lax.psum_scatter(out_bias_grad, ("seq", "fsdp"), scatter_dimension=0, tiled=True),
        lax.psum_scatter(first_gain_grad, ("seq", "fsdp"), scatter_dimension=0, tiled=True),
        lax.psum_scatter(first_shift_grad, ("seq", "fsdp"), scatter_dimension=0, tiled=True),
        lax.psum_scatter(in_weight_grad, ("seq", "fsdp"), scatter_dimension=0, tiled=True),
        lax.psum_scatter(in_bias_grad, ("seq", "fsdp"), scatter_dimension=0, tiled=True),
        lax.psum_scatter(down_weight_grad, ("seq", "fsdp"), scatter_dimension=0, tiled=True),
        lax.psum_scatter(down_bias_grad, ("seq", "fsdp"), scatter_dimension=0, tiled=True),
        lax.psum_scatter(second_gain_grad, ("seq", "fsdp"), scatter_dimension=0, tiled=True),
        lax.psum_scatter(second_shift_grad, ("seq", "fsdp"), scatter_dimension=0, tiled=True),
    )
    return (
        output_local[None],
        input_grad[None],
        shares[0],
        shares[1],
        shares[2],
        shares[3],
        shares[4],
        shares[5],
        shares[6],
        shares[7],
        shares[8],
        shares[9],
        shares[10],
        shares[11],
        shares[12],
    )


def solution(mesh):
    placed = (
        P("fsdp", "seq", None),
        P("fsdp", None),
        P("fsdp", None),
        P(("seq", "fsdp"), None),
        P(("seq", "fsdp")),
        P(("seq", "fsdp")),
        P(("seq", "fsdp"), None),
        P(("seq", "fsdp")),
        P(("seq", "fsdp")),
        P(("seq", "fsdp")),
        P(("seq", "fsdp"), None),
        P(("seq", "fsdp")),
        P(("seq", "fsdp"), None),
        P(("seq", "fsdp")),
        P(("seq", "fsdp")),
        P(("seq", "fsdp")),
        P("fsdp", "seq", None),
    )
    return jax.shard_map(
        local,
        mesh=mesh,
        in_specs=placed,
        out_specs=(
            P("fsdp", "seq", None),
            P("fsdp", "seq", None),
            P(("seq", "fsdp"), None),
            P(("seq", "fsdp")),
            P(("seq", "fsdp")),
            P(("seq", "fsdp"), None),
            P(("seq", "fsdp")),
            P(("seq", "fsdp")),
            P(("seq", "fsdp")),
            P(("seq", "fsdp"), None),
            P(("seq", "fsdp")),
            P(("seq", "fsdp"), None),
            P(("seq", "fsdp")),
            P(("seq", "fsdp")),
            P(("seq", "fsdp")),
        ),
        check_vma=False,
    )
```

profile of v0, /device:TPU:1, one launch (start us, length us, event | category | flops | bytes accessed | tf_op | source)
XLA Modules:
  0.0 1652.0 jit_solution(4438718923494278183)
XLA Ops:
  12.4 43.5 %all-reduce.19 = (bf16[768]{0:T(1024)(128)(2,1)S(1)}, bf16[768]{0:T(1024)(128)(2,1)S(1)}, bf16[768]{0:T(1024)(128)(2,1)}, bf16[768]{0:T(1024)(128)(2,1)}, bf16[7...) all-reduce(bf16[768]{0:T(1024)(128)(2,1)S(1)} %dynamic-update-slice, ...), channel_id=1, replica_groups=mesh['seq'=2,'fsdp'=16] {'seq','fsdp'}, use_global_device_ids=true, to_apply=%add.1 | all-reduce | flops 9216 | bytes 36864
  60.0 44.0 %all-gather.23.cloned.1.call-done = bf16[1,2048,768]{2,1,0:T(8,128)(2,1)} async-done(((bf16[1,1024,768]{2,1,0:T(8,128)(2,1)}), bf16[1,2048,768]{2,1,0:T(8,128)(2,1)}) %all-gather.23.cloned.1.call-update) | async-done | bytes 3145744 | tf_op jit(solution)/shard_map/all_gather | solution.py:81
  111.2 56.3 %all-gather.11.cloned.1.call-done = bf16[768,2304]{1,0:T(8,128)(2,1)} async-done(((bf16[24,2304]{1,0:T(8,128)(2,1)}), bf16[768,2304]{1,0:T(8,128)(2,1)}) %all-gather.11.cloned.1.call-update) | async-done | bytes 3538960 | tf_op jit(solution)/shard_map/all_gather | solution.py:88
  196.8 55.0 %all-to-all-done = bf16[1024,3,2,384]{3,0,1,2:T(8,128)(2,1)} async-done(((bf16[1024,3,2,384]{3,0,1,2:T(8,128)(2,1)}), bf16[1024,3,2,384]{3,0,1,2:T(8,128)(2,1)}, u32[]{:S(2)}, u32[]{:S(2)}) %all-to-all-start) | async-done | bytes 4718624 | tf_op jit(solution)/shard_map/all_to_all | solution.py:126
  265.0 148.8 %while.27 = (s32[]{:T(128)}, bf16[4,512,6,64]{1,3,2,0:T(8,128)(2,1)}, f32[4,6,512]{2,1,0:T(8,128)}, s32[4,512]{1,0:T(4,128)S(1)}, s32[2048]{0:T(1024)S(1)}, /*in...) while((s32[]{:T(128)}, ...), condition=%wide.region_5.7_spmd, body=%wide.region_2.6_spmd.sunk | while | flops 1687352320 | bytes 83742304 | solution.py:160
  290.4 12.2 fusion.109
  327.5 12.2 fusion.109
  401.6 12.2 fusion.109
  418.7 15.4 reshape.334
  449.9 14.6 all-to-all-done.1
  480.1 37.7 %multiply_convert_fusion.1 = (bf16[1024,3072]{1,0:T(8,128)(2,1)}, f32[1024,3072]{1,0:T(8,128)}, f32[1024,3072]{1,0:T(8,128)}) fusion(f32[3072]{0:T(1024)S(1)} %convert_element_type.115, bf16[768,3072]{1,0:T(8,128)(2,1)} %all-gather.15.cloned.1.call-done, f32[1024,768]{0,1:T(8,128)} %copy-done.6, f32[768]{0:T(1024)S(1)} %convert_element_type.113, ...), kind=kOutput, calls=%fused_computation.56 | convolution fusion | flops 5043388416 | bytes 39348224 | tf_op jit(solution)/shard_map/dot_general | solution.py:173
  534.5 19.1 %convert_reduce_fusion = (f32[3072]{0:T(1024)}, bf16[1024,3072]{1,0:T(8,128)(2,1)}) fusion(f32[1024,3072]{1,0:T(8,128)} %get-tuple-element.345, bf16[1024,768]{0,1:T(8,128)(2,1)} %get-tuple-element.335, bf16[3072,768]{1,0:T(8,128)(2,1)} %all-gather.17.cloned.1.call-done, f32[1024,3072]{1,0:T(8,128)} %get-tuple-element.364, f32[3072]{0:T(1024)S(1)} %convert_element_type.115), kind=kOutput, calls=%fused_computation.54 | convolution fusion | flops 4885312512 | bytes 37773312 | tf_op jit(solution)/shard_map/dot_general | solution.py:39
  573.2 17.5 %all-to-all-done.2 = bf16[1024,2,384]{0,2,1:T(8,128)(2,1)S(1)} async-done(((bf16[1024,2,384]{0,2,1:T(8,128)(2,1)}), bf16[1024,2,384]{0,2,1:T(8,128)(2,1)S(1)}, u32[]{:S(2)}, u32[]{:S(2)}) %all-to-all-start.2) | async-done | bytes 1572896 | tf_op jit(solution)/shard_map/all_to_all | solution.py:223
  597.1 338.5 %while.28 = (s32[]{:T(128)}, f32[2048,6,64]{0,2,1:T(8,128)}, f32[2048,6,64]{0,2,1:T(8,128)}, bf16[4,512,6,64]{1,3,2,0:T(8,128)(2,1)}, bf16[4,512,6,64]{1,3,2,0:T...) while((s32[]{:T(128)}, f32[2048,6,64]{0,2,1:T(8,128)}, ...), condition=%wide.region_17.19_spmd.clone, body=%wide.region_15.18_spmd.clone.sunk | while | flops 4126077952 | bytes 212701840 | solution.py:266
  610.4 18.2 %multiply_reduce_fusion.8 = (f32[6,512]{1,0:T(8,128)S(1)}, f32[6,512,2048]{2,1,0:T(8,128)}) fusion(f32[6,512,2048]{2,1,0:T(8,128)} %fusion.119, f32[6,512]{1,0:T(8,128)S(1)} %dynamic-slice_bitcast_fusion.2, pred[512,2048]{1,0:T(8,128)(4,1)S(1)} %broadcast_compare_fusion.5, bf16[2048,6,64]{0,2,1:T(8,128)(2,1)} %get-tuple-element.557, ...), kind=kOutput, calls=%fused_computation.23.clone.1 | convolution fusion | flops 836760576 | bytes 53371392 | tf_op jit(solution)/shard_map/while/body/eval_jaxpr/qhd,khd->hqk/dot_general | solution.py:247
  628.6 21.2 %multiply_convert_fusion.3 = bf16[6,512,2048]{2,1,0:T(8,128)(2,1)} fusion(f32[6,512,2048]{2,1,0:T(8,128)} %get-tuple-element.492, f32[6,512,2048]{2,1,0:T(8,128)} %fusion.119, f32[6,512]{1,0:T(8,128)S(1)} %get-tuple-element.493, f32[6,512]{1,0:T(8,128)S(1)} %dynamic-slice_bitcast_fusion.2, pred[512,2048]{1,0:T(8,128)(4,1)S(1)} %broadcast_compare_fusion.5), kind=kLoop, calls=%fused_computation.22.clone.1 | loop fusion | flops 37748736 | bytes 63987712 | tf_op jit(solution)/shard_map/while/body/eval_jaxpr/convert_element_type | solution.py:251
  667.8 12.3 bitcast_add_fusion.5
  693.2 18.2 %multiply_reduce_fusion.8 = (f32[6,512]{1,0:T(8,128)S(1)}, f32[6,512,2048]{2,1,0:T(8,128)}) fusion(f32[6,512,2048]{2,1,0:T(8,128)} %fusion.119, f32[6,512]{1,0:T(8,128)S(1)} %dynamic-slice_bitcast_fusion.2, pred[512,2048]{1,0:T(8,128)(4,1)S(1)} %broadcast_compare_fusion.5, bf16[2048,6,64]{0,2,1:T(8,128)(2,1)} %get-tuple-element.557, ...), kind=kOutput, calls=%fused_computation.23.clone.1 | convolution fusion | flops 836760576 | bytes 53371392 | tf_op jit(solution)/shard_map/while/body/eval_jaxpr/qhd,khd->hqk/dot_general | solution.py:247
  711.4 21.2 %multiply_convert_fusion.3 = bf16[6,512,2048]{2,1,0:T(8,128)(2,1)} fusion(f32[6,512,2048]{2,1,0:T(8,128)} %get-tuple-element.492, f32[6,512,2048]{2,1,0:T(8,128)} %fusion.119, f32[6,512]{1,0:T(8,128)S(1)} %get-tuple-element.493, f32[6,512]{1,0:T(8,128)S(1)} %dynamic-slice_bitcast_fusion.2, pred[512,2048]{1,0:T(8,128)(4,1)S(1)} %broadcast_compare_fusion.5), kind=kLoop, calls=%fused_computation.22.clone.1 | loop fusion | flops 37748736 | bytes 63987712 | tf_op jit(solution)/shard_map/while/body/eval_jaxpr/convert_element_type | solution.py:251
  751.5 13.7 bitcast_add_fusion.5
  778.3 18.2 %multiply_reduce_fusion.8 = (f32[6,512]{1,0:T(8,128)S(1)}, f32[6,512,2048]{2,1,0:T(8,128)}) fusion(f32[6,512,2048]{2,1,0:T(8,128)} %fusion.119, f32[6,512]{1,0:T(8,128)S(1)} %dynamic-slice_bitcast_fusion.2, pred[512,2048]{1,0:T(8,128)(4,1)S(1)} %broadcast_compare_fusion.5, bf16[2048,6,64]{0,2,1:T(8,128)(2,1)} %get-tuple-element.557, ...), kind=kOutput, calls=%fused_computation.23.clone.1 | convolution fusion | flops 836760576 | bytes 53371392 | tf_op jit(solution)/shard_map/while/body/eval_jaxpr/qhd,khd->hqk/dot_general | solution.py:247
  796.5 21.2 %multiply_convert_fusion.3 = bf16[6,512,2048]{2,1,0:T(8,128)(2,1)} fusion(f32[6,512,2048]{2,1,0:T(8,128)} %get-tuple-element.492, f32[6,512,2048]{2,1,0:T(8,128)} %fusion.119, f32[6,512]{1,0:T(8,128)S(1)} %get-tuple-element.493, f32[6,512]{1,0:T(8,128)S(1)} %dynamic-slice_bitcast_fusion.2, pred[512,2048]{1,0:T(8,128)(4,1)S(1)} %broadcast_compare_fusion.5), kind=kLoop, calls=%fused_computation.22.clone.1 | loop fusion | flops 37748736 | bytes 63987712 | tf_op jit(solution)/shard_map/while/body/eval_jaxpr/convert_element_type | solution.py:251
  836.6 13.7 bitcast_add_fusion.5
  863.5 18.2 %multiply_reduce_fusion.8 = (f32[6,512]{1,0:T(8,128)S(1)}, f32[6,512,2048]{2,1,0:T(8,128)}) fusion(f32[6,512,2048]{2,1,0:T(8,128)} %fusion.119, f32[6,512]{1,0:T(8,128)S(1)} %dynamic-slice_bitcast_fusion.2, pred[512,2048]{1,0:T(8,128)(4,1)S(1)} %broadcast_compare_fusion.5, bf16[2048,6,64]{0,2,1:T(8,128)(2,1)} %get-tuple-element.557, ...), kind=kOutput, calls=%fused_computation.23.clone.1 | convolution fusion | flops 836760576 | bytes 53371392 | tf_op jit(solution)/shard_map/while/body/eval_jaxpr/qhd,khd->hqk/dot_general | solution.py:247
  881.6 21.2 %multiply_convert_fusion.3 = bf16[6,512,2048]{2,1,0:T(8,128)(2,1)} fusion(f32[6,512,2048]{2,1,0:T(8,128)} %get-tuple-element.492, f32[6,512,2048]{2,1,0:T(8,128)} %fusion.119, f32[6,512]{1,0:T(8,128)S(1)} %get-tuple-element.493, f32[6,512]{1,0:T(8,128)S(1)} %dynamic-slice_bitcast_fusion.2, pred[512,2048]{1,0:T(8,128)(4,1)S(1)} %broadcast_compare_fusion.5), kind=kLoop, calls=%fused_computation.22.clone.1 | loop fusion | flops 37748736 | bytes 63987712 | tf_op jit(solution)/shard_map/while/body/eval_jaxpr/convert_element_type | solution.py:251
  921.7 13.7 bitcast_add_fusion.5
  965.7 100.2 %all-to-all-done.3 = bf16[2048,3,1,384]{3,1,2,0:T(4,128)(2,1)} async-done(((bf16[2048,3,1,384]{3,1,2,0:T(4,128)(2,1)}), bf16[2048,3,1,384]{3,1,2,0:T(4,128)(2,1)}, u32[]{:S(2)}, u32[]{:S(2)}) %all-to-all-start.3) | async-done | bytes 4718624 | tf_op jit(solution)/shard_map/all_to_all | solution.py:277
  1129.5 41.9 %all-reduce.18 = (f32[768]{0:T(1024)S(1)}, f32[768]{0:T(1024)S(1)}, f32[768]{0:T(1024)S(1)}, f32[768]{0:T(1024)S(1)}, f32[768]{0:T(1024)S(1)}, /*index=5*/f32[30...) all-reduce(f32[768]{0:T(1024)S(1)} %slice.25, ...), channel_id=5, replica_groups=mesh['seq'=2,'fsdp'=16] {'seq','fsdp'}, use_global_device_ids=true, to_apply=%region_20.22.clone | all-reduce | flops 9216 | bytes 73728
  1190.9 46.1 %reduce-scatter.7.cloned.1.call-done = f32[24,768]{1,0:T(8,128)} async-done(((f32[768,768]{1,0:T(8,128)}), f32[24,768]{1,0:T(8,128)}) %reduce-scatter.7.cloned.1.call-update) | async-done | bytes 73744 | tf_op jit(solution)/shard_map/reduce_scatter | solution.py:295
  1237.0 141.4 %reduce-scatter.11.cloned.1.call-done = f32[96,768]{1,0:T(8,128)} async-done(((f32[3072,768]{1,0:T(8,128)}), f32[96,768]{1,0:T(8,128)}) %reduce-scatter.11.cloned.1.call-update) | async-done | bytes 294928 | tf_op jit(solution)/shard_map/reduce_scatter | solution.py:301
  1378.4 141.7 %reduce-scatter.9.cloned.1.call-done = f32[24,3072]{1,0:T(8,128)} async-done(((f32[768,3072]{1,0:T(8,128)}), f32[24,3072]{1,0:T(8,128)}) %reduce-scatter.9.cloned.1.call-update) | async-done | bytes 294928 | tf_op jit(solution)/shard_map/reduce_scatter | solution.py:299
  1520.0 124.7 %reduce-scatter.5.cloned.1.call-done = f32[24,2304]{1,0:T(8,128)} async-done(((f32[768,2304]{1,0:T(8,128)}), f32[24,2304]{1,0:T(8,128)}) %reduce-scatter.5.cloned.1.call-update) | async-done | bytes 221200 | tf_op jit(solution)/shard_map/reduce_scatter | solution.py:292
  (320 shorter events, 489.4 us)
Async XLA Ops:
  7.3 50.2 %all-gather.25.cloned.1.call-start = ((), (), s32[]{:S(2)}) async-start(), calls=%async_computation.19 | async-start | bytes 4718592 | tf_op jit(solution)/shard_map/all_gather | solution.py:82
  8.0 96.0 %all-gather.23.cloned.1.call-start = ((), (), s32[]{:S(2)}) async-start(), calls=%async_computation.18 | async-start | bytes 4718592 | tf_op jit(solution)/shard_map/all_gather | solution.py:81
  8.8 158.7 %all-gather.11.cloned.1.call-start = ((), (), s32[]{:S(2)}) async-start(), calls=%async_computation.8 | async-start | bytes 3649536 | tf_op jit(solution)/shard_map/all_gather | solution.py:88
  9.5 464.4 %all-gather.13.cloned.1.call-start = ((), (), s32[]{:S(2)}) async-start(), calls=%async_computation.9 | async-start | bytes 1216512 | tf_op jit(solution)/shard_map/all_gather | solution.py:91
  10.2 97.5 %copy-start.36 = (pred[8]{0:T(512)(128)(4,1)}, pred[8]{0:T(512)(128)(4,1)S(1)}, u32[]{:S(2)}) copy-start(pred[8]{0:T(512)(128)(4,1)S(1)} %get-tuple-element.346) | copy-start | bytes 28
  60.0 51.2 %copy-start.4 = (bf16[8,128,768]{2,1,0:T(8,128)(2,1)}, bf16[8,128,768]{2,1,0:T(8,128)(2,1)S(1)}, u32[]{:S(2)}) copy-start(bf16[8,128,768]{2,1,0:T(8,128)(2,1)S(1)} %gather_fusion.2) | copy-start | bytes 4718596
  111.2 63.7 %copy-start.14 = (bf16[8,128,768]{2,1,0:T(8,128)(2,1)}, bf16[8,128,768]{2,1,0:T(8,128)(2,1)S(1)}, u32[]{:S(2)}) copy-start(bf16[8,128,768]{2,1,0:T(8,128)(2,1)S(1)} %get-tuple-element.361) | copy-start | bytes 4718596
  189.8 61.9 %all-to-all-start = ((bf16[1024,3,2,384]{3,0,1,2:T(8,128)(2,1)}), bf16[1024,3,2,384]{3,0,1,2:T(8,128)(2,1)}, u32[]{:S(2)}, u32[]{:S(2)}) async-start(bf16[1024,3,2,384]{3,0,1,2:T(8,128)(2,1)} %copy.148), calls=%async_computation | async-start | bytes 9437184 | tf_op jit(solution)/shard_map/all_to_all | solution.py:126
  195.8 284.3 %all-gather.15.cloned.1.call-start = ((), (), s32[]{:S(2)}) async-start(), calls=%async_computation.10 | async-start | bytes 4866048 | tf_op jit(solution)/shard_map/all_gather | solution.py:95
  413.8 20.4 %copy-start = (bf16[2048,6,64]{0,2,1:T(8,128)(2,1)}, bf16[2048,6,64]{0,2,1:T(8,128)(2,1)S(1)}, u32[]{:S(2)}) copy-start(bf16[2048,6,64]{0,2,1:T(8,128)(2,1)S(1)} %get-tuple-element.572) | copy-start | bytes 4718596
  413.8 20.4 %copy-start.3 = (bf16[2048,6,64]{0,2,1:T(8,128)(2,1)}, bf16[2048,6,64]{0,2,1:T(8,128)(2,1)S(1)}, u32[]{:S(2)}) copy-start(bf16[2048,6,64]{0,2,1:T(8,128)(2,1)S(1)} %get-tuple-element.573) | copy-start | bytes 4718596
  413.8 20.4 %copy-start.20 = (s32[2048]{0:T(1024)}, s32[2048]{0:T(1024)S(1)}, u32[]{:S(2)}) copy-start(s32[2048]{0:T(1024)S(1)} %get-tuple-element.597) | copy-start | bytes 24580
  413.8 20.4 %copy-start.22 = (s32[4,512]{1,0:T(4,128)}, s32[4,512]{1,0:T(4,128)S(1)}, u32[]{:S(2)}) copy-start(s32[4,512]{1,0:T(4,128)S(1)} %get-tuple-element.606) | copy-start | bytes 24580
  438.9 6.8 copy-start.42
  438.9 6.8 copy-start.15
  440.3 24.1 %all-to-all-start.1 = ((bf16[2,2,196608]{2,1,0:T(2,128)(2,1)}), bf16[2,2,196608]{2,1,0:T(2,128)(2,1)}, u32[]{:S(2)}, u32[]{:S(2)}) async-start(bf16[2,2,196608]{2,1,0:T(2,128)(2,1)} %reshape.410), calls=%async_computation.1 | async-start | bytes 3145728 | tf_op jit(solution)/shard_map/all_to_all | solution.py:162
  445.0 72.8 %all-gather.17.cloned.1.call-start = ((), (), s32[]{:S(2)}) async-start(), calls=%async_computation.11 | async-start | bytes 4866048 | tf_op jit(solution)/shard_map/all_gather | solution.py:97
  445.7 118.3 %copy-start.25 = (f32[768]{0:T(1024)}, f32[768]{0:T(1024)S(1)}, u32[]{:S(2)}) copy-start(f32[768]{0:T(1024)S(1)} %convert_element_type.112) | copy-start | bytes 9220
  445.7 72.1 %copy-start.38 = (f32[768]{0:T(1024)}, f32[768]{0:T(1024)S(1)}, u32[]{:S(2)}) copy-start(f32[768]{0:T(1024)S(1)} %convert_element_type.113) | copy-start | bytes 9220
  478.0 86.0 %copy-start.23 = (f32[1024]{0:T(1024)}, f32[1024]{0:T(1024)S(1)}, u32[]{:S(2)}) copy-start(f32[1024]{0:T(1024)S(1)} %broadcast_multiply_fusion.1) | copy-start | bytes 12292
  480.1 83.9 %copy-start.27 = (f32[1024]{0:T(1024)}, f32[1024]{0:T(1024)S(1)}, u32[]{:S(2)}) copy-start(f32[1024]{0:T(1024)S(1)} %fusion.43) | copy-start | bytes 12292
  534.5 19.1 %copy-start.7 = (f32[1024,768]{0,1:T(8,128)S(1)}, f32[1024,768]{0,1:T(8,128)}, u32[]{:S(2)}) copy-start(f32[1024,768]{0,1:T(8,128)} %copy-done.6) | copy-start | bytes 9437188
  534.5 19.1 %copy-start.12 = (f32[1024,768]{0,1:T(8,128)S(1)}, f32[1024,768]{0,1:T(8,128)}, u32[]{:S(2)}) copy-start(f32[1024,768]{0,1:T(8,128)} %copy-done.11) | copy-start | bytes 9437188
  569.5 21.2 %all-to-all-start.2 = ((bf16[1024,2,384]{0,2,1:T(8,128)(2,1)}), bf16[1024,2,384]{0,2,1:T(8,128)(2,1)S(1)}, u32[]{:S(2)}, u32[]{:S(2)}) async-start(bf16[1024,2,384]{0,2,1:T(8,128)(2,1)} %bitcast.23), calls=%async_computation.2 | async-start | bytes 3145728 | tf_op jit(solution)/shard_map/all_to_all | solution.py:223
  935.6 7.8 copy-start.2
  958.6 107.3 %all-to-all-start.3 = ((bf16[2048,3,1,384]{3,1,2,0:T(4,128)(2,1)}), bf16[2048,3,1,384]{3,1,2,0:T(4,128)(2,1)}, u32[]{:S(2)}, u32[]{:S(2)}) async-start(bf16[2048,3,1,384]{3,1,2,0:T(4,128)(2,1)} %copy.164), calls=%async_computation.3 | async-start | bytes 12582912 | tf_op jit(solution)/shard_map/all_to_all | solution.py:277
  964.9 211.8 %all-gather.19.cloned.1.call-start = ((), (), s32[]{:S(2)}) async-start(), calls=%async_computation.12 | async-start | bytes 4718592 | tf_op jit(solution)/shard_map/all_gather | solution.py:286
  965.6 216.0 %all-gather.21.cloned.1.call-start = ((), (), s32[]{:S(2)}) async-start(), calls=%async_computation.13 | async-start | bytes 4718592 | tf_op jit(solution)/shard_map/all_gather | solution.py:287
  1086.8 150.2 %reduce-scatter.7.cloned.1.call-start = ((), (), s32[]{:S(2)}) async-start(), calls=%async_computation.15 | async-start | bytes 2433024 | tf_op jit(solution)/shard_map/reduce_scatter | solution.py:295
  1091.7 286.7 %reduce-scatter.11.cloned.1.call-start = ((), (), s32[]{:S(2)}) async-start(), calls=%async_computation.17 | async-start | bytes 9732096 | tf_op jit(solution)/shard_map/reduce_scatter | solution.py:301
  1102.2 417.9 %reduce-scatter.9.cloned.1.call-start = ((), (), s32[]{:S(2)}) async-start(), calls=%async_computation.16 | async-start | bytes 9732096 | tf_op jit(solution)/shard_map/reduce_scatter | solution.py:299
  1114.5 530.2 %reduce-scatter.5.cloned.1.call-start = ((), (), s32[]{:S(2)}) async-start(), calls=%async_computation.14 | async-start | bytes 7299072 | tf_op jit(solution)/shard_map/reduce_scatter | solution.py:292
  (45 other events, 172.4 us)
Sparse Core Ops, SparseCore 0:
  9.6 47.7 all-gather.24
  59.0 44.9 all-gather.22
  106.9 60.4 all-gather.10
  170.2 54.0 all-gather.12
  227.1 63.2 all-gather.14
  448.4 65.4 all-gather.16
  967.8 80.7 all-gather.18
  1086.9 45.8 all-gather.20
  1138.7 98.2 reduce-scatter.6
  1243.3 135.0 reduce-scatter.10
  1384.8 135.1 reduce-scatter.8
  1526.2 118.5 reduce-scatter.4
where the time goes:
time: 1660 us; the launch traced here: 1650 us
  waiting for transfers between devices  747 us (45%)
  matrix products  474 us (29%)
  other arithmetic  167 us (10%)
  local copies, waits for them, and re-layouts  141 us (8%)
  blocking collectives  85.4 us (5%)
  starting transfers between devices  21.1 us (1%)
    reduce_scatter x1, waiting for transfers between devices, local(): lax.psum_scatter(in_weight_grad, ('seq', 'fsdp'), scatter_dimension=0, ti...  142 us
    reduce_scatter x1, waiting for transfers between devices, local(): lax.psum_scatter(down_weight_grad, ('seq', 'fsdp'), scatter_dimension=0,...  141 us
    reduce_scatter x1, waiting for transfers between devices, local(): lax.psum_scatter(qkv_weight_grad, ('seq', 'fsdp'), scatter_dimension=0, t...  125 us
    all_to_all x1, waiting for transfers between devices, local(): lax.all_to_all(qkv_grad_heads[:, :, None, :], 'seq', split_axis=0, concat...  100 us
    unnamed x2, blocking collectives  85.4 us
    convert_element_type x4, other arithmetic, attend_back(): score_grad = (soft_weights * (weight_grad - row_dot)).astype(jnp.bfloat16)  84.8 us
    dot_general x4, matrix products, attend_back(): jnp.einsum('qhd,khd->hqk', out_grad, value_rows, preferred_element_type=j...  72.6 us
    all_gather x1, waiting for transfers between devices, local(): lax.all_gather(qkv_weight, ('seq', 'fsdp'), axis=0, tiled=True)  56.3 us
  transfers between devices with their start and end apart: 16, of which 11 were waited for; matrix products, arithmetic and copies ran while one was open for 22% of the time, Pallas kernels for 0%

commit v1 on v0

v1 whole, which is shorter than its diff:
```python
import jax
import jax.numpy as jnp
import numpy as np
from jax import lax
from jax.sharding import Mesh, PartitionSpec as P
from jax.experimental import pallas as pl
from jax.experimental.pallas import tpu as pltpu

HD = 64
LOG2E = 1.4426950408889634
LN2 = 0.6931471805599453
BIG = 1e30
TQ = 512
STEP = 512
BSTEP = 512
NT = (((1,), (1,)), ((), ()))
NN = (((1,), (0,)), ((), ()))
TN = (((0,), (0,)), ((), ()))


def mxu(a, b, dims):
    return lax.dot_general(a, b, dims, preferred_element_type=jnp.float32)


def lanes(rows):
    return lax.broadcasted_iota(jnp.int32, (rows, 128), 1)


def seg_rows(segs_ref, base_block, rows):
    place = lax.broadcasted_iota(jnp.int32, (rows, 128), 0)
    out = jnp.zeros((rows, 128), jnp.int32)
    for b in range(rows // 128):
        s = segs_ref[base_block + b]
        out = jnp.where(place >= b * 128, s, out)
    return out


def split3(v):
    hi = v.astype(jnp.bfloat16).astype(jnp.float32)
    mid = (v - hi).astype(jnp.bfloat16).astype(jnp.float32)
    low = v - hi - mid
    return hi, mid, low


def both_heads(pair_rows):
    lane = lanes(pair_rows.shape[0])
    zero = jnp.zeros_like(pair_rows)
    return jnp.concatenate(
        [jnp.where(lane < HD, pair_rows, zero), jnp.where(lane < HD, zero, pair_rows)], axis=0
    )


def fill_keys(segs_ref, k_own, k_far, v_own, v_far, k_aug, v_aug):
    half = k_own.shape[0]
    step = 512
    for part, (k_in, v_in) in enumerate(((k_own, v_own), (k_far, v_far))):
        for at in range(0, half, step):
            row = part * half + at
            k_aug[row : row + step, :128] = k_in[at : at + step, :]
            v_aug[row : row + step, :128] = v_in[at : at + step, :]
    total = 2 * half
    for at in range(0, total, step):
        lane = lanes(step)
        seg = seg_rows(segs_ref, at // 128, step)
        hot = (lane == seg) | ((lane >= 64) & (lane < 67))
        k_aug[at : at + step, 128:] = jnp.where(hot, 1.0, 0.0).astype(jnp.bfloat16)
        v_aug[at : at + step, 128:] = jnp.ones((step, 128), jnp.bfloat16)


def fwd_body(segs_ref, q_own, q_far, k_own, k_far, v_own, v_far, o_own, o_far, lse_ref, k_aug, v_aug):
    i = pl.program_id(1)
    n_half = pl.num_programs(1) // 2
    total = k_aug.shape[0]

    @pl.when(i == 0)
    def _():
        fill_keys(segs_ref, k_own, k_far, v_own, v_far, k_aug, v_aug)

    pair_rows = jnp.where(i < n_half, q_own[...], q_far[...])
    lane = lanes(TQ)
    seg = seg_rows(segs_ref, i * (TQ // 128), TQ)
    off = jnp.where((lane < 16) & (lane != seg), -BIG, 0.0).astype(jnp.bfloat16)
    q_aug = jnp.concatenate([both_heads(pair_rows), jnp.concatenate([off, off], axis=0)], axis=1)
    step = STEP
    top = None
    acc = None
    for at in range(0, total, step):
        s = mxu(q_aug, k_aug[at : at + step, :], NT)
        here = jnp.max(s, axis=1, keepdims=True)
        new_top = here if top is None else jnp.maximum(top, here)
        p = jnp.exp2(s - new_top).astype(jnp.bfloat16)
        add = mxu(p, v_aug[at : at + step, :], NN)
        acc = add if acc is None else acc * jnp.exp2(top - new_top) + add
        top = new_top
    both = jnp.where(lane < HD, acc[:TQ, :128], acc[TQ:, :128])
    sums = jnp.where(lane < HD, acc[:TQ, 128:], acc[TQ:, 128:])
    tops = jnp.where(lane < HD, top[:TQ], top[TQ:])
    out = (both / sums).astype(jnp.bfloat16)
    lse_ref[...] = tops + jnp.log2(sums)

    @pl.when(i < n_half)
    def _():
        o_own[...] = out

    @pl.when(i >= n_half)
    def _():
        o_far[...] = out


def pair_specs(half, n_half, parts):
    own_q = lambda at: pl.BlockSpec((TQ, 128), lambda h, i, *_: (jnp.minimum(i, n_half - 1), at * parts + h))
    far_q = lambda at: pl.BlockSpec((TQ, 128), lambda h, i, *_: (jnp.maximum(i - n_half, 0), at * parts + h))
    whole = lambda at: pl.BlockSpec((half, 128), lambda h, i, *_: (0, at * parts + h))
    return own_q, far_q, whole


def attention(segs, own, far):
    half, width = own.shape
    parts = width // 3 // 128
    n_half = half // TQ
    own_q, far_q, whole = pair_specs(half, n_half, parts)
    return pl.pallas_call(
        fwd_body,
        grid_spec=pltpu.PrefetchScalarGridSpec(
            num_scalar_prefetch=1,
            grid=(parts, 2 * n_half),
            in_specs=[own_q(0), far_q(0), whole(1), whole(1), whole(2), whole(2)],
            out_specs=[own_q(0), far_q(0), pl.BlockSpec((TQ, 128), lambda h, i, *_: (i, h))],
            scratch_shapes=[
                pltpu.VMEM((2 * half, 256), jnp.bfloat16),
                pltpu.VMEM((2 * half, 256), jnp.bfloat16),
            ],
        ),
        out_shape=[
            jax.ShapeDtypeStruct((half, parts * 128), jnp.bfloat16),
            jax.ShapeDtypeStruct((half, parts * 128), jnp.bfloat16),
            jax.ShapeDtypeStruct((2 * half, parts * 128), jnp.float32),
        ],
        compiler_params=pltpu.CompilerParams(dimension_semantics=("arbitrary", "arbitrary"), vmem_limit_bytes=50 << 20),
        cost_estimate=pl.CostEstimate(flops=2 * 4 * half * half * 4 * 64 * 2 * parts, bytes_accessed=half * width * 4, transcendentals=8 * half * half * parts),
    )(segs, own, far, own, far, own, far)


def bwd_body(segs_ref, q_own, q_far, k_own, k_far, v_own, v_far, o_own, o_far, d_own, d_far, lse_ref,
             dq_own, dq_far, dk_own, dk_far, dv_own, dv_far, k_aug, v_aug, dk_acc, dv_acc):
    i = pl.program_id(1)
    n = pl.num_programs(1)
    n_half = n // 2
    total = k_aug.shape[0]
    half = total // 2

    @pl.when(i == 0)
    def _():
        fill_keys(segs_ref, k_own, k_far, v_own, v_far, k_aug, v_aug)
        dk_acc[...] = jnp.zeros_like(dk_acc)
        dv_acc[...] = jnp.zeros_like(dv_acc)

    near = i < n_half
    q_rows = jnp.where(near, q_own[...], q_far[...])
    d_rows = jnp.where(near, d_own[...], d_far[...])
    o_rows = jnp.where(near, o_own[...], o_far[...])
    lane = lanes(TQ)
    seg = seg_rows(segs_ref, i * (TQ // 128), TQ)
    off = jnp.where((lane < 16) & (lane != seg), -BIG, 0.0)
    prod = d_rows.astype(jnp.float32) * o_rows.astype(jnp.float32)
    q_side, d_side = [], []
    for head in range(2):
        mine = (lane < HD) if head == 0 else (lane >= HD)
        dot_row = jnp.sum(jnp.where(mine, prod, 0.0), axis=1, keepdims=True)
        lse = jnp.broadcast_to(lse_ref[:, head * HD : head * HD + 1], (TQ, 128))
        h, m, l = split3(-lse)
        q_side.append(jnp.where(lane == 64, h, jnp.where(lane == 65, m, jnp.where(lane == 66, l, off))).astype(jnp.bfloat16))
        h, m, l = split3(-jnp.broadcast_to(dot_row, (TQ, 128)))
        d_side.append(jnp.where(lane == 64, h, jnp.where(lane == 65, m, jnp.where(lane == 66, l, 0.0))).astype(jnp.bfloat16))
    q2 = both_heads(q_rows)
    d2 = both_heads(d_rows)
    q_aug = jnp.concatenate([q2, jnp.concatenate(q_side, axis=0)], axis=1)
    d_aug = jnp.concatenate([d2, jnp.concatenate(d_side, axis=0)], axis=1)
    step = BSTEP
    dq = None
    for at in range(0, total, step):
        keys = k_aug[at : at + step, :]
        p = jnp.exp2(mxu(q_aug, keys, NT))
        dp = mxu(d_aug, v_aug[at : at + step, :], NT)
        ds = (p * dp).astype(jnp.bfloat16)
        dv_acc[at : at + step, :] += mxu(p.astype(jnp.bfloat16), d2, TN)
        dk_acc[at : at + step, :] += mxu(ds, q2, TN)
        add = mxu(ds, keys[:, :128], NN)
        dq = add if dq is None else dq + add
    out = (jnp.where(lane < HD, dq[:TQ], dq[TQ:]) * (HD ** -0.5)).astype(jnp.bfloat16)

    @pl.when(near)
    def _():
        dq_own[...] = out

    @pl.when(i >= n_half)
    def _():
        dq_far[...] = out

    @pl.when(i == n - 1)
    def _():
        dk_own[...] = (dk_acc[:half, :] * LN2).astype(jnp.bfloat16)
        dk_far[...] = (dk_acc[half:, :] * LN2).astype(jnp.bfloat16)
        dv_own[...] = dv_acc[:half, :].astype(jnp.bfloat16)
        dv_far[...] = dv_acc[half:, :].astype(jnp.bfloat16)


def attention_back(segs, own, far, o_own, o_far, d_own, d_far, lse):
    half, width = own.shape
    parts = width // 3 // 128
    n_half = half // TQ
    own_q, far_q, whole = pair_specs(half, n_half, parts)
    one = jax.ShapeDtypeStruct((half, parts * 128), jnp.bfloat16)
    return pl.pallas_call(
        bwd_body,
        grid_spec=pltpu.PrefetchScalarGridSpec(
            num_scalar_prefetch=1,
            grid=(parts, 2 * n_half),
            in_specs=[own_q(0), far_q(0), whole(1), whole(1), whole(2), whole(2),
                      own_q(0), far_q(0), own_q(0), far_q(0), pl.BlockSpec((TQ, 128), lambda h, i, *_: (i, h))],
            out_specs=[own_q(0), far_q(0), whole(0), whole(0), whole(0), whole(0)],
            scratch_shapes=[
                pltpu.VMEM((2 * half, 256), jnp.bfloat16),
                pltpu.VMEM((2 * half, 256), jnp.bfloat16),
                pltpu.VMEM((2 * half, 128), jnp.float32),
                pltpu.VMEM((2 * half, 128), jnp.float32),
            ],
        ),
        out_shape=[one] * 6,
        compiler_params=pltpu.CompilerParams(dimension_semantics=("arbitrary", "arbitrary"), vmem_limit_bytes=50 << 20),
        cost_estimate=pl.CostEstimate(flops=5 * 4 * half * half * 4 * 64 * 2 * parts, bytes_accessed=half * width * 8, transcendentals=8 * half * half * parts),
    )(segs, own, far, own, far, own, far, o_own, o_far, d_own, d_far, lse)


D = 768
UNITS = 16
norm_eps = 1e-12
bf16 = jnp.bfloat16
f32 = jnp.float32


def shift(n, k):
    return [(i, (i + k) % n) for i in range(n)]


class Plan:
    def __init__(self, seq, fsdp):
        rest = fsdp // 2
        dims = []
        while rest > 1:
            want = 4 if len(dims) % 2 == 0 and rest % 4 == 0 else 2
            dims.append(want)
            rest //= want
        self.dims = [seq] + dims + [2]
        self.names = ["s"] + ["r%d" % i for i in range(len(dims))] + ["c"]
        count = len(self.dims)
        self.stages = ([1] if dims else []) + [0] + list(range(2, count - 1)) + [count - 1]
        self.total = seq * fsdp

    def places(self, sign):
        shape = [self.dims[a] for a in reversed(self.stages)]
        grid = np.indices(self.dims).reshape(len(self.dims), -1)
        flat = jnp.zeros((self.total,), jnp.int32)
        if sign < 0:
            for a in reversed(self.stages):
                n = self.dims[a]
                off = (lax.axis_index(self.names[a]) - jnp.asarray(grid[a], jnp.int32)) % n
                flat = flat * n + off
            return flat
        offs = np.indices(shape).reshape(len(shape), -1)
        by_axis = {a: offs[j] for j, a in enumerate(reversed(self.stages))}
        for a in range(len(self.dims)):
            n = self.dims[a]
            flat = flat * n + (lax.axis_index(self.names[a]) + jnp.asarray(by_axis[a], jnp.int32)) % n
        return flat


def gather_all(plan, shard):
    buf = shard[None]
    for a in plan.stages:
        n = plan.dims[a]
        if n == 1:
            continue
        parts = [buf] + [lax.ppermute(buf, plan.names[a], shift(n, k)) for k in range(1, n)]
        buf = jnp.concatenate(parts, axis=0)
    return jnp.take(buf, plan.places(-1), axis=0)


def reduce_all(plan, grads):
    buf = jnp.take(grads, plan.places(1), axis=0)
    for a in reversed(plan.stages):
        n = plan.dims[a]
        size = buf.shape[0] // n
        keep = buf[:size].astype(f32)
        for k in range(1, n):
            got = lax.ppermute(buf[k * size : (k + 1) * size].astype(bf16), plan.names[a], shift(n, k))
            keep = keep + got.astype(f32)
        buf = keep if a == plan.stages[0] else keep.astype(bf16)
    return buf[0]


def norm_stats(rows):
    mean = jnp.mean(rows, axis=-1, keepdims=True)
    centered = rows - mean
    var = jnp.mean(centered * centered, axis=-1, keepdims=True)
    rstd = lax.rsqrt(var + norm_eps)
    return centered * rstd, rstd


def norm_back(grad, unit, rstd, gain):
    eg = grad * gain
    mean_eg = jnp.mean(eg, axis=-1, keepdims=True)
    mean_en = jnp.mean(eg * unit, axis=-1, keepdims=True)
    return (eg - mean_eg - unit * mean_en) * rstd


def dot(a, b, dims=NN):
    return lax.dot_general(a, b, dims, preferred_element_type=f32)


def swap_pair(x):
    return lax.ppermute(x, "c", [(0, 1), (1, 0)])


def relocate(x):
    return lax.ppermute(x, ("s", "c"), [(0, 0), (1, 2), (2, 1), (3, 3)])


def pick(pair, at):
    return lax.dynamic_index_in_dim(pair, at, 0, keepdims=False)


def local(plan, tokens, lengths, block_order, qkv_weight, query_bias, value_bias, out_weight, out_bias,
          norm1_gain, norm1_shift, in_weight, in_bias, down_weight, down_bias, norm2_gain, norm2_shift, cotangent):
    half = tokens.shape[1]
    me = lax.axis_index("c")
    rows_dev = qkv_weight.shape[0]
    ff_dev = down_weight.shape[0]
    ff_cols = in_weight.shape[1] // D
    width = D // 2
    count = plan.total

    tok = relocate(tokens[0])
    ends = jnp.cumsum(lengths[0])
    unit = 2 * half // UNITS
    seg_packed = jnp.sum((jnp.arange(UNITS)[:, None] * unit >= ends[None, :]).astype(jnp.int32), axis=1)
    hit = block_order[0][:, None] == jnp.arange(UNITS)[None, :]
    seg_here = jnp.sum(jnp.where(hit, seg_packed[:, None], 0), axis=0)
    seg_pair = swap_pair(seg_here)
    segs = jnp.where(lax.axis_index("s") == me, seg_here, seg_pair)
    segs = jnp.roll(segs.reshape(2, UNITS // 2), me, axis=0).reshape(UNITS)

    smalls = (query_bias, value_bias, out_bias, norm1_gain, norm1_shift, in_bias, down_bias, norm2_gain, norm2_shift)
    small_row = jnp.concatenate(smalls)
    small_size = small_row.shape[0]
    small_rows = jnp.zeros((8, D), bf16).at[0, :small_size].set(small_row)
    first = jnp.concatenate([qkv_weight[:, j * D : (j + 1) * D] for j in range(3)] + [small_rows], axis=0)
    second = jnp.concatenate([out_weight] + [in_weight[:, j * D : (j + 1) * D] for j in range(ff_cols)] + [down_weight], axis=0)
    first_all = gather_all(plan, first)
    second_all = gather_all(plan, second)
    small_all = first_all[:, 3 * rows_dev, :small_size]
    small_full = []
    at = 0
    for piece in smalls:
        size = piece.shape[0]
        small_full.append(small_all[:, at : at + size].reshape(count * size).astype(f32))
        at += size
    bias_q, bias_v, bias_o, gain1, shift1, bias_in, bias_down, gain2, shift2 = small_full

    def rows_of(buf, start, size):
        return buf[:, start : start + size].reshape(count * size, D)

    w_qkv = jnp.stack([rows_of(first_all, j * rows_dev, rows_dev) for j in range(3)])
    w_heads = jnp.stack([jnp.concatenate([w_qkv[j][:, c * width : (c + 1) * width] for j in range(3)], axis=1) for c in range(2)])
    bias_heads = jnp.stack([jnp.concatenate([bias_q[c * width : (c + 1) * width], jnp.zeros((width,), f32), bias_v[c * width : (c + 1) * width]]) for c in range(2)])
    fold = jnp.concatenate([jnp.full((width,), LOG2E * HD ** -0.5, f32), jnp.ones((2 * width,), f32)])
    w_mine, w_far = pick(w_heads, me), pick(w_heads, 1 - me)
    send = ((dot(tok, w_far) + pick(bias_heads, 1 - me)) * fold).astype(bf16)
    far = swap_pair(send)
    own = ((dot(tok, w_mine) + pick(bias_heads, me)) * fold).astype(bf16)
    o_own, o_far, lse = attention(segs, own, far)
    o_got = swap_pair(o_far)
    w_out = rows_of(second_all, 0, rows_dev)
    w_in = jnp.concatenate([rows_of(second_all, (1 + j) * rows_dev, rows_dev) for j in range(ff_cols)], axis=1)
    w_down = rows_of(second_all, (1 + ff_cols) * rows_dev, ff_dev)
    w_out_pair = w_out.reshape(2, width, D)
    out_mine, out_far = pick(w_out_pair, me), pick(w_out_pair, 1 - me)
    attn_out = dot(o_own, out_mine) + dot(o_got, out_far) + bias_o
    unit1, rstd1 = norm_stats(tok.astype(f32) + attn_out)
    hidden = unit1 * gain1 + shift1
    low = hidden.astype(bf16)
    inner = dot(low, w_in) + bias_in
    phi = 0.5 * (1.0 + lax.erf(inner * (0.5 ** 0.5)))
    act = (inner * phi).astype(bf16)
    slope = phi + inner * (jnp.exp(-0.5 * inner * inner) * 0.3989422804014327)
    unit2, rstd2 = norm_stats(hidden + dot(act, w_down) + bias_down)
    out_rows = (unit2 * gain2 + shift2).astype(bf16)
    output = relocate(out_rows)

    back = relocate(cotangent[0]).astype(f32)
    g_gain2 = jnp.sum(back * unit2, axis=0)
    g_shift2 = jnp.sum(back, axis=0)
    resid2 = norm_back(back, unit2, rstd2, gain2)
    branch = resid2.astype(bf16)
    g_bdown = jnp.sum(branch.astype(f32), axis=0)
    g_down = dot(act, branch, TN).astype(bf16)
    inner_grad = (dot(branch, w_down, NT) * slope).astype(bf16)
    g_bin = jnp.sum(inner_grad.astype(f32), axis=0)
    g_in = dot(low, inner_grad, TN).astype(bf16)
    blocks = [g_in[:, j * D : (j + 1) * D].reshape(count, rows_dev, D) for j in range(ff_cols)]
    ffn_sum = reduce_all(plan, jnp.concatenate(blocks + [g_down.reshape(count, ff_dev, D)], axis=1))
    hidden_grad = resid2 + dot(inner_grad, w_in, NT)
    g_gain1 = jnp.sum(hidden_grad * unit1, axis=0)
    g_shift1 = jnp.sum(hidden_grad, axis=0)
    resid1 = norm_back(hidden_grad, unit1, rstd1, gain1)
    attn_grad = resid1.astype(bf16)
    g_bout = jnp.sum(attn_grad.astype(f32), axis=0)
    d_far = dot(attn_grad, out_far, NT).astype(bf16)
    d_got = swap_pair(d_far)
    d_own = dot(attn_grad, out_mine, NT).astype(bf16)
    g_out_mine = dot(o_own, attn_grad, TN).astype(bf16)
    g_out_far = dot(o_got, attn_grad, TN).astype(bf16)
    g_out = jnp.stack([jnp.where(me == 0, g_out_mine, g_out_far), jnp.where(me == 0, g_out_far, g_out_mine)]).reshape(D, D)
    pieces = attention_back(segs, own, far, o_own, o_far, d_own, d_got, lse)
    back_own = jnp.concatenate(pieces[0::2], axis=1)
    back_got = swap_pair(jnp.concatenate(pieces[1::2], axis=1))
    sums_own = jnp.sum(back_own.astype(f32), axis=0)
    sums_got = jnp.sum(back_got.astype(f32), axis=0)

    def order_heads(mine, other):
        return jnp.where(me == 0, mine, other), jnp.where(me == 0, other, mine)

    lo, hi = order_heads(sums_own, sums_got)
    g_bq = jnp.concatenate([lo[:width], hi[:width]])
    g_bv = jnp.concatenate([lo[2 * width :], hi[2 * width :]])
    g_lo, g_hi = order_heads(dot(tok, back_own, TN).astype(bf16), dot(tok, back_got, TN).astype(bf16))
    g_parts = [jnp.concatenate([g_lo[:, j * width : (j + 1) * width], g_hi[:, j * width : (j + 1) * width]], axis=1).reshape(count, rows_dev, D) for j in range(3)]
    small_grads = (g_bq, g_bv, g_bout, g_gain1, g_shift1, g_bin, g_bdown, g_gain2, g_shift2)
    small_back = jnp.concatenate([g.reshape(count, -1) for g in small_grads], axis=1).astype(bf16)
    small_back = jnp.zeros((count, 8, D), bf16).at[:, 0, :small_size].set(small_back)
    attn_sum = reduce_all(plan, jnp.concatenate(g_parts + [g_out.reshape(count, rows_dev, D), small_back], axis=1))
    packed_grad = (resid1 + dot(back_own, w_mine, NT) + dot(back_got, w_far, NT)).astype(bf16)
    input_grad = relocate(packed_grad)

    out_qkv = jnp.concatenate([attn_sum[j * rows_dev : (j + 1) * rows_dev] for j in range(3)], axis=1)
    out_out = attn_sum[3 * rows_dev : 4 * rows_dev]
    out_in = jnp.concatenate([ffn_sum[j * rows_dev : (j + 1) * rows_dev] for j in range(ff_cols)], axis=1)
    out_down = ffn_sum[ff_cols * rows_dev :]
    line = attn_sum[4 * rows_dev]
    small_out = []
    at = 0
    for piece in smalls:
        small_out.append(line[at : at + piece.shape[0]])
        at += piece.shape[0]
    s = small_out
    return (output[None], input_grad[None], out_qkv, s[0], s[1], out_out, s[2], s[3], s[4], out_in, s[5], out_down, s[6], s[7], s[8])


def solution(mesh):
    plan = Plan(mesh.shape["seq"], mesh.shape["fsdp"])
    inner_mesh = Mesh(mesh.devices.reshape(plan.dims), tuple(plan.names))
    groups = tuple(plan.names[1:])
    every = tuple(plan.names)
    rows = P(groups, "s", None)
    table = P(groups, None)
    mat = P(every, None)
    vec = P(every)
    placed = (rows, table, table, mat, vec, vec, mat, vec, vec, vec, mat, vec, mat, vec, vec, vec, rows)
    outs = (rows, rows, mat, vec, vec, mat, vec, vec, vec, mat, vec, mat, vec, vec, vec)

    def run(*args):
        return local(plan, *args)

    return jax.shard_map(run, mesh=inner_mesh, in_specs=placed, out_specs=outs, check_vma=False)
```

time: 1660 us -> 671 us (0.40)
  waiting for transfers between devices: 747 us -> 198 us
  matrix products: 474 us -> 95.7 us
  Pallas kernels: 0 us -> 120 us
  other arithmetic: 167 us -> 51.8 us
  blocking collectives: 85.4 us -> 0 us
  starting transfers between devices: 21.1 us -> 54.5 us
    reduce_scatter x4 -> x0, waiting for transfers between devices: 454 us -> none  [the longest x1 142 us: local(): lax.psum_scatter(in_weight_grad, ('seq', 'fsdp'), scatter_dimension=0, ti...]
    dot_general x40 -> x18, matrix products: 474 us -> 95.7 us  [dot(): return lax.dot_general(a, b, dims, preferred_element_type=f32)]
    ppermute x0 -> x33, waiting for transfers between devices: none -> 198 us  [the longest x12 107 us: reduce_all(): lax.ppermute(buf[k * size:(k + 1) * size].astype(bf16), plan.names[a], sh...]
    all_to_all x4 -> x0, waiting for transfers between devices: 187 us -> none  [the longest x1 100 us: local(): lax.all_to_all(qkv_grad_heads[:, :, None, :], 'seq', split_axis=0, concat...]
    pallas_call x0 -> x2, Pallas kernels: none -> 120 us  [the longest x1 79.7 us: attention_back(): pl.pallas_call(bwd_body, grid_spec=pltpu.PrefetchScalarGridSpec(num_scala...]
    all_gather x8 -> x0, waiting for transfers between devices: 102 us -> none  [the longest x1 56.3 us: local(): lax.all_gather(qkv_weight, ('seq', 'fsdp'), axis=0, tiled=True)]
    unnamed x2 -> x0, blocking collectives: 85.4 us -> none
    convert_element_type x13 -> x8, other arithmetic: 88.2 us -> 8.83 us  [the longest x6 8.67 us: reduce_all(): buf = keep if a == plan.stages[0] else keep.astype(bf16)]
  transfers between devices with their start and end apart: 16 -> 33, of which waited for: 11 -> 12; matrix products, arithmetic and copies ran while one was open for 22% -> 33% of each run, Pallas kernels for 0% -> 6%
where the time goes in v1:
time: 671 us; the launch traced here: 657 us
  waiting for transfers between devices  198 us (30%)
  local copies, waits for them, and re-layouts  135 us (20%)
  Pallas kernels  120 us (18%)
  matrix products  95.7 us (14%)
  starting transfers between devices  54.5 us (8%)
  other arithmetic  51.8 us (8%)
    ppermute x12, waiting for transfers between devices, reduce_all(): lax.ppermute(buf[k * size:(k + 1) * size].astype(bf16), plan.names[a], sh...  107 us
    dot_general x18, matrix products, dot(): return lax.dot_general(a, b, dims, preferred_element_type=f32)  95.7 us
    ppermute x12, waiting for transfers between devices, gather_all(): lax.ppermute(buf, plan.names[a], shift(n, k))  90.6 us
    pallas_call x1, Pallas kernels, attention_back(): pl.pallas_call(bwd_body, grid_spec=pltpu.PrefetchScalarGridSpec(num_scala...  79.7 us
    unnamed x137, local copies, waits for them, and re-layouts  41.5 us
    pallas_call x1, Pallas kernels, attention(): pl.pallas_call(fwd_body, grid_spec=pltpu.PrefetchScalarGridSpec(num_scala...  40.6 us
    ppermute x12, starting transfers between devices, reduce_all(): lax.ppermute(buf[k * size:(k + 1) * size].astype(bf16), plan.names[a], sh...  20.9 us
    ppermute x12, starting transfers between devices, gather_all(): lax.ppermute(buf, plan.names[a], shift(n, k))  17.9 us
  transfers between devices with their start and end apart: 33, of which 12 were waited for; matrix products, arithmetic and copies ran while one was open for 33% of the time, Pallas kernels for 6%

profile of v1, /device:TPU:1, one launch (start us, length us, event | category | flops | bytes accessed | tf_op | source)
XLA Modules:
  0.0 657.3 jit_solution(15856351249304152973)
XLA Ops:
  0.7 6.1 concatenate.127
  16.3 4.6 collective-permute-done.3
  25.9 7.3 %collective-permute-done.5 = bf16[4,80,768]{2,1,0:T(8,128)(2,1)S(1)} collective-permute-done((bf16[4,80,768]{2,1,0:T(8,128)(2,1)S(1)}, bf16[4,80,768]{2,1,0:T(8,128)(2,1)S(1)}, u32[]{:S(2)}, u32[]{:S(2)}) %collective-permute-start.5) | collective-permute-done | bytes 491552 | tf_op jit(solution)/shard_map/ppermute | solution.py:284
  45.1 16.3 %collective-permute-done.10 = bf16[1,216,768]{2,1,0:T(8,128)(2,1)S(1)} collective-permute-done((bf16[1,216,768]{2,1,0:T(8,128)(2,1)S(1)}, bf16[1,216,768]{2,1,0:T(8,128)(2,1)S(1)}, u32[]{:S(2)}, u32[]{:S(2)}) %collective-permute-start.10) | collective-permute-done | bytes 331808 | tf_op jit(solution)/shard_map/ppermute | solution.py:284
  69.0 22.7 %collective-permute-done.12 = bf16[4,216,768]{2,1,0:T(8,128)(2,1)S(1)} collective-permute-done((bf16[4,216,768]{2,1,0:T(8,128)(2,1)S(1)}, bf16[4,216,768]{2,1,0:T(8,128)(2,1)S(1)}, u32[]{:S(2)}, u32[]{:S(2)}) %collective-permute-start.12) | collective-permute-done | bytes 1327136 | tf_op jit(solution)/shard_map/ppermute | solution.py:284
  98.6 4.7 collective-permute-start
  106.4 4.8 gather_fusion
  118.3 35.4 %collective-permute-done.13 = bf16[8,216,768]{2,1,0:T(8,128)(2,1)S(1)} collective-permute-done((bf16[8,216,768]{2,1,0:T(8,128)(2,1)}, bf16[8,216,768]{2,1,0:T(8,128)(2,1)S(1)}, u32[]{:S(2)}, u32[]{:S(2)}) %collective-permute-start.13) | collective-permute-done | bytes 2654240 | tf_op jit(solution)/shard_map/ppermute | solution.py:284
  159.9 6.1 fusion.10
  178.7 40.6 %shard_map.424 = (bf16[1024,384]{1,0:T(8,128)(2,1)S(1)}, bf16[1024,384]{1,0:T(8,128)(2,1)S(1)}, f32[2048,384]{1,0:T(8,128)}) custom-call(s32[16]{0:T(128)S(1)} %reshape.462.segs_ref, bf16[1024,1152]{1,0:T(8,128)(2,1)S(1)} %fusion.9.q_own.k_own.v_own, bf16[1024,1152]{1,0:T(8,128)(2,1)} %collective-permute-done.8.q_far.k_far.v_far, ...), custom_call_target="tpu_custom_call" | custom-call | flops 12884901888 | bytes 4718592 | tf_op jit(solution)/shard_map/pallas_call | solution.py:122
  219.6 5.6 constant_dynamic-update-slice_fusion.35
  225.2 10.0 %gather_fusion.1 = bf16[32,216,768]{2,1,0:T(8,128)(2,1)} fusion(bf16[32,216,768]{2,1,0:T(8,128)(2,1)} %constant_dynamic-update-slice_fusion.35, s32[1024]{0:T(1024)S(1)} %pad_clamp_fusion.1), kind=kCustom, calls=%fused_computation.1 | custom fusion | bytes 21233792 | tf_op jit(solution)/shard_map/jit(_take)/gather | solution.py:286
  235.1 6.0 broadcast_select_fusion
  252.1 14.1 %multiply_convert_fusion = (bf16[1024,3072]{1,0:T(8,128)(2,1)}, f32[1024,3072]{1,0:T(8,128)}) fusion(f32[3072]{0:T(1024)S(1)} %reshape.480, bf16[768,768]{1,0:T(8,128)(2,1)S(1)} %bitcast.167, bf16[768,768]{1,0:T(8,128)(2,1)S(1)} %bitcast.169, bf16[768,768]{1,0:T(8,128)(2,1)} %bitcast.171, bf16[768,768]{1,0:T(8,128)(2,1)} %bitcast.173, ...), kind=kOutput, calls=%fused_computation.11 | convolution fusion | flops 4873519104 | bytes 26765312 | tf_op jit(solution)/shard_map/dot_general | solution.py:318
  266.3 7.6 %fusion.97 = (f32[1024]{0:T(1024)S(1)}, f32[1024,768]{0,1:T(8,128)S(1)}) fusion(f32[768]{0:T(1024)S(1)} %reshape.481, bf16[1024,3072]{1,0:T(8,128)(2,1)} %get-tuple-element.245, bf16[3072,768]{1,0:T(8,128)(2,1)S(1)} %bitcast.151, f32[768]{0:T(1024)S(1)} %reshape.479, f32[768]{0:T(1024)S(1)} %reshape.478, f32[1024]{0:T(1024)S(1)} %add_rsqrt_fusion.1, ...), kind=kOutput, calls=%fused_computation.293 | convolution fusion | flops 4837342208 | bytes 17323008 | tf_op jit(solution)/shard_map/dot_general | solution.py:318
  278.5 6.9 %convolution_convert_fusion = bf16[3072,768]{1,0:T(8,128)(2,1)} fusion(bf16[1024,3072]{1,0:T(8,128)(2,1)S(1)} %bitcast.180, bf16[1024,768]{0,1:T(8,128)(2,1)S(1)} %get-tuple-element.129), kind=kOutput, calls=%fused_computation.18 | convolution fusion | flops 4834197504 | bytes 12582912 | tf_op jit(solution)/shard_map/dot_general | solution.py:318
  285.4 11.8 %fusion.98 = (bf16[3072]{0:T(1024)(128)(2,1)S(1)}, bf16[1024,3072]{1,0:T(8,128)(2,1)S(1)}) fusion(f32[1024,3072]{1,0:T(8,128)} %get-tuple-element.246, f32[3072]{0:T(1024)S(1)} %reshape.480, bf16[1024,768]{0,1:T(8,128)(2,1)S(1)} %get-tuple-element.129, bf16[3072,768]{1,0:T(8,128)(2,1)S(1)} %bitcast.152), kind=kOutput, calls=%fused_computation.294 | convolution fusion | flops 4869583872 | bytes 25184256 | tf_op jit(solution)/shard_map/dot_general | solution.py:318
  299.8 7.4 %convolution_convert_fusion.1 = bf16[768,3072]{1,0:T(8,128)(2,1)} fusion(bf16[1024,3072]{1,0:T(8,128)(2,1)S(1)} %get-tuple-element.251, f32[1024,768]{0,1:T(8,128)S(1)} %get-tuple-element.244, f32[768]{0:T(1024)S(1)} %reshape.479, f32[768]{0:T(1024)S(1)} %reshape.478, f32[1024]{0:T(1024)S(1)} %add_rsqrt_fusion.1, f32[1024]{0:T(1024)S(1)} %broadcast_multiply_fusion.5), kind=kOutput, calls=%fused_computation.19 | convolution fusion | flops 4838129664 | bytes 14170112 | tf_op jit(solution)/shard_map/dot_general | solution.py:318
  307.2 9.6 %multiply_reduce_fusion = (bf16[768]{0:T(1024)(128)(2,1)S(1)}, f32[1024]{0:T(1024)S(1)}, f32[1024]{0:T(1024)S(1)}, bf16[768]{0:T(1024)(128)(2,1)S(1)}, f32[1024,768]{0,1:T(8,128)S(1)}) fusion(f32[1024,768]{0,1:T(8,128)S(1)} %get-tuple-element.244, f32[1024]{0:T(1024)S(1)} %add_rsqrt_fusion.1, f32[1024]{0:T(1024)S(1)} %broadcast_multiply_fusion.5, ...), kind=kOutput, calls=%fused_computation.44 | convolution fusion | flops 4864864256 | bytes 22062080 | tf_op jit(solution)/shard_map/dot_general | solution.py:318
  335.3 9.4 %gather_fusion.3 = bf16[32,192,768]{2,1,0:T(8,128)(2,1)} fusion(bf16[32,192,768]{2,1,0:T(8,128)(2,1)} %constant_dynamic-update-slice_fusion.49, s32[1024]{0:T(1024)S(1)} %pad_clamp_fusion), kind=kCustom, calls=%fused_computation.3 | custom fusion | bytes 18874496 | tf_op jit(solution)/shard_map/jit(_take)/gather | solution.py:290
  346.5 79.7 %shard_map.425 = (bf16[1024,384]{1,0:T(8,128)(2,1)S(1)}, bf16[1024,384]{1,0:T(8,128)(2,1)S(1)}, bf16[1024,384]{1,0:T(8,128)(2,1)S(1)}, bf16[1024,384]{1,0:T(8,12...) custom-call(s32[16]{0:T(128)S(1)} %reshape.462.segs_ref, bf16[1024,1152]{1,0:T(8,128)(2,1)} %copy-done.3, ...), custom_call_target="tpu_custom_call" | custom-call | flops 32212254720 | bytes 9437184 | tf_op jit(solution)/shard_map/pallas_call | solution.py:214
  429.4 8.3 %broadcast_select_fusion.1 = bf16[32,192,768]{2,1,0:T(8,128)(2,1)} fusion(bf16[32,192,768]{2,1,0:T(8,128)(2,1)} %gather_fusion.3, pred[32]{0:T(512)(128)(4,1)S(1)} %copy-done.36), kind=kLoop, calls=%fused_computation.15 | loop fusion | flops 4718592 | bytes 18874400 | tf_op jit(solution)/shard_map/jit(_take)/select_n | solution.py:290
  437.7 5.1 slice.593
  485.4 5.8 gather_fusion.2
  494.8 5.2 add_convert_fusion
  507.6 5.6 add_convert_fusion.3
  516.7 63.5 %collective-permute-done.22 = bf16[8,104,768]{2,1,0:T(8,128)(2,1)S(1)} collective-permute-done((bf16[8,104,768]{2,1,0:T(8,128)(2,1)S(1)}, bf16[8,104,768]{2,1,0:T(8,128)(2,1)S(1)}, u32[]{:S(2)}, u32[]{:S(2)}) %collective-permute-start.22) | collective-permute-done | bytes 1277984 | tf_op jit(solution)/shard_map/ppermute | solution.py:296
  583.9 11.6 %collective-permute-done.23 = bf16[4,104,768]{2,1,0:T(8,128)(2,1)S(1)} collective-permute-done((bf16[4,104,768]{2,1,0:T(8,128)(2,1)S(1)}, bf16[4,104,768]{2,1,0:T(8,128)(2,1)S(1)}, u32[]{:S(2)}, u32[]{:S(2)}) %collective-permute-start.23) | collective-permute-done | bytes 639008 | tf_op jit(solution)/shard_map/ppermute | solution.py:296
  596.5 5.6 collective-permute-start.26
  610.3 7.9 %collective-permute-done.25 = bf16[1,104,768]{2,1,0:T(8,128)(2,1)S(1)} collective-permute-done((bf16[1,104,768]{2,1,0:T(8,128)(2,1)}, bf16[1,104,768]{2,1,0:T(8,128)(2,1)S(1)}, u32[]{:S(2)}, u32[]{:S(2)}) %collective-permute-start.25) | collective-permute-done | bytes 159776 | tf_op jit(solution)/shard_map/ppermute | solution.py:296
  622.7 5.5 collective-permute-start.32
  635.6 19.9 %collective-permute-done.31 = bf16[1,192,768]{2,1,0:T(8,128)(2,1)S(1)} collective-permute-done((bf16[1,192,768]{2,1,0:T(8,128)(2,1)S(1)}, bf16[1,192,768]{2,1,0:T(8,128)(2,1)S(1)}, u32[]{:S(2)}, u32[]{:S(2)}) %collective-permute-start.31) | collective-permute-done | bytes 294944 | tf_op jit(solution)/shard_map/ppermute | solution.py:296
  (326 shorter events, 194.7 us)
Async XLA Ops:
  7.6 8.6 %collective-permute-start.2 = (bf16[1,80,768]{2,1,0:T(8,128)(2,1)S(1)}, bf16[1,80,768]{2,1,0:T(8,128)(2,1)S(1)}, u32[]{:S(2)}, u32[]{:S(2)}) collective-permute-start(bf16[1,80,768]{2,1,0:T(8,128)(2,1)S(1)} %fusion.33), channel_id=1, source_target_pairs={{0,4},{4,8},{8,12},{12,0},{1,5},{5,9},{9,13},{13,1},{2,6},{6,10},{... | collective-permute-start | bytes 368648 | tf_op jit(solution)/shard_map/ppermute | solution.py:284
  9.8 11.1 %collective-permute-start.3 = (bf16[1,80,768]{2,1,0:T(8,128)(2,1)S(1)}, bf16[1,80,768]{2,1,0:T(8,128)(2,1)S(1)}, u32[]{:S(2)}, u32[]{:S(2)}) collective-permute-start(bf16[1,80,768]{2,1,0:T(8,128)(2,1)S(1)} %fusion.33), channel_id=1, source_target_pairs={{0,8},{4,12},{8,0},{12,4},{1,9},{5,13},{9,1},{13,5},{2,10},{6,14},... | collective-permute-start | bytes 368648 | tf_op jit(solution)/shard_map/ppermute | solution.py:284
  12.1 8.8 %collective-permute-start.4 = (bf16[1,80,768]{2,1,0:T(8,128)(2,1)S(1)}, bf16[1,80,768]{2,1,0:T(8,128)(2,1)S(1)}, u32[]{:S(2)}, u32[]{:S(2)}) collective-permute-start(bf16[1,80,768]{2,1,0:T(8,128)(2,1)S(1)} %fusion.33), channel_id=1, source_target_pairs={{0,12},{4,0},{8,4},{12,8},{1,13},{5,1},{9,5},{13,9},{2,14},{6,2},{... | collective-permute-start | bytes 368648 | tf_op jit(solution)/shard_map/ppermute | solution.py:284
  20.9 12.3 %collective-permute-start.5 = (bf16[4,80,768]{2,1,0:T(8,128)(2,1)S(1)}, bf16[4,80,768]{2,1,0:T(8,128)(2,1)S(1)}, u32[]{:S(2)}, u32[]{:S(2)}) collective-permute-start(bf16[4,80,768]{2,1,0:T(8,128)(2,1)S(1)} %pad_maximum_fusion.9), channel_id=1, source_target_pairs={{0,16},{16,0},{1,17},{17,1},{2,18},{18,2},{3,19},{19,3},{4,20},{20... | collective-permute-start | bytes 1474568 | tf_op jit(solution)/shard_map/ppermute | solution.py:284
  34.2 28.5 %collective-permute-start.6 = (bf16[8,80,768]{2,1,0:T(8,128)(2,1)S(1)}, bf16[8,80,768]{2,1,0:T(8,128)(2,1)S(1)}, u32[]{:S(2)}, u32[]{:S(2)}) collective-permute-start(bf16[8,80,768]{2,1,0:T(8,128)(2,1)S(1)} %get-tuple-element.183), channel_id=1, source_target_pairs={{0,2},{2,0},{1,3},{3,1},{4,6},{6,4},{5,7},{7,5},{8,10},{10,8},{9,1... | collective-permute-start | bytes 2949128 | tf_op jit(solution)/shard_map/ppermute | solution.py:284
  35.5 9.6 %collective-permute-start.9 = (bf16[1,216,768]{2,1,0:T(8,128)(2,1)S(1)}, bf16[1,216,768]{2,1,0:T(8,128)(2,1)S(1)}, u32[]{:S(2)}, u32[]{:S(2)}) collective-permute-start(bf16[1,216,768]{2,1,0:T(8,128)(2,1)S(1)} %bitcast.163), channel_id=1, source_target_pairs={{0,4},{4,8},{8,12},{12,0},{1,5},{5,9},{9,13},{13,1},{2,6},{6,10},{... | collective-permute-start | bytes 995336 | tf_op jit(solution)/shard_map/ppermute | solution.py:284
  38.6 22.8 %collective-permute-start.10 = (bf16[1,216,768]{2,1,0:T(8,128)(2,1)S(1)}, bf16[1,216,768]{2,1,0:T(8,128)(2,1)S(1)}, u32[]{:S(2)}, u32[]{:S(2)}) collective-permute-start(bf16[1,216,768]{2,1,0:T(8,128)(2,1)S(1)} %bitcast.164), channel_id=1, source_target_pairs={{0,8},{4,12},{8,0},{12,4},{1,9},{5,13},{9,1},{13,5},{2,10},{6,14},... | collective-permute-start | bytes 995336 | tf_op jit(solution)/shard_map/ppermute | solution.py:284
  38.6 22.8 %collective-permute-start.11 = (bf16[1,216,768]{2,1,0:T(8,128)(2,1)S(1)}, bf16[1,216,768]{2,1,0:T(8,128)(2,1)S(1)}, u32[]{:S(2)}, u32[]{:S(2)}) collective-permute-start(bf16[1,216,768]{2,1,0:T(8,128)(2,1)S(1)} %bitcast.165), channel_id=1, source_target_pairs={{0,12},{4,0},{8,4},{12,8},{1,13},{5,1},{9,5},{13,9},{2,14},{6,2},{... | collective-permute-start | bytes 995336 | tf_op jit(solution)/shard_map/ppermute | solution.py:284
  61.5 30.2 %collective-permute-start.12 = (bf16[4,216,768]{2,1,0:T(8,128)(2,1)S(1)}, bf16[4,216,768]{2,1,0:T(8,128)(2,1)S(1)}, u32[]{:S(2)}, u32[]{:S(2)}) collective-permute-start(bf16[4,216,768]{2,1,0:T(8,128)(2,1)S(1)} %pad_maximum_fusion.2), channel_id=1, source_target_pairs={{0,16},{16,0},{1,17},{17,1},{2,18},{18,2},{3,19},{19,3},{4,20},{20... | collective-permute-start | bytes 3981320 | tf_op jit(solution)/shard_map/ppermute | solution.py:284
  64.3 39.2 %collective-permute-start.7 = (bf16[16,80,768]{2,1,0:T(8,128)(2,1)}, bf16[16,80,768]{2,1,0:T(8,128)(2,1)}, u32[]{:S(2)}, u32[]{:S(2)}) collective-permute-start(bf16[16,80,768]{2,1,0:T(8,128)(2,1)} %get-tuple-element.172), channel_id=1, source_target_pairs={{0,1},{1,0},{2,3},{3,2},{4,5},{5,4},{6,7},{7,6},{8,9},{9,8},{10,11... | collective-permute-start | bytes 5898248 | tf_op jit(solution)/shard_map/ppermute | solution.py:284
  95.8 57.9 %collective-permute-start.13 = (bf16[8,216,768]{2,1,0:T(8,128)(2,1)}, bf16[8,216,768]{2,1,0:T(8,128)(2,1)S(1)}, u32[]{:S(2)}, u32[]{:S(2)}) collective-permute-start(bf16[8,216,768]{2,1,0:T(8,128)(2,1)} %get-tuple-element.160), channel_id=1, source_target_pairs={{0,2},{2,0},{1,3},{3,1},{4,6},{6,4},{5,7},{7,5},{8,10},{10,8},{9,1... | collective-permute-start | bytes 7962632 | tf_op jit(solution)/shard_map/ppermute | solution.py:284
  98.6 61.0 %collective-permute-start = (bf16[1024,768]{0,1:T(8,128)(2,1)}, bf16[1024,768]{0,1:T(8,128)(2,1)}, u32[]{:S(2)}, u32[]{:S(2)}) collective-permute-start(bf16[1024,768]{0,1:T(8,128)(2,1)} %bitcast.162), channel_id=1, source_target_pairs={{0,0},{1,16},{16,1},{17,17},{2,2},{3,18},{18,3},{19,19},{4,4},{5,2... | collective-permute-start | bytes 4718600 | tf_op jit(solution)/shard_map/ppermute | solution.py:326
  156.4 63.2 %collective-permute-start.14 = (bf16[16,216,768]{2,1,0:T(8,128)(2,1)}, bf16[16,216,768]{2,1,0:T(8,128)(2,1)}, u32[]{:S(2)}, u32[]{:S(2)}) collective-permute-start(bf16[16,216,768]{2,1,0:T(8,128)(2,1)} %get-tuple-element.149), channel_id=1, source_target_pairs={{0,1},{1,0},{2,3},{3,2},{4,5},{5,4},{6,7},{7,6},{8,9},{9,8},{10,11... | collective-permute-start | bytes 15925256 | tf_op jit(solution)/shard_map/ppermute | solution.py:284
  166.1 12.6 %collective-permute-start.8 = (bf16[1024,1152]{1,0:T(8,128)(2,1)}, bf16[1024,1152]{1,0:T(8,128)(2,1)}, u32[]{:S(2)}, u32[]{:S(2)}) collective-permute-start(bf16[1024,1152]{1,0:T(8,128)(2,1)} %fusion.10), channel_id=1, source_target_pairs={{0,1},{1,0},{2,3},{3,2},{4,5},{5,4},{6,7},{7,6},{8,9},{9,8},{10,11... | collective-permute-start | bytes 7077896 | tf_op jit(solution)/shard_map/ppermute | solution.py:322
  167.8 106.6 %collective-permute-start.17 = (bf16[1024,768]{0,1:T(8,128)(2,1)}, bf16[1024,768]{0,1:T(8,128)(2,1)S(1)}, u32[]{:S(2)}, u32[]{:S(2)}) collective-permute-start(bf16[1024,768]{0,1:T(8,128)(2,1)} %bitcast.161), channel_id=1, source_target_pairs={{0,0},{1,16},{16,1},{17,17},{2,2},{3,18},{18,3},{19,19},{4,4},{5,2... | collective-permute-start | bytes 4718600 | tf_op jit(solution)/shard_map/ppermute | solution.py:326
  219.3 24.7 %collective-permute-start.15 = (bf16[1024,384]{1,0:T(8,128)(2,1)S(1)}, bf16[1024,384]{1,0:T(8,128)(2,1)}, u32[]{:S(2)}, u32[]{:S(2)}) collective-permute-start(bf16[1024,384]{1,0:T(8,128)(2,1)S(1)} %get-tuple-element.49.o_far), channel_id=1, source_target_pairs={{0,1},{1,0},{2,3},{3,2},{4,5},{5,4},{6,7},{7,6},{8,9},{9,8},{10,11... | collective-permute-start | bytes 2359304 | tf_op jit(solution)/shard_map/ppermute | solution.py:322
  320.4 26.1 %collective-permute-start.18 = (bf16[1024,384]{1,0:T(8,128)(2,1)}, bf16[1024,384]{1,0:T(8,128)(2,1)}, u32[]{:S(2)}, u32[]{:S(2)}) collective-permute-start(bf16[1024,384]{1,0:T(8,128)(2,1)} %convolution_convert_fusion.4), channel_id=1, source_target_pairs={{0,1},{1,0},{2,3},{3,2},{4,5},{5,4},{6,7},{7,6},{8,9},{9,8},{10,11... | collective-permute-start | bytes 2359304 | tf_op jit(solution)/shard_map/ppermute | solution.py:322
  429.0 17.8 %collective-permute-start.19 = (bf16[1024,1152]{1,0:T(8,128)(2,1)}, bf16[1024,1152]{1,0:T(8,128)(2,1)}, u32[]{:S(2)}, u32[]{:S(2)}) collective-permute-start(bf16[1024,1152]{1,0:T(8,128)(2,1)} %pad_maximum_fusion.1), channel_id=1, source_target_pairs={{0,1},{1,0},{2,3},{3,2},{4,5},{5,4},{6,7},{7,6},{8,9},{9,8},{10,11... | collective-permute-start | bytes 7077896 | tf_op jit(solution)/shard_map/ppermute | solution.py:322
  442.8 52.0 %collective-permute-start.27 = (bf16[16,192,768]{2,1,0:T(8,128)(2,1)}, bf16[16,192,768]{2,1,0:T(8,128)(2,1)}, u32[]{:S(2)}, u32[]{:S(2)}) collective-permute-start(bf16[16,192,768]{2,1,0:T(8,128)(2,1)} %slice.593), channel_id=1, source_target_pairs={{0,1},{1,0},{2,3},{3,2},{4,5},{5,4},{6,7},{7,6},{8,9},{9,8},{10,11... | collective-permute-start | bytes 14155784 | tf_op jit(solution)/shard_map/ppermute | solution.py:296
  494.4 8.6 %collective-permute-start.21 = (bf16[16,104,768]{2,1,0:T(8,128)(2,1)S(1)}, bf16[16,104,768]{2,1,0:T(8,128)(2,1)S(1)}, u32[]{:S(2)}, u32[]{:S(2)}) collective-permute-start(bf16[16,104,768]{2,1,0:T(8,128)(2,1)S(1)} %slice.570), channel_id=1, source_target_pairs={{0,1},{1,0},{2,3},{3,2},{4,5},{5,4},{6,7},{7,6},{8,9},{9,8},{10,11... | collective-permute-start | bytes 7667720 | tf_op jit(solution)/shard_map/ppermute | solution.py:296
  500.2 80.5 %collective-permute-start.28 = (bf16[8,192,768]{2,1,0:T(8,128)(2,1)S(1)}, bf16[8,192,768]{2,1,0:T(8,128)(2,1)S(1)}, u32[]{:S(2)}, u32[]{:S(2)}) collective-permute-start(bf16[8,192,768]{2,1,0:T(8,128)(2,1)S(1)} %slice.595), channel_id=1, source_target_pairs={{0,2},{2,0},{1,3},{3,1},{4,6},{6,4},{5,7},{7,5},{8,10},{10,8},{9,1... | collective-permute-start | bytes 7077896 | tf_op jit(solution)/shard_map/ppermute | solution.py:296
  500.5 104.7 %collective-permute-start.16 = (bf16[1024,768]{0,1:T(8,128)(2,1)}, bf16[1024,768]{0,1:T(8,128)(2,1)}, u32[]{:S(2)}, u32[]{:S(2)}) collective-permute-start(bf16[1024,768]{0,1:T(8,128)(2,1)} %get-tuple-element.148), channel_id=1, source_target_pairs={{0,0},{1,16},{16,1},{17,17},{2,2},{3,18},{18,3},{19,19},{4,4},{5,2... | collective-permute-start | bytes 4718600 | tf_op jit(solution)/shard_map/ppermute | solution.py:326
  504.0 76.2 %collective-permute-start.22 = (bf16[8,104,768]{2,1,0:T(8,128)(2,1)S(1)}, bf16[8,104,768]{2,1,0:T(8,128)(2,1)S(1)}, u32[]{:S(2)}, u32[]{:S(2)}) collective-permute-start(bf16[8,104,768]{2,1,0:T(8,128)(2,1)S(1)} %slice.572), channel_id=1, source_target_pairs={{0,2},{2,0},{1,3},{3,1},{4,6},{6,4},{5,7},{7,5},{8,10},{10,8},{9,1... | collective-permute-start | bytes 3833864 | tf_op jit(solution)/shard_map/ppermute | solution.py:296
  513.2 94.5 %collective-permute-start.20 = (bf16[1024,768]{0,1:T(8,128)(2,1)}, bf16[1024,768]{0,1:T(8,128)(2,1)}, u32[]{:S(2)}, u32[]{:S(2)}) collective-permute-start(bf16[1024,768]{0,1:T(8,128)(2,1)} %add_convert_fusion.3), channel_id=1, source_target_pairs={{0,0},{1,16},{16,1},{17,17},{2,2},{3,18},{18,3},{19,19},{4,4},{5,2... | collective-permute-start | bytes 4718600 | tf_op jit(solution)/shard_map/ppermute | solution.py:326
  580.6 14.9 %collective-permute-start.23 = (bf16[4,104,768]{2,1,0:T(8,128)(2,1)S(1)}, bf16[4,104,768]{2,1,0:T(8,128)(2,1)S(1)}, u32[]{:S(2)}, u32[]{:S(2)}) collective-permute-start(bf16[4,104,768]{2,1,0:T(8,128)(2,1)S(1)} %slice.574), channel_id=1, source_target_pairs={{0,16},{16,0},{1,17},{17,1},{2,18},{18,2},{3,19},{19,3},{4,20},{20... | collective-permute-start | bytes 1916936 | tf_op jit(solution)/shard_map/ppermute | solution.py:296
  582.5 38.6 %collective-permute-start.29 = (bf16[4,192,768]{2,1,0:T(8,128)(2,1)}, bf16[4,192,768]{2,1,0:T(8,128)(2,1)}, u32[]{:S(2)}, u32[]{:S(2)}) collective-permute-start(bf16[4,192,768]{2,1,0:T(8,128)(2,1)} %slice.597), channel_id=1, source_target_pairs={{0,16},{16,0},{1,17},{17,1},{2,18},{18,2},{3,19},{19,3},{4,20},{20... | collective-permute-start | bytes 3538952 | tf_op jit(solution)/shard_map/ppermute | solution.py:296
  596.5 13.8 %collective-permute-start.26 = (bf16[1,104,768]{2,1,0:T(8,128)(2,1)}, bf16[1,104,768]{2,1,0:T(8,128)(2,1)S(1)}, u32[]{:S(2)}, u32[]{:S(2)}) collective-permute-start(bf16[1,104,768]{2,1,0:T(8,128)(2,1)} %get-tuple-element.175), channel_id=1, source_target_pairs={{0,12},{4,0},{8,4},{12,8},{1,13},{5,1},{9,5},{13,9},{2,14},{6,2},{... | collective-permute-start | bytes 479240 | tf_op jit(solution)/shard_map/ppermute | solution.py:296
  602.0 16.2 %collective-permute-start.25 = (bf16[1,104,768]{2,1,0:T(8,128)(2,1)}, bf16[1,104,768]{2,1,0:T(8,128)(2,1)S(1)}, u32[]{:S(2)}, u32[]{:S(2)}) collective-permute-start(bf16[1,104,768]{2,1,0:T(8,128)(2,1)} %get-tuple-element.176), channel_id=1, source_target_pairs={{0,8},{4,12},{8,0},{12,4},{1,9},{5,13},{9,1},{13,5},{2,10},{6,14},... | collective-permute-start | bytes 479240 | tf_op jit(solution)/shard_map/ppermute | solution.py:296
  605.1 13.1 %collective-permute-start.24 = (bf16[1,104,768]{2,1,0:T(8,128)(2,1)S(1)}, bf16[1,104,768]{2,1,0:T(8,128)(2,1)}, u32[]{:S(2)}, u32[]{:S(2)}) collective-permute-start(bf16[1,104,768]{2,1,0:T(8,128)(2,1)S(1)} %get-tuple-element.174), channel_id=1, source_target_pairs={{0,4},{4,8},{8,12},{12,0},{1,5},{5,9},{9,13},{13,1},{2,6},{6,10},{... | collective-permute-start | bytes 479240 | tf_op jit(solution)/shard_map/ppermute | solution.py:296
  622.7 12.9 %collective-permute-start.32 = (bf16[1,192,768]{2,1,0:T(8,128)(2,1)S(1)}, bf16[1,192,768]{2,1,0:T(8,128)(2,1)S(1)}, u32[]{:S(2)}, u32[]{:S(2)}) collective-permute-start(bf16[1,192,768]{2,1,0:T(8,128)(2,1)S(1)} %get-tuple-element.162), channel_id=1, source_target_pairs={{0,12},{4,0},{8,4},{12,8},{1,13},{5,1},{9,5},{13,9},{2,14},{6,2},{... | collective-permute-start | bytes 884744 | tf_op jit(solution)/shard_map/ppermute | solution.py:296
  628.2 27.2 %collective-permute-start.31 = (bf16[1,192,768]{2,1,0:T(8,128)(2,1)S(1)}, bf16[1,192,768]{2,1,0:T(8,128)(2,1)S(1)}, u32[]{:S(2)}, u32[]{:S(2)}) collective-permute-start(bf16[1,192,768]{2,1,0:T(8,128)(2,1)S(1)} %get-tuple-element.163), channel_id=1, source_target_pairs={{0,8},{4,12},{8,0},{12,4},{1,9},{5,13},{9,1},{13,5},{2,10},{6,14},... | collective-permute-start | bytes 884744 | tf_op jit(solution)/shard_map/ppermute | solution.py:296
  631.3 24.1 %collective-permute-start.30 = (bf16[1,192,768]{2,1,0:T(8,128)(2,1)S(1)}, bf16[1,192,768]{2,1,0:T(8,128)(2,1)S(1)}, u32[]{:S(2)}, u32[]{:S(2)}) collective-permute-start(bf16[1,192,768]{2,1,0:T(8,128)(2,1)S(1)} %get-tuple-element.161), channel_id=1, source_target_pairs={{0,4},{4,8},{8,12},{12,0},{1,5},{5,9},{9,13},{13,1},{2,6},{6,10},{... | collective-permute-start | bytes 884744 | tf_op jit(solution)/shard_map/ppermute | solution.py:296
  (55 other events, 680.1 us)

commit v2 on v1

v2 whole, which is shorter than its diff:
```python
import jax
import jax.numpy as jnp
import numpy as np
from jax import lax
from jax.sharding import Mesh, PartitionSpec as P
from jax.experimental import pallas as pl
from jax.experimental.pallas import tpu as pltpu

D = 768
HALF = D // 2
HD = 64
UNITS = 16
SLOTS = 16
ROWS = D // SLOTS
PAIRS = HALF // 128
LOG2E = 1.4426950408889634
LN2 = 0.6931471805599453
BIG = 1e30
TQ = 512
STEP = 512
TM = 256
norm_eps = 1e-12
bf16 = jnp.bfloat16
f32 = jnp.float32
NT = (((1,), (1,)), ((), ()))
NN = (((1,), (0,)), ((), ()))
TN = (((0,), (0,)), ((), ()))
VMEM_CAP = 58 << 20


def mxu(a, b, dims=NN):
    return lax.dot_general(a, b, dims, preferred_element_type=f32)


def shape(size, kind=bf16):
    return jax.ShapeDtypeStruct(size, kind)


def params(axes=1):
    return pltpu.CompilerParams(dimension_semantics=("arbitrary",) * axes, vmem_limit_bytes=VMEM_CAP)


def cost(flops, moved):
    return pl.CostEstimate(flops=int(flops), bytes_accessed=int(moved), transcendentals=0)


def tie(value, *others):
    return lax.optimization_barrier((value,) + others)[0]


def lanes(rows):
    return lax.broadcasted_iota(jnp.int32, (rows, 128), 1)


def seg_rows(segs_ref, base_block, rows):
    place = lax.broadcasted_iota(jnp.int32, (rows, 128), 0)
    out = jnp.zeros((rows, 128), jnp.int32)
    for b in range(rows // 128):
        out = jnp.where(place >= b * 128, segs_ref[base_block + b], out)
    return out


def split3(v):
    hi = v.astype(bf16).astype(f32)
    mid = (v - hi).astype(bf16).astype(f32)
    return hi, mid, v - hi - mid


def both_heads(pair_rows):
    lane = lanes(pair_rows.shape[0])
    zero = jnp.zeros_like(pair_rows)
    first = jnp.where(lane < HD, pair_rows, zero)
    return jnp.concatenate([first, jnp.where(lane < HD, zero, pair_rows)], axis=0)


def fill_keys(segs_ref, k_in, v_in, k_aug, v_aug):
    for at in range(0, k_in.shape[0], STEP):
        rows = slice(at, at + STEP)
        lane = lanes(STEP)
        hot = (lane == seg_rows(segs_ref, at // 128, STEP)) | ((lane >= 64) & (lane < 67))
        k_aug[rows, :128] = k_in[rows, :]
        k_aug[rows, 128:] = jnp.where(hot, 1.0, 0.0).astype(bf16)
        v_aug[rows, :128] = v_in[rows, :]
        v_aug[rows, 128:] = jnp.ones((STEP, 128), bf16)


def attend_body(segs_ref, q_in, k_in, v_in, *refs):
    o_own, o_far, lse_ref, k_aug, v_aug = refs[-5:]
    i = pl.program_id(1)
    n_half = pl.num_programs(1) // 2

    @pl.when(i == 0)
    def _():
        fill_keys(segs_ref, k_in, v_in, k_aug, v_aug)

    lane = lanes(TQ)
    seg = seg_rows(segs_ref, i * (TQ // 128), TQ)
    off = jnp.where((lane < 16) & (lane != seg), -BIG, 0.0).astype(bf16)
    q_aug = jnp.concatenate([both_heads(q_in[...]), jnp.concatenate([off, off], axis=0)], axis=1)
    top = None
    acc = None
    for at in range(0, k_aug.shape[0], STEP):
        s = mxu(q_aug, k_aug[at : at + STEP, :], NT)
        here = jnp.max(s, axis=1, keepdims=True)
        new_top = here if top is None else jnp.maximum(top, here)
        p = jnp.exp2(s - new_top).astype(bf16)
        add = mxu(p, v_aug[at : at + STEP, :])
        acc = add if acc is None else acc * jnp.exp2(top - new_top) + add
        top = new_top
    both = jnp.where(lane < HD, acc[:TQ, :128], acc[TQ:, :128])
    sums = jnp.where(lane < HD, acc[:TQ, 128:], acc[TQ:, 128:])
    tops = jnp.where(lane < HD, top[:TQ], top[TQ:])
    out = (both / sums).astype(bf16)
    lse_ref[...] = tops + jnp.log2(sums)

    @pl.when(i < n_half)
    def _():
        o_own[...] = out

    @pl.when(i >= n_half)
    def _():
        o_far[...] = out


def anyspec():
    return pl.BlockSpec(memory_space=pl.ANY)


def pair_specs(n_half, first):
    own = pl.BlockSpec((TQ, 128), lambda h, i, *_: (jnp.minimum(i, n_half - 1), first + h))
    far = pl.BlockSpec((TQ, 128), lambda h, i, *_: (jnp.maximum(i - n_half, 0), first + h))
    return own, far


def attention(segs, qkv, first, count, prev):
    total = qkv.shape[0]
    half = total // 2
    n_half = half // TQ
    own, far = pair_specs(n_half, first)
    row = pl.BlockSpec((TQ, 128), lambda h, i, *_: (i, first + h))
    whole = lambda part: pl.BlockSpec((total, 128), lambda h, i, *_: (0, part * PAIRS + first + h))
    prev = () if prev is None else tuple(prev)
    return pl.pallas_call(
        attend_body,
        grid_spec=pltpu.PrefetchScalarGridSpec(
            num_scalar_prefetch=1,
            grid=(count, 2 * n_half),
            in_specs=[row, whole(1), whole(2)] + [anyspec()] * len(prev),
            out_specs=[own, far, row],
            scratch_shapes=[pltpu.VMEM((total, 256), bf16), pltpu.VMEM((total, 256), bf16)],
        ),
        out_shape=[shape((half, HALF)), shape((half, HALF)), shape((total, HALF), f32)],
        input_output_aliases={4 + j: j for j in range(len(prev))},
        compiler_params=params(2),
        cost_estimate=cost(count * total * total * 2048, total * 128 * 2 * 8),
    )(segs, qkv, qkv, qkv, *prev)


def attend_back_body(segs_ref, q_in, k_in, v_in, o_own, o_far, d_own, d_far, lse_ref, *refs):
    dq_out, dk_out, dv_out, k_aug, v_aug, dk_acc, dv_acc = refs[-7:]
    i = pl.program_id(1)
    n = pl.num_programs(1)

    @pl.when(i == 0)
    def _():
        fill_keys(segs_ref, k_in, v_in, k_aug, v_aug)
        dk_acc[...] = jnp.zeros_like(dk_acc)
        dv_acc[...] = jnp.zeros_like(dv_acc)

    near = i < n // 2
    d_rows = jnp.where(near, d_own[...], d_far[...])
    o_rows = jnp.where(near, o_own[...], o_far[...])
    lane = lanes(TQ)
    seg = seg_rows(segs_ref, i * (TQ // 128), TQ)
    off = jnp.where((lane < 16) & (lane != seg), -BIG, 0.0)
    prod = d_rows.astype(f32) * o_rows.astype(f32)
    q_side, d_side = [], []
    for head in range(2):
        mine = (lane < HD) if head == 0 else (lane >= HD)
        dot_row = jnp.sum(jnp.where(mine, prod, 0.0), axis=1, keepdims=True)
        lse = jnp.broadcast_to(lse_ref[:, head * HD : head * HD + 1], (TQ, 128))
        for side, value, rest in ((q_side, -lse, off), (d_side, -jnp.broadcast_to(dot_row, (TQ, 128)), 0.0)):
            h, m, l = split3(value)
            cols = jnp.where(lane == 64, h, jnp.where(lane == 65, m, jnp.where(lane == 66, l, rest)))
            side.append(cols.astype(bf16))
    q2 = both_heads(q_in[...])
    d2 = both_heads(d_rows)
    q_aug = jnp.concatenate([q2, jnp.concatenate(q_side, axis=0)], axis=1)
    d_aug = jnp.concatenate([d2, jnp.concatenate(d_side, axis=0)], axis=1)
    dq = None
    for at in range(0, k_aug.shape[0], STEP):
        rows = slice(at, at + STEP)
        keys = k_aug[rows, :]
        p = jnp.exp2(mxu(q_aug, keys, NT))
        ds = (p * mxu(d_aug, v_aug[rows, :], NT)).astype(bf16)
        dv_acc[rows, :] += mxu(p.astype(bf16), d2, TN)
        dk_acc[rows, :] += mxu(ds, q2, TN)
        add = mxu(ds, keys[:, :128])
        dq = add if dq is None else dq + add
    dq_out[...] = (jnp.where(lane < HD, dq[:TQ], dq[TQ:]) * (HD ** -0.5)).astype(bf16)

    @pl.when(i == n - 1)
    def _():
        dk_out[...] = (dk_acc[...] * LN2).astype(bf16)
        dv_out[...] = dv_acc[...].astype(bf16)


def attention_back(segs, qkv, o_own, o_far, d_own, d_far, lse, first, count, prev):
    total = qkv.shape[0]
    half = total // 2
    n_half = half // TQ
    own, far = pair_specs(n_half, first)
    row = pl.BlockSpec((TQ, 128), lambda h, i, *_: (i, first + h))
    whole = lambda part: pl.BlockSpec((total, 128), lambda h, i, *_: (0, part * PAIRS + first + h))
    prev = () if prev is None else tuple(prev)
    return pl.pallas_call(
        attend_back_body,
        grid_spec=pltpu.PrefetchScalarGridSpec(
            num_scalar_prefetch=1,
            grid=(count, 2 * n_half),
            in_specs=[row, whole(1), whole(2), own, far, own, far, row] + [anyspec()] * len(prev),
            out_specs=[row, whole(0), whole(0)],
            scratch_shapes=[
                pltpu.VMEM((total, 256), bf16),
                pltpu.VMEM((total, 256), bf16),
                pltpu.VMEM((total, 128), f32),
                pltpu.VMEM((total, 128), f32),
            ],
        ),
        out_shape=[shape((total, HALF))] * 3,
        input_output_aliases={9 + j: j for j in range(len(prev))},
        compiler_params=params(2),
        cost_estimate=cost(count * total * total * 5120, total * 128 * 2 * 12),
    )(segs, qkv, qkv, qkv, o_own, o_far, d_own, d_far, lse, *prev)


def each_slot(pieces):
    at = 0
    for ref in pieces:
        for slot in range(ref.shape[0]):
            yield at, ref, slot
            at += 1


def wait_for(dst, sem):
    pltpu.make_async_copy(dst, dst, sem).wait()


def proj_body(info, t_own, t_got, bias, *refs):
    pieces, (out, w_out, w, sem) = refs[:-4], refs[-4:]
    i = pl.program_id(0)

    @pl.when(i == 0)
    def _():
        for at, ref, slot in each_slot(pieces):
            rows = pl.ds(pl.multiple_of(info[1 + at] * ROWS, ROWS), ROWS)
            for j in range(3):
                src = ref.at[slot, j * ROWS : (j + 1) * ROWS, :]
                pltpu.make_async_copy(src, w.at[rows, j * HALF : (j + 1) * HALF], sem).start()
        wait_for(w, sem)

    tile = jnp.where(i < pl.num_programs(0) // 2, t_own[...], t_got[...])
    for j in range(3):
        cols = slice(j * HALF, (j + 1) * HALF)
        part = mxu(tile, w[:, cols]) + bias[0:1, cols]
        if j == 0:
            part = part * (LOG2E * HD ** -0.5)
        out[:, cols] = part.astype(bf16)
    w_out[...] = w[...]


def project(info, t_own, t_got, bias, pieces):
    half = t_own.shape[0]
    tile = 512
    n_half = half // tile
    own = pl.BlockSpec((tile, D), lambda i, *_: (jnp.minimum(i, n_half - 1), 0))
    got = pl.BlockSpec((tile, D), lambda i, *_: (jnp.maximum(i - n_half, 0), 0))
    return pl.pallas_call(
        proj_body,
        grid_spec=pltpu.PrefetchScalarGridSpec(
            num_scalar_prefetch=1,
            grid=(2 * n_half,),
            in_specs=[own, got, pl.BlockSpec((1, 3 * HALF), lambda i, *_: (0, 0))] + [anyspec()] * len(pieces),
            out_specs=[
                pl.BlockSpec((tile, 3 * HALF), lambda i, *_: (i, 0)),
                pl.BlockSpec((D, 3 * HALF), lambda i, *_: (0, 0)),
            ],
            scratch_shapes=[pltpu.VMEM((D, 3 * HALF), bf16), pltpu.SemaphoreType.DMA],
        ),
        out_shape=[shape((2 * half, 3 * HALF)), shape((D, 3 * HALF))],
        compiler_params=params(),
        cost_estimate=cost(half * D * D * 6, half * D * 12),
    )(info, t_own, t_got, bias, *pieces)


def norm_stats(rows):
    mean = jnp.mean(rows, axis=-1, keepdims=True)
    centered = rows - mean
    var = jnp.mean(centered * centered, axis=-1, keepdims=True)
    rstd = lax.rsqrt(var + norm_eps)
    return centered * rstd, rstd


def norm_back(grad, unit, rstd, gain):
    eg = grad * gain
    mean_eg = jnp.mean(eg, axis=-1, keepdims=True)
    mean_en = jnp.mean(eg * unit, axis=-1, keepdims=True)
    return (eg - mean_eg - unit * mean_en) * rstd


def mid_body(info, tok, o_own, o_got, back, vecs, bias_in, *refs):
    n_out = 10
    outs, scratch = refs[-n_out - 5 : -5], refs[-5:]
    pieces = refs[: -n_out - 5]
    own_pieces, far_pieces = pieces[: len(pieces) // 2], pieces[len(pieces) // 2 :]
    out_rows, act_out, ig_out, low_out, branch_out, attn_out, resid_out, d_own, d_far, sums = outs
    w_out, w_in, w_down, slope, sems = scratch
    ff_cols = w_in.shape[1] // D
    me = info[0]

    @pl.when(pl.program_id(0) == 0)
    def _():
        for kind in range(3):
            for here, part in ((me, own_pieces), (1 - me, far_pieces)):
                for at, ref, slot in each_slot(part):
                    chip = info[1 + at]
                    lane0 = pl.multiple_of(here * HALF, HALF)
                    rows = pl.ds(pl.multiple_of(chip * ROWS, ROWS), ROWS)
                    if kind == 0:
                        pltpu.make_async_copy(ref.at[slot, 0:ROWS, :], w_out.at[rows, pl.ds(lane0, HALF)], sems.at[0]).start()
                    elif kind == 1:
                        for j in range(ff_cols):
                            src = ref.at[slot, (1 + j) * ROWS : (2 + j) * ROWS, :]
                            dst = w_in.at[rows, pl.ds(pl.multiple_of(lane0 + j * D, HALF), HALF)]
                            pltpu.make_async_copy(src, dst, sems.at[1]).start()
                    else:
                        size = ROWS * ff_cols
                        src = ref.at[slot, (1 + ff_cols) * ROWS : (1 + 2 * ff_cols) * ROWS, :]
                        dst = w_down.at[pl.ds(pl.multiple_of(chip * size, size), size), pl.ds(lane0, HALF)]
                        pltpu.make_async_copy(src, dst, sems.at[2]).start()
        sums[...] = jnp.zeros_like(sums)
        wait_for(w_out, sems.at[0])

    bias_o, gain1, shift1 = vecs[0:1, :], vecs[1:2, :], vecs[2:3, :]
    bias_d, gain2, shift2 = vecs[3:4, :], vecs[4:5, :], vecs[5:6, :]
    mine = w_out[pl.ds(pl.multiple_of(me * HALF, HALF), HALF), :]
    other = w_out[pl.ds(pl.multiple_of((1 - me) * HALF, HALF), HALF), :]
    resid = tok[...].astype(f32) + mxu(o_own[...], mine) + mxu(o_got[...], other) + bias_o
    unit1, rstd1 = norm_stats(resid)
    hidden = unit1 * gain1 + shift1
    low = hidden.astype(bf16)
    low_out[...] = low

    @pl.when(pl.program_id(0) == 0)
    def _():
        wait_for(w_in, sems.at[1])
        wait_for(w_down, sems.at[2])

    branch = bias_d
    for j in range(ff_cols):
        cols = slice(j * D, (j + 1) * D)
        inner = mxu(low, w_in[:, cols]) + bias_in[:, cols]
        phi = 0.5 + 0.5 * lax.erf(inner * (0.5 ** 0.5))
        act = (inner * phi).astype(bf16)
        act_out[:, cols] = act
        slope[:, cols] = phi + inner * (jnp.exp2(inner * inner * (-0.5 * LOG2E)) * 0.3989422804014327)
        branch = branch + mxu(act, w_down[cols, :])
    unit2, rstd2 = norm_stats(hidden + branch)
    out_rows[...] = (unit2 * gain2 + shift2).astype(bf16)
    grad = back[...].astype(f32)
    resid2 = norm_back(grad, unit2, rstd2, gain2)
    low_branch = resid2.astype(bf16)
    branch_out[...] = low_branch
    hidden_grad = resid2
    for j in range(ff_cols):
        cols = slice(j * D, (j + 1) * D)
        ig = (mxu(low_branch, w_down[cols, :], NT) * slope[:, cols]).astype(bf16)
        ig_out[:, cols] = ig
        hidden_grad = hidden_grad + mxu(ig, w_in[:, cols], NT)
        sums[3 + j : 4 + j, :] += jnp.sum(ig.astype(f32), axis=0, keepdims=True)
    resid1 = norm_back(hidden_grad, unit1, rstd1, gain1)
    resid_out[...] = resid1
    attn_grad = resid1.astype(bf16)
    attn_out[...] = attn_grad
    d_own[...] = mxu(attn_grad, mine, NT).astype(bf16)
    d_far[...] = mxu(attn_grad, other, NT).astype(bf16)
    rows = (
        (0, attn_grad.astype(f32)),
        (1, hidden_grad * unit1),
        (2, hidden_grad),
        (3 + ff_cols, low_branch.astype(f32)),
        (4 + ff_cols, grad * unit2),
        (5 + ff_cols, grad),
    )
    for at, value in rows:
        sums[at : at + 1, :] += jnp.sum(value, axis=0, keepdims=True)


def middle(info, tok, o_own, o_got, back, vecs, bias_in, own_pieces, far_pieces):
    half = tok.shape[0]
    ff = bias_in.shape[1]
    wide = pl.BlockSpec((TM, D), lambda i, *_: (i, 0))
    thin = pl.BlockSpec((TM, HALF), lambda i, *_: (i, 0))
    full = pl.BlockSpec((TM, ff), lambda i, *_: (i, 0))
    fixed = lambda rows, cols: pl.BlockSpec((rows, cols), lambda i, *_: (0, 0))
    pieces = tuple(own_pieces) + tuple(far_pieces)
    return pl.pallas_call(
        mid_body,
        grid_spec=pltpu.PrefetchScalarGridSpec(
            num_scalar_prefetch=1,
            grid=(half // TM,),
            in_specs=[wide, thin, thin, wide, fixed(8, D), fixed(1, ff)] + [anyspec()] * len(pieces),
            out_specs=[wide, full, full, wide, wide, wide, wide, thin, thin, fixed(16, D)],
            scratch_shapes=[
                pltpu.VMEM((D, D), bf16),
                pltpu.VMEM((D, ff), bf16),
                pltpu.VMEM((ff, D), bf16),
                pltpu.VMEM((TM, ff), f32),
                pltpu.SemaphoreType.DMA((3,)),
            ],
        ),
        out_shape=[
            shape((half, D)),
            shape((half, ff)),
            shape((half, ff)),
            shape((half, D)),
            shape((half, D)),
            shape((half, D)),
            shape((half, D), f32),
            shape((half, HALF)),
            shape((half, HALF)),
            shape((16, D), f32),
        ],
        compiler_params=params(),
        cost_estimate=cost(half * D * (D + 2 * ff) * 4, half * D * 40),
    )(info, tok, o_own, o_got, back, vecs, bias_in, *pieces)


def wgrad_body(info, act, ig, low, branch, o_own, o_got, attn_grad, keep, send, res_in, res_down, res_out, sems):
    j = pl.program_id(0)
    n = pl.num_programs(0)
    me = info[0]
    par = lax.rem(j, 2)
    down_rows = ROWS * n
    per_step = SLOTS // n

    @pl.when(j == 0)
    def _():
        for at, dst in ((0, send), (1, keep)):
            half_at = me if at == 1 else 1 - me
            lane = pl.ds(pl.multiple_of(half_at * HALF, HALF), HALF)
            grad = attn_grad[:, lane]
            for here, rows in ((me, o_own), (1 - me, o_got)):
                spot = pl.ds(pl.multiple_of(here * HALF, HALF), HALF)
                res_out[at, spot, :] = mxu(rows[...], grad, TN).astype(bf16)
            for chip in range(SLOTS):
                src = res_out.at[at, chip * ROWS : (chip + 1) * ROWS, :]
                pltpu.make_async_copy(src, dst.at[info[1 + chip], 0:ROWS, :], sems.at[2]).start()

    for at, dst in ((0, send), (1, keep)):
        half_at = me if at == 1 else 1 - me
        lane = pl.ds(pl.multiple_of(half_at * HALF, HALF), HALF)
        res_in[par, at] = mxu(low[...], ig[:, lane], TN).astype(bf16)
        for chip in range(SLOTS):
            src = res_in.at[par, at, chip * ROWS : (chip + 1) * ROWS, :]
            spot = pl.ds(pl.multiple_of((1 + j) * ROWS, ROWS), ROWS)
            pltpu.make_async_copy(src, dst.at[info[1 + chip], spot, :], sems.at[par]).start()
        res_down[par, at] = mxu(act[...], branch[:, lane], TN).astype(bf16)
        for q in range(per_step):
            src = res_down.at[par, at, q * down_rows : (q + 1) * down_rows, :]
            slot = info[1 + j * per_step + q]
            pltpu.make_async_copy(src, dst.at[slot, ROWS * (1 + n) : ROWS * (1 + 2 * n), :], sems.at[par]).start()

    def settle(which):
        wait_for(res_in.at[which], sems.at[which])
        wait_for(res_down.at[which], sems.at[which])

    @pl.when(j > 0)
    def _():
        settle(1 - par)

    @pl.when(j == n - 1)
    def _():
        settle(par)
        wait_for(res_out, sems.at[2])


def weight_grads(info, act, ig, low, branch, o_own, o_got, attn_grad):
    half, ff = act.shape
    n = ff // D
    strip = pl.BlockSpec((half, D), lambda j, *_: (0, j))
    fixed = lambda cols: pl.BlockSpec((half, cols), lambda j, *_: (0, 0))
    size = (SLOTS, ROWS * (1 + 2 * n), HALF)
    return pl.pallas_call(
        wgrad_body,
        grid_spec=pltpu.PrefetchScalarGridSpec(
            num_scalar_prefetch=1,
            grid=(n,),
            in_specs=[strip, strip, fixed(D), fixed(D), fixed(HALF), fixed(HALF), fixed(D)],
            out_specs=[anyspec(), anyspec()],
            scratch_shapes=[
                pltpu.VMEM((2, 2, D, HALF), bf16),
                pltpu.VMEM((2, 2, D, HALF), bf16),
                pltpu.VMEM((2, D, HALF), bf16),
                pltpu.SemaphoreType.DMA((3,)),
            ],
        ),
        out_shape=[shape(size), shape(size)],
        compiler_params=params(),
        cost_estimate=cost(half * D * (D + 2 * ff) * 2, half * ff * 8),
    )(info, act, ig, low, branch, o_own, o_got, attn_grad)


def qkv_grad_body(info, small, t_own, t_got, dq, dk, dv, out, t_all, d_all, res, res_small, sems):
    half = t_own.shape[0]
    pltpu.make_async_copy(t_own, t_all.at[0:half, :], sems.at[0]).start()
    pltpu.make_async_copy(t_got, t_all.at[half:, :], sems.at[0]).start()
    for j, src in enumerate((dq, dk, dv)):
        pltpu.make_async_copy(src, d_all.at[j], sems.at[1 + j]).start()
    wait_for(t_all, sems.at[0])
    res_small[...] = small[...].astype(bf16)
    row = lax.broadcasted_iota(jnp.int32, (16, HALF), 0)
    for j in range(3):
        wait_for(d_all.at[j], sems.at[1 + j])
        grads = d_all[j]
        res[j] = mxu(t_all[...], grads, TN).astype(bf16)
        for chip in range(SLOTS):
            src = res.at[j, chip * ROWS : (chip + 1) * ROWS, :]
            pltpu.make_async_copy(src, out.at[info[1 + chip], j * ROWS : (j + 1) * ROWS, :], sems.at[4]).start()
        if j != 1:
            total = jnp.sum(grads.astype(f32), axis=0, keepdims=True)
            place = 14 if j == 0 else 15
            res_small[...] = jnp.where(row == place, total, res_small[...].astype(f32)).astype(bf16)
    for slot in range(SLOTS):
        pltpu.make_async_copy(res_small, out.at[slot, 3 * ROWS : 3 * ROWS + 16, :], sems.at[5]).start()
    wait_for(res, sems.at[4])
    for slot in range(SLOTS):
        pltpu.make_async_copy(res_small, out.at[slot, 3 * ROWS : 3 * ROWS + 16, :], sems.at[5]).wait()


def qkv_grads(info, small, t_own, t_got, dq, dk, dv):
    total = dq.shape[0]
    return pl.pallas_call(
        qkv_grad_body,
        grid_spec=pltpu.PrefetchScalarGridSpec(
            num_scalar_prefetch=1,
            grid=(),
            in_specs=[pl.BlockSpec(memory_space=pltpu.VMEM)] + [anyspec()] * 5,
            out_specs=anyspec(),
            scratch_shapes=[
                pltpu.VMEM((total, D), bf16),
                pltpu.VMEM((3, total, HALF), bf16),
                pltpu.VMEM((3, D, HALF), bf16),
                pltpu.VMEM((16, HALF), bf16),
                pltpu.SemaphoreType.DMA((6,)),
            ],
        ),
        out_shape=shape((SLOTS, 3 * ROWS + 16, HALF)),
        compiler_params=pltpu.CompilerParams(vmem_limit_bytes=VMEM_CAP),
        cost_estimate=cost(total * D * HALF * 6, total * D * 5),
    )(info, small, t_own, t_got, dq, dk, dv)


def input_back_body(*refs):
    w = refs[0]
    dq, dk, dv = refs[1:4]
    out = refs[-1]
    total = None
    for j, part in enumerate((dq, dk, dv)):
        add = mxu(part[...], w[:, j * HALF : (j + 1) * HALF], NT)
        total = add if total is None else total + add
    for extra in refs[4:-1]:
        total = total + extra[...].astype(f32)
    out[...] = total.astype(bf16)


def input_back(w, dq, dk, dv, far, extras):
    half = dq.shape[0] // 2
    tile = 512
    base = half // tile if far else 0
    part = pl.BlockSpec((tile, HALF), lambda i: (base + i, 0))
    row = pl.BlockSpec((tile, D), lambda i: (i, 0))
    return pl.pallas_call(
        input_back_body,
        grid=(half // tile,),
        in_specs=[pl.BlockSpec((D, 3 * HALF), lambda i: (0, 0)), part, part, part] + [row] * len(extras),
        out_specs=row,
        out_shape=shape((half, D)),
        compiler_params=params(),
        cost_estimate=cost(half * D * HALF * 6, half * D * 8),
    )(w, dq, dk, dv, *extras)


def shift(n, k):
    return [(i, (i + k) % n) for i in range(n)]


class Plan:
    def __init__(self, seq, fsdp):
        rest = fsdp // 2
        dims = []
        while rest > 1:
            want = 4 if len(dims) % 2 == 0 and rest % 4 == 0 else 2
            dims.append(want)
            rest //= want
        self.dims = [seq] + dims + [2]
        self.names = ["s"] + ["r%d" % i for i in range(len(dims))] + ["c"]
        self.chips = seq * fsdp // 2
        self.direct = self.dims == [2, 4, 2, 2]
        self.stages = ([1] if dims else []) + [0] + list(range(2, len(dims) + 1))

    def at(self, a):
        return lax.axis_index(self.names[a])

    def chip_table(self, sign):
        if not self.direct:
            return jnp.arange(SLOTS, dtype=jnp.int32)
        spots = []
        for dx, dy in ((0, 0), (1, 0), (0, 1), (1, 1)):
            spots += [(dx, dy, z) for z in range(4)]
        dx, dy, dz = (jnp.asarray(v, jnp.int32) for v in zip(*spots))
        return ((self.at(0) + sign * dx) % 2) * 8 + ((self.at(1) + sign * dz) % 4) * 2 + (self.at(2) + sign * dy) % 2

    def slot_table(self, sign):
        table = self.chip_table(sign)
        hit = table[:, None] == jnp.arange(SLOTS, dtype=jnp.int32)[None, :]
        return jnp.sum(jnp.where(hit, jnp.arange(SLOTS, dtype=jnp.int32)[:, None], 0), axis=0)

    def places(self, sign):
        grid = np.indices(self.dims[:-1]).reshape(len(self.dims) - 1, -1)
        flat = jnp.zeros((self.chips,), jnp.int32)
        if sign < 0:
            for a in reversed(self.stages):
                n = self.dims[a]
                flat = flat * n + (self.at(a) - jnp.asarray(grid[a], jnp.int32)) % n
            return flat
        sizes = [self.dims[a] for a in reversed(self.stages)]
        offs = np.indices(sizes).reshape(len(sizes), -1)
        by_axis = {a: offs[j] for j, a in enumerate(reversed(self.stages))}
        for a in range(len(self.dims) - 1):
            n = self.dims[a]
            flat = flat * n + (self.at(a) + jnp.asarray(by_axis[a], jnp.int32)) % n
        return flat

    def send(self, x, a, k=1):
        return lax.ppermute(x, self.names[a], shift(self.dims[a], k))


def gather_chips(plan, unit):
    buf = unit[None]
    for a in plan.stages:
        n = plan.dims[a]
        if n > 1:
            buf = jnp.concatenate([buf] + [plan.send(buf, a, k) for k in range(1, n)], axis=0)
    return jnp.take(buf, plan.places(-1), axis=0, mode="clip")


def reduce_chips(plan, grads):
    buf = jnp.take(grads, plan.places(1), axis=0, mode="clip")
    for a in reversed(plan.stages):
        n = plan.dims[a]
        size = buf.shape[0] // n
        keep = buf[:size].astype(f32)
        for k in range(1, n):
            keep = keep + plan.send(buf[k * size : (k + 1) * size].astype(bf16), a, k).astype(f32)
        buf = keep if a == plan.stages[0] else keep.astype(bf16)
    return buf[0]


def regroup(buf, sizes, count):
    n, _, w = buf.shape
    parts = []
    at = 0
    for size in sizes:
        parts.append(buf[:, at : at + size].reshape(count, n * size // count, w))
        at += size
    return jnp.concatenate(parts, axis=1)


def gather_z(plan, unit):
    return jnp.concatenate([unit[None]] + [plan.send(unit, 1, k)[None] for k in range(1, 4)], axis=0)


def swap_pair(x):
    return lax.ppermute(x, "c", [(0, 1), (1, 0)])


def relocate(x):
    return lax.ppermute(x, ("s", "c"), [(0, 0), (1, 2), (2, 1), (3, 3)])


def half_of(x, at):
    return lax.dynamic_slice_in_dim(x, at * HALF, HALF, axis=x.ndim - 1)


def chip_units(me, mine, got, sizes):
    low = jnp.where(me == 0, mine, got)
    high = jnp.where(me == 0, got, mine)
    parts = []
    at = 0
    for size in sizes:
        parts += [low[at : at + size], high[at : at + size]]
        at += size
    return jnp.concatenate(parts, axis=0)


def own_rows(me, total, sizes):
    first, second = [], []
    at = 0
    for size in sizes:
        first.append(total[at : at + size])
        second.append(total[at + size : at + 2 * size])
        at += 2 * size
    first = jnp.concatenate(first, axis=0)
    second = jnp.concatenate(second, axis=0)
    return jnp.where(me == 0, first, second), jnp.where(me == 0, second, first)


def local(plan, tokens, lengths, block_order, qkv_weight, query_bias, value_bias, out_weight, out_bias,
          norm1_gain, norm1_shift, in_weight, in_bias, down_weight, down_bias, norm2_gain, norm2_shift, cotangent):
    half = tokens.shape[1]
    me = plan.at(len(plan.dims) - 1)
    rows_dev = qkv_weight.shape[0]
    ff_dev = down_weight.shape[0]
    ff_cols = in_weight.shape[1] // D
    me32 = me.astype(jnp.int32)
    pull = jnp.concatenate([me32[None], plan.chip_table(-1)])
    push = jnp.concatenate([me32[None], plan.slot_table(1)])

    sizes1 = [rows_dev] * 3
    sizes2 = [rows_dev] * (1 + ff_cols) + [ff_dev]
    first = jnp.concatenate([qkv_weight[:, j * D : (j + 1) * D] for j in range(3)], axis=0)
    second = jnp.concatenate([out_weight] + [in_weight[:, j * D : (j + 1) * D] for j in range(ff_cols)] + [down_weight], axis=0)
    smalls = (query_bias, value_bias, out_bias, norm1_gain, norm1_shift, in_bias, down_bias, norm2_gain, norm2_shift)
    line = jnp.concatenate(smalls)
    both = jnp.concatenate([first, second], axis=0)
    got = swap_pair(half_of(both, 1 - me))
    mine = half_of(both, me)
    cut = 3 * rows_dev
    unit1 = chip_units(me, mine[:cut], got[:cut], sizes1)
    unit2 = chip_units(me, mine[cut:], got[cut:], sizes2)
    line_got = swap_pair(line)
    line_unit = jnp.stack([jnp.where(me == 0, line, line_got), jnp.where(me == 0, line_got, line)])

    tok = relocate(tokens[0])
    if plan.direct:
        z1 = gather_z(plan, unit1)
        x1, y1 = plan.send(z1, 0), plan.send(z1, 2)
        pieces1 = [z1, x1, y1, plan.send(y1[0:2], 0), plan.send(x1[2:4], 2)]
        z2 = gather_z(plan, tie(unit2, z1))
    else:
        pieces1 = [regroup(gather_chips(plan, unit1), [2 * r for r in sizes1], SLOTS)]
        pieces2 = [regroup(gather_chips(plan, unit2), [2 * r for r in sizes2], SLOTS)]
        far2 = [swap_pair(p) for p in pieces2]
    lines = gather_chips(plan, line_unit).reshape(2 * plan.chips, line.shape[0])
    vectors = []
    at = 0
    for piece in smalls:
        size = piece.shape[0]
        vectors.append(lines[:, at : at + size].reshape(2 * plan.chips * size).astype(f32))
        at += size
    bias_q, bias_v, bias_o, gain1, shift1, bias_in, bias_d, gain2, shift2 = vectors
    bias_qkv = jnp.concatenate([half_of(bias_q, me), jnp.zeros((HALF,), f32), half_of(bias_v, me)])[None]
    zero = jnp.zeros((D,), f32)
    vecs = jnp.stack([bias_o, gain1, shift1, bias_d, gain2, shift2, zero, zero])

    ends = jnp.cumsum(lengths[0])
    unit_rows = 2 * half // UNITS
    seg_packed = jnp.sum((jnp.arange(UNITS)[:, None] * unit_rows >= ends[None, :]).astype(jnp.int32), axis=1)
    hit = block_order[0][:, None] == jnp.arange(UNITS)[None, :]
    seg_here = jnp.sum(jnp.where(hit, seg_packed[:, None], 0), axis=0)
    segs = jnp.where(plan.at(0) == me, seg_here, swap_pair(seg_here))
    segs = jnp.where(me == 0, segs, jnp.roll(segs, UNITS // 2))

    tok_got = swap_pair(tok)
    qkv, w_qkv = project(pull, tok, tok_got, bias_qkv, pieces1)
    back = relocate(tie(cotangent[0], pieces1[-1]))
    if plan.direct:
        qkv = tie(qkv, z2)
        x2, y2 = plan.send(z2, 0), plan.send(z2, 2)
        z2_far = swap_pair(z2)
    att = attention(segs, qkv, 0, 2, None)
    if plan.direct:
        y2_cut, x2_cut = lax.optimization_barrier((y2[0:2], x2[2:4], att[0]))[:2]
        d2a, d2b = plan.send(y2_cut, 0), plan.send(x2_cut, 2)
        x2_far, y2_far = swap_pair(x2), swap_pair(y2)
        att = lax.optimization_barrier(tuple(att) + (y2_cut, x2_cut))[:3]
    o_own, o_far, lse = attention(segs, qkv, 2, PAIRS - 2, att)
    o_got = swap_pair(o_far)
    if plan.direct:
        pieces2 = [z2, x2, y2, d2a, d2b]
        far2 = [z2_far, x2_far, y2_far, swap_pair(d2a), swap_pair(d2b)]
    (out_rows, act, ig, low, branch, attn_grad, resid1, d_own, d_far, sums) = middle(
        pull, tok, o_own, o_got, back, vecs, bias_in[None], pieces2, far2)
    d_got = swap_pair(d_far)
    sum_got = swap_pair(half_of(sums, 1 - me))
    small = half_of(sums, me) + sum_got
    keep, give = weight_grads(push, act, ig, low, branch, o_own, o_got, attn_grad)
    back_args = (o_own, o_far, d_own, d_got, lse)
    if plan.direct:
        got_g = swap_pair(give)
        g0 = attention_back(segs, tie(qkv, give), *back_args, 0, 1, None)
        output = relocate(tie(out_rows, give))

        def both_sums(lo, hi):
            return keep[lo:hi].astype(f32) + got_g[lo:hi].astype(f32)

        step1 = both_sums(12, 16).astype(bf16)
        sx, sy = lax.optimization_barrier((step1[:2], step1[2:], g0[0]))[:2]
        rx, ry = plan.send(sx, 0), plan.send(sy, 2)
        g0 = lax.optimization_barrier(tuple(g0) + (sx, sy))[:3]
        g1 = attention_back(segs, qkv, *back_args, 1, 1, g0)
        rx, ry = lax.optimization_barrier((rx, ry, g1[0]))[:2]
        send_x = jnp.concatenate([both_sums(4, 6), both_sums(6, 8) + ry.astype(f32)], axis=0).astype(bf16)
        send_y = jnp.concatenate([both_sums(8, 10) + rx.astype(f32), both_sums(10, 12)], axis=0).astype(bf16)
        px, py = plan.send(send_x, 0), plan.send(send_y, 2)
        g1 = lax.optimization_barrier(tuple(g1) + (send_x, send_y))[:3]
        dq, dk, dv = attention_back(segs, qkv, *back_args, 2, PAIRS - 2, g1)
        px, py = lax.optimization_barrier((px, py, dq))[:2]
        z_sum = both_sums(0, 4) + px.astype(f32) + py.astype(f32)
        z_low = z_sum[1:].astype(bf16)
        ffn = z_sum[0]
        for k in range(1, 4):
            ffn = ffn + plan.send(z_low[k - 1], 1, k).astype(f32)
        dq = tie(dq, z_low)
    else:
        output = relocate(out_rows)
        dq, dk, dv = attention_back(segs, qkv, *back_args, 0, PAIRS, None)
        summed = (keep.astype(f32) + swap_pair(give).astype(f32)).astype(bf16)
        scale = plan.chips // SLOTS
        units = regroup_back(summed, [ROWS] * (1 + ff_cols) + [ROWS * ff_cols], scale)
        ffn = reduce_chips(plan, units)
    tail = qkv_grads(push, small, tok, tok_got, dq, dk, dv)
    if plan.direct:
        rx, ry = plan.send(tail[12:14], 0), plan.send(tail[14:16], 2)
        far_back = swap_pair(input_back(w_qkv, dq, dk, dv, True, ()))
        send_x = jnp.concatenate([tail[4:6], (tail[6:8].astype(f32) + ry.astype(f32)).astype(bf16)], axis=0)
        send_y = jnp.concatenate([(tail[8:10].astype(f32) + rx.astype(f32)).astype(bf16), tail[10:12]], axis=0)
        px, py = plan.send(send_x, 0), plan.send(send_y, 2)
        packed = input_back(w_qkv, dq, dk, dv, False, (resid1, far_back))
        input_grad = relocate(packed)
        z_sum = tail[0:4].astype(f32) + px.astype(f32) + py.astype(f32)
        z_low = z_sum[1:].astype(bf16)
        qkv_sum = z_sum[0]
        for k in range(1, 4):
            qkv_sum = qkv_sum + plan.send(z_low[k - 1], 1, k).astype(f32)
    else:
        far_back = swap_pair(input_back(w_qkv, dq, dk, dv, True, ()))
        input_grad = relocate(input_back(w_qkv, dq, dk, dv, False, (resid1, far_back)))
        units = regroup_back(tail[:, : 3 * ROWS], [ROWS] * 3, scale)
        extra = jnp.broadcast_to(tail[0:1, 3 * ROWS :], (plan.chips, 16, HALF))
        qkv_sum = reduce_chips(plan, jnp.concatenate([units, extra], axis=1))

    small_sum = qkv_sum[6 * rows_dev :]
    sizes = sizes1 + sizes2
    total = jnp.concatenate([qkv_sum[: 6 * rows_dev], ffn], axis=0)
    mine, other = own_rows(me, total, sizes)
    got = swap_pair(jnp.concatenate([other, small_sum], axis=0))
    count = mine.shape[0]
    mine = jnp.concatenate([mine, small_sum], axis=0)
    full = jnp.concatenate([jnp.where(me == 0, mine, got), jnp.where(me == 0, got, mine)], axis=1)
    take = lambda at, size: full[at : at + size]
    out_qkv = jnp.concatenate([take(j * rows_dev, rows_dev) for j in range(3)], axis=1)
    out_out = take(3 * rows_dev, rows_dev)
    out_in = jnp.concatenate([take((4 + j) * rows_dev, rows_dev) for j in range(ff_cols)], axis=1)
    out_down = take((4 + ff_cols) * rows_dev, ff_dev)
    small_full = full[count:]
    device = plan.at(0)
    for a in range(1, len(plan.dims)):
        device = device * plan.dims[a] + plan.at(a)
    order = (14, 15, 0, 1, 2, 3, 3 + ff_cols, 4 + ff_cols, 5 + ff_cols)
    outs = []
    for piece, row in zip(smalls, order):
        size = piece.shape[0]
        span = small_full[row : row + size * 2 * plan.chips // D].reshape(-1)
        outs.append(lax.dynamic_slice_in_dim(span, device * size, size))
    s = outs
    return (output[None], input_grad[None], out_qkv, s[0], s[1], out_out, s[2], s[3], s[4], out_in, s[5], out_down, s[6], s[7], s[8])


def regroup_back(buf, sizes, scale):
    n, _, w = buf.shape
    parts = []
    at = 0
    for size in sizes:
        parts.append(buf[:, at : at + size].reshape(n * scale, size // scale, w))
        at += size
    return jnp.concatenate(parts, axis=1)


def solution(mesh):
    plan = Plan(mesh.shape["seq"], mesh.shape["fsdp"])
    inner_mesh = Mesh(mesh.devices.reshape(plan.dims), tuple(plan.names))
    groups = tuple(plan.names[1:])
    every = tuple(plan.names)
    rows = P(groups, "s", None)
    table = P(groups, None)
    mat = P(every, None)
    vec = P(every)
    placed = (rows, table, table, mat, vec, vec, mat, vec, vec, vec, mat, vec, mat, vec, vec, vec, rows)
    outs = (rows, rows, mat, vec, vec, mat, vec, vec, vec, mat, vec, mat, vec, vec, vec)

    def run(*args):
        return local(plan, *args)

    return jax.shard_map(run, mesh=inner_mesh, in_specs=placed, out_specs=outs, check_vma=False)
```

time: 671 us -> 505 us (0.75); the launches traced: 657 us -> 498 us
  local copies, waits for them, and re-layouts: 135 us -> 29 us
  Pallas kernels: 120 us -> 223 us
  matrix products: 95.7 us -> 0 us
  waiting for transfers between devices: 198 us -> 108 us
  starting transfers between devices: 54.5 us -> 111 us
  other arithmetic: 51.8 us -> 25.1 us
    ppermute x24 -> x33, waiting for transfers between devices: 197 us -> 86.2 us  [send(): return lax.ppermute(x, self.names[a], shift(self.dims[a], k))]
    pallas_call x2 -> x11, Pallas kernels: 120 us -> 223 us  [the longest x3 85.4 us: attention_back(): pl.pallas_call(attend_back_body, grid_spec=pltpu.PrefetchScalarGridSpec(n...]
    dot_general x18 -> x0, matrix products: 95.7 us -> none  [dot(): return lax.dot_general(a, b, dims, preferred_element_type=f32)]
    ppermute x5 -> x15, starting transfers between devices: 0.87 us -> 50.5 us  [swap_pair(): return lax.ppermute(x, 'c', [(0, 1), (1, 0)])]
    unnamed x137 -> x60, local copies, waits for them, and re-layouts: 41.5 us -> 11.2 us
    gather x4 -> x1, local copies, waits for them, and re-layouts: 29.9 us -> 0.61 us  [gather_chips(): return jnp.take(buf, plan.places(-1), axis=0, mode='clip')]
    concatenate x22 -> x7, local copies, waits for them, and re-layouts: 35 us -> 7.1 us  [the longest x1 6.1 us: local(): line = jnp.concatenate(smalls)]
    slice x35 -> x10, local copies, waits for them, and re-layouts: 28 us -> 5.77 us  [the longest x2 1.92 us: local(): pieces1 = [z1, x1, y1, plan.send(y1[0:2], 0), plan.send(x1[2:4], 2)]]
  transfers between devices with their start and end apart: 33 -> 52, of which waited for: 12 -> 15; matrix products, arithmetic and copies ran while one was open for 33% -> 7% of each run, Pallas kernels for 6% -> 25%
where the time goes in v2:
time: 505 us; the launch traced here: 498 us
  Pallas kernels  223 us (44%)
  starting transfers between devices  111 us (22%)
  waiting for transfers between devices  108 us (21%)
  local copies, waits for them, and re-layouts  29 us (6%)
  other arithmetic  25.1 us (5%)
    ppermute x33, waiting for transfers between devices, send(): return lax.ppermute(x, self.names[a], shift(self.dims[a], k))  86.2 us
    pallas_call x3, Pallas kernels, attention_back(): pl.pallas_call(attend_back_body, grid_spec=pltpu.PrefetchScalarGridSpec(n...  85.4 us
    ppermute x15, starting transfers between devices, swap_pair(): return lax.ppermute(x, 'c', [(0, 1), (1, 0)])  50.5 us
    pallas_call x2, Pallas kernels, attention(): pl.pallas_call(attend_body, grid_spec=pltpu.PrefetchScalarGridSpec(num_sc...  42.9 us
    ppermute x33, starting transfers between devices, send(): return lax.ppermute(x, self.names[a], shift(self.dims[a], k))  41.6 us
    pallas_call x1, Pallas kernels, middle(): pl.pallas_call(mid_body, grid_spec=pltpu.PrefetchScalarGridSpec(num_scala...  39.4 us
    pallas_call x1, Pallas kernels, weight_grads(): pl.pallas_call(wgrad_body, grid_spec=pltpu.PrefetchScalarGridSpec(num_sca...  21.2 us
    ppermute x4, starting transfers between devices, relocate(): return lax.ppermute(x, ('s', 'c'), [(0, 0), (1, 2), (2, 1), (3, 3)])  19.1 us
  transfers between devices with their start and end apart: 52, of which 15 were waited for; matrix products, arithmetic and copies ran while one was open for 7% of the time, Pallas kernels for 25%

profile of v2, /device:TPU:1, one launch (start us, length us, event | category | flops | bytes accessed | tf_op | source)
XLA Modules:
  0.0 498.1 jit_solution(1794121081785270098)
XLA Ops:
  0.6 6.1 %concatenate.79 = bf16[288]{0:T(512)(128)(2,1)S(1)} concatenate(bf16[24]{0:T(256)(128)(2,1)} %param.30, bf16[24]{0:T(256)(128)(2,1)} %param.31, bf16[24]{0:T(256)(128)(2,1)} %param.33, bf16[24]{0:T(256)(128)(2,1)} %param.34, bf16[24]{0:T(256)(128)(2,1)} %param.35, bf16[96]{0:T(256)(128)(2,1)} %param.37, bf16[24]{0:T(256)(128)(2,1)} %param.39, bf16[24]{0:T(256)(128)(2,1)} %param.40, ...), dimensions={0} | concatenate | bytes 1152 | tf_op jit(solution)/shard_map/concatenate | solution.py:735
  14.5 4.5 collective-permute-start
  22.3 3.4 collective-permute-start.6
  33.0 3.3 collective-permute-start.19
  37.3 21.5 %collective-permute-start.1 = (s32[16]{0:T(128)S(1)}, s32[16]{0:T(128)S(1)}, u32[]{:S(2)}, u32[]{:S(2)}) collective-permute-start(s32[16]{0:T(128)S(1)} %select_reduce_fusion.1), channel_id=1, source_target_pairs={{0,1},{1,0},{2,3},{3,2},{4,5},{5,4},{6,7},{7,6},{8,9},{9,8},{10,11... | collective-permute-start | bytes 200 | tf_op jit(solution)/shard_map/ppermute | solution.py:685
  59.9 10.7 %collective-permute-start.21 = (bf16[4,432,384]{2,1,0:T(8,128)(2,1)S(1)}, bf16[4,432,384]{2,1,0:T(8,128)(2,1)S(1)}, u32[]{:S(2)}, u32[]{:S(2)}) collective-permute-start(bf16[4,432,384]{2,1,0:T(8,128)(2,1)S(1)} %pad_maximum_fusion.refs_0_), channel_id=1, source_target_pairs={{0,16},{16,0},{1,17},{17,1},{2,18},{18,2},{3,19},{19,3},{4,20},{20... | collective-permute-start | bytes 3981320 | tf_op jit(solution)/shard_map/ppermute | solution.py:646
  73.5 26.2 %collective-permute-done.8 = bf16[8,2,288]{2,1,0:T(2,128)(2,1)S(1)} collective-permute-done((bf16[8,2,288]{2,1,0:T(2,128)(2,1)S(1)}, bf16[8,2,288]{2,1,0:T(2,128)(2,1)S(1)}, u32[]{:S(2)}, u32[]{:S(2)}) %collective-permute-start.8) | collective-permute-done | bytes 9248 | tf_op jit(solution)/shard_map/ppermute | solution.py:646
  101.0 8.2 %collective-permute-done.14.refs_2_ = bf16[4,144,384]{2,1,0:T(8,128)(2,1)} collective-permute-done((bf16[4,144,384]{2,1,0:T(8,128)(2,1)S(1)}, bf16[4,144,384]{2,1,0:T(8,128)(2,1)}, u32[]{:S(2)}, u32[]{:S(2)}) %collective-permute-start.14) | collective-permute-done | bytes 442400 | tf_op jit(solution)/shard_map/ppermute | solution.py:646
  116.5 4.9 collective-permute-start.26
  121.4 4.3 collective-permute-start.23
  125.8 9.2 %collective-permute-start.27 = (bf16[4,432,384]{2,1,0:T(8,128)(2,1)S(1)}, bf16[4,432,384]{2,1,0:T(8,128)(2,1)}, u32[]{:S(2)}, u32[]{:S(2)}) collective-permute-start(bf16[4,432,384]{2,1,0:T(8,128)(2,1)S(1)} %collective-permute-done.21.refs_1_), channel_id=1, source_target_pairs={{0,1},{1,0},{2,3},{3,2},{4,5},{5,4},{6,7},{7,6},{8,9},{9,8},{10,11... | collective-permute-start | bytes 3981320 | tf_op jit(solution)/shard_map/ppermute | solution.py:685
  136.3 11.0 %shard_map.361 = (bf16[2048,1152]{1,0:T(8,128)(2,1)}, bf16[768,1152]{1,0:T(8,128)(2,1)}) custom-call(s32[17]{0:T(128)} %pad_add_fusion.info, bf16[1024,768]{1,0:T(8,128)(2,1)} %collective-permute-done.t_own.tok, bf16[1024,768]{1,0:T(8,128)(2,1)} %collective-permute-done.2.t_got, f32[1,1152]{1,0:T(1,128)} %broadcast_in_dim.79.bias, ...), custom_call_target="tpu_custom_call" | custom-call | flops 3623878656 | bytes 9437184 | tf_op jit(solution)/shard_map/pallas_call | solution.py:278
  147.3 27.7 %shard_map.362 = (bf16[1024,384]{1,0:T(8,128)(2,1)}, bf16[1024,384]{1,0:T(8,128)(2,1)}, f32[2048,384]{1,0:T(8,128)}) custom-call(s32[16]{0:T(128)} %broadcast_select_fusion.9.segs_ref, bf16[2048,1152]{1,0:T(8,128)(2,1)} %get-tuple-element.92.q_in.k_in.v_in, bf16[2048,1152]{1,0:T(8,128)(2,1)} %get-tuple-element.92.q_in.k_in.v_in, ...), custom_call_target="tpu_custom_call" | custom-call | flops 17179869184 | bytes 4194304 | tf_op jit(solution)/shard_map/pallas_call | solution.py:143
  179.1 15.2 %shard_map.363 = (bf16[1024,384]{1,0:T(8,128)(2,1)}, bf16[1024,384]{1,0:T(8,128)(2,1)}, f32[2048,384]{1,0:T(8,128)}) custom-call(s32[16]{0:T(128)} %broadcast_select_fusion.9.segs_ref, bf16[2048,1152]{1,0:T(8,128)(2,1)} %get-tuple-element.92.q_in.k_in.v_in, ...), custom_call_target="tpu_custom_call", output_to_operand_aliasing={{0}: (4, {}), {1}: (5, {}), {2}: (6, {})} | custom-call | flops 8589934592 | bytes 4194304 | tf_op jit(solution)/shard_map/pallas_call | solution.py:143
  199.0 39.4 %shard_map.364 = (bf16[1024,768]{1,0:T(8,128)(2,1)}, bf16[1024,3072]{1,0:T(8,128)(2,1)}, bf16[1024,3072]{1,0:T(8,128)(2,1)}, bf16[1024,768]{1,0:T(8,128)(2,1)}, ...) custom-call(s32[17]{0:T(128)} %pad_add_fusion.info, ...), custom_call_target="tpu_custom_call" | custom-call | flops 21743271936 | bytes 31457280 | tf_op jit(solution)/shard_map/pallas_call | solution.py:407
  238.5 21.2 %shard_map.365 = (bf16[16,432,384]{2,1,0:T(8,128)(2,1)}, bf16[16,432,384]{2,1,0:T(8,128)(2,1)}) custom-call(s32[17]{0:T(128)} %pad_add_fusion.1.info, bf16[1024,3072]{1,0:T(8,128)(2,1)} %get-tuple-element.81.act, bf16[1024,3072]{1,0:T(8,128)(2,1)} %get-tuple-element.82.ig, bf16[1024,768]{1,0:T(8,128)(2,1)} %get-tuple-element.83.low, ...), custom_call_target="tpu_custom_call" | custom-call | flops 10871635968 | bytes 25165824 | tf_op jit(solution)/shard_map/pallas_call | solution.py:494
  260.7 9.2 %collective-permute-done.38 = f32[16,384]{1,0:T(8,128)S(1)} collective-permute-done((f32[16,384]{1,0:T(8,128)S(1)}, f32[16,384]{1,0:T(8,128)S(1)}, u32[]{:S(2)}, u32[]{:S(2)}) %collective-permute-start.38) | collective-permute-done | bytes 24608 | tf_op jit(solution)/shard_map/ppermute | solution.py:685
  271.4 28.9 %shard_map.366 = (bf16[2048,384]{1,0:T(8,128)(2,1)}, bf16[2048,384]{1,0:T(8,128)(2,1)}, bf16[2048,384]{1,0:T(8,128)(2,1)}) custom-call(s32[16]{0:T(128)} %broadcast_select_fusion.9.segs_ref, bf16[2048,1152]{1,0:T(8,128)(2,1)} %get-tuple-element.92.q_in.k_in.v_in, bf16[2048,1152]{1,0:T(8,128)(2,1)} %get-tuple-element.92.q_in.k_in.v_in, ...), custom_call_target="tpu_custom_call" | custom-call | flops 21474836480 | bytes 6291456 | tf_op jit(solution)/shard_map/pallas_call | solution.py:216
  304.2 28.1 %shard_map.367 = (bf16[2048,384]{1,0:T(8,128)(2,1)}, bf16[2048,384]{1,0:T(8,128)(2,1)}, bf16[2048,384]{1,0:T(8,128)(2,1)}) custom-call(s32[16]{0:T(128)} %broadcast_select_fusion.9.segs_ref, bf16[2048,1152]{1,0:T(8,128)(2,1)} %get-tuple-element.92.q_in.k_in.v_in, ...), custom_call_target="tpu_custom_call", output_to_operand_aliasing={{0}: (9, {}), {1}: (10, {}), {2}: (11, {})} | custom-call | flops 21474836480 | bytes 6291456 | tf_op jit(solution)/shard_map/pallas_call | solution.py:216
  337.8 28.4 %shard_map.368 = (bf16[2048,384]{1,0:T(8,128)(2,1)}, bf16[2048,384]{1,0:T(8,128)(2,1)}, bf16[2048,384]{1,0:T(8,128)(2,1)}) custom-call(s32[16]{0:T(128)} %broadcast_select_fusion.9.segs_ref, bf16[2048,1152]{1,0:T(8,128)(2,1)} %get-tuple-element.92.q_in.k_in.v_in, ...), custom_call_target="tpu_custom_call", output_to_operand_aliasing={{0}: (9, {}), {1}: (10, {}), {2}: (11, {})} | custom-call | flops 21474836480 | bytes 6291456 | tf_op jit(solution)/shard_map/pallas_call | solution.py:216
  366.2 10.2 %shard_map.371 = bf16[16,160,384]{2,1,0:T(8,128)(2,1)} custom-call(s32[17]{0:T(128)} %pad_add_fusion.1.info, f32[16,384]{1,0:T(8,128)} %dynamic-slice_add_fusion.small, bf16[1024,768]{1,0:T(8,128)(2,1)} %collective-permute-done.t_own.tok, bf16[1024,768]{1,0:T(8,128)(2,1)} %collective-permute-done.2.t_got, bf16[2048,384]{1,0:T(8,128)(2,1)} %get-tuple-element.110.refs_1_.dq, ...), custom_call_target="tpu_custom_call" | custom-call | flops 3623878656 | bytes 7864320 | tf_op jit(solution)/shard_map/pallas_call | solution.py:543
  379.7 4.8 collective-permute-done.41
  389.0 7.9 %collective-permute-done.42 = bf16[4,160,384]{2,1,0:T(8,128)(2,1)S(1)} collective-permute-done((bf16[4,160,384]{2,1,0:T(8,128)(2,1)S(1)}, bf16[4,160,384]{2,1,0:T(8,128)(2,1)S(1)}, u32[]{:S(2)}, u32[]{:S(2)}) %collective-permute-start.42) | collective-permute-done | bytes 491552 | tf_op jit(solution)/shard_map/ppermute | solution.py:646
  398.1 3.5 collective-permute-start.45
  401.6 5.7 %shard_map.369 = bf16[1024,768]{1,0:T(8,128)(2,1)} custom-call(bf16[768,1152]{1,0:T(8,128)(2,1)} %get-tuple-element.88.refs_0_, bf16[2048,384]{1,0:T(8,128)(2,1)} %get-tuple-element.110.refs_1_.dq, bf16[2048,384]{1,0:T(8,128)(2,1)} %get-tuple-element.111.refs_2_.dk, bf16[2048,384]{1,0:T(8,128)(2,1)} %get-tuple-element.112.refs_3_.dv), custom_call_target="tpu_custom_call" | custom-call | flops 1811939328 | bytes 6291456 | tf_op jit(solution)/shard_map/pallas_call | solution.py:583
  407.3 8.4 %collective-permute-start.31 = (bf16[1024,768]{1,0:T(8,128)(2,1)}, bf16[1024,768]{1,0:T(8,128)(2,1)}, u32[]{:S(2)}, u32[]{:S(2)}) collective-permute-start(bf16[1024,768]{1,0:T(8,128)(2,1)} %get-tuple-element.87), channel_id=1, source_target_pairs={{0,0},{1,16},{16,1},{17,17},{2,2},{3,18},{18,3},{19,19},{4,4},{5,2... | collective-permute-start | bytes 4718600 | tf_op jit(solution)/shard_map/ppermute | solution.py:689
  415.7 11.4 %collective-permute-start.36 = (bf16[1024,768]{1,0:T(8,128)(2,1)}, bf16[1024,768]{1,0:T(8,128)(2,1)}, u32[]{:S(2)}, u32[]{:S(2)}) collective-permute-start(bf16[1024,768]{1,0:T(8,128)(2,1)} %shard_map.369), channel_id=1, source_target_pairs={{0,1},{1,0},{2,3},{3,2},{4,5},{5,4},{6,7},{7,6},{8,9},{9,8},{10,11... | collective-permute-start | bytes 4718600 | tf_op jit(solution)/shard_map/ppermute | solution.py:685
  435.3 6.0 %collective-permute-done.48 = bf16[432,384]{1,0:T(8,128)(2,1)S(1)} collective-permute-done((bf16[432,384]{1,0:T(8,128)(2,1)S(1)}, bf16[432,384]{1,0:T(8,128)(2,1)S(1)}, u32[]{:S(2)}, u32[]{:S(2)}) %collective-permute-start.48) | collective-permute-done | bytes 331808 | tf_op jit(solution)/shard_map/ppermute | solution.py:646
  441.2 7.8 %collective-permute-done.50 = bf16[432,384]{1,0:T(8,128)(2,1)S(1)} collective-permute-done((bf16[432,384]{1,0:T(8,128)(2,1)S(1)}, bf16[432,384]{1,0:T(8,128)(2,1)S(1)}, u32[]{:S(2)}, u32[]{:S(2)}) %collective-permute-start.50) | collective-permute-done | bytes 331808 | tf_op jit(solution)/shard_map/ppermute | solution.py:646
  449.1 14.9 %collective-permute-done.49 = bf16[432,384]{1,0:T(8,128)(2,1)S(1)} collective-permute-done((bf16[432,384]{1,0:T(8,128)(2,1)S(1)}, bf16[432,384]{1,0:T(8,128)(2,1)S(1)}, u32[]{:S(2)}, u32[]{:S(2)}) %collective-permute-start.49) | collective-permute-done | bytes 331808 | tf_op jit(solution)/shard_map/ppermute | solution.py:646
  464.9 7.0 %shard_map.370 = bf16[1024,768]{1,0:T(8,128)(2,1)} custom-call(bf16[768,1152]{1,0:T(8,128)(2,1)} %get-tuple-element.88.refs_0_, bf16[2048,384]{1,0:T(8,128)(2,1)} %get-tuple-element.110.refs_1_.dq, bf16[2048,384]{1,0:T(8,128)(2,1)} %get-tuple-element.111.refs_2_.dk, bf16[2048,384]{1,0:T(8,128)(2,1)} %get-tuple-element.112.refs_3_.dv, ...), custom_call_target="tpu_custom_call" | custom-call | flops 1811939328 | bytes 6291456 | tf_op jit(solution)/shard_map/pallas_call | solution.py:583
  482.1 11.7 %collective-permute-done.37 = bf16[1024,768]{1,0:T(8,128)(2,1)S(1)} collective-permute-done((bf16[1024,768]{1,0:T(8,128)(2,1)}, bf16[1024,768]{1,0:T(8,128)(2,1)S(1)}, u32[]{:S(2)}, u32[]{:S(2)}) %collective-permute-start.37) | collective-permute-done | bytes 1572896 | tf_op jit(solution)/shard_map/ppermute | solution.py:689
  (236 shorter events, 85.4 us)
Async XLA Ops:
  6.7 15.5 %collective-permute-start.3 = (bf16[288]{0:T(512)(128)(2,1)S(1)}, bf16[288]{0:T(512)(128)(2,1)S(1)}, u32[]{:S(2)}, u32[]{:S(2)}) collective-permute-start(bf16[288]{0:T(512)(128)(2,1)S(1)} %concatenate.79), channel_id=1, source_target_pairs={{0,1},{1,0},{2,3},{3,2},{4,5},{5,4},{6,7},{7,6},{8,9},{9,8},{10,11... | collective-permute-start | bytes 1736 | tf_op jit(solution)/shard_map/ppermute | solution.py:685
  14.5 44.3 %collective-permute-start = (bf16[1024,768]{1,0:T(8,128)(2,1)}, bf16[1024,768]{1,0:T(8,128)(2,1)}, u32[]{:S(2)}, u32[]{:S(2)}) collective-permute-start(bf16[1024,768]{1,0:T(8,128)(2,1)} %bitcast.72), channel_id=1, source_target_pairs={{0,0},{1,16},{16,1},{17,17},{2,2},{3,18},{18,3},{19,19},{4,4},{5,2... | collective-permute-start | bytes 4718600 | tf_op jit(solution)/shard_map/ppermute | solution.py:689
  22.3 14.1 %collective-permute-start.6 = (bf16[1,2,288]{2,1,0:T(2,128)(2,1)S(1)}, bf16[1,2,288]{2,1,0:T(2,128)(2,1)S(1)}, u32[]{:S(2)}, u32[]{:S(2)}) collective-permute-start(bf16[1,2,288]{2,1,0:T(2,128)(2,1)S(1)} %get-tuple-element.122), channel_id=1, source_target_pairs={{0,12},{4,0},{8,4},{12,8},{1,13},{5,1},{9,5},{13,9},{2,14},{6,2},{... | collective-permute-start | bytes 3464 | tf_op jit(solution)/shard_map/ppermute | solution.py:646
  33.0 25.9 %collective-permute-start.19 = (bf16[432,384]{1,0:T(8,128)(2,1)S(1)}, bf16[432,384]{1,0:T(8,128)(2,1)S(1)}, u32[]{:S(2)}, u32[]{:S(2)}) collective-permute-start(bf16[432,384]{1,0:T(8,128)(2,1)S(1)} %constant_dynamic-update-slice_fusion.26), channel_id=1, source_target_pairs={{0,12},{4,0},{8,4},{12,8},{1,13},{5,1},{9,5},{13,9},{2,14},{6,2},{... | collective-permute-start | bytes 995336 | tf_op jit(solution)/shard_map/ppermute | solution.py:646
  36.3 23.4 %collective-permute-start.18 = (bf16[432,384]{1,0:T(8,128)(2,1)S(1)}, bf16[432,384]{1,0:T(8,128)(2,1)S(1)}, u32[]{:S(2)}, u32[]{:S(2)}) collective-permute-start(bf16[432,384]{1,0:T(8,128)(2,1)S(1)} %constant_dynamic-update-slice_fusion.26), channel_id=1, source_target_pairs={{0,8},{4,12},{8,0},{12,4},{1,9},{5,13},{9,1},{13,5},{2,10},{6,14},... | collective-permute-start | bytes 995336 | tf_op jit(solution)/shard_map/ppermute | solution.py:646
  37.3 22.4 %collective-permute-start.17 = (bf16[432,384]{1,0:T(8,128)(2,1)S(1)}, bf16[432,384]{1,0:T(8,128)(2,1)S(1)}, u32[]{:S(2)}, u32[]{:S(2)}) collective-permute-start(bf16[432,384]{1,0:T(8,128)(2,1)S(1)} %constant_dynamic-update-slice_fusion.26), channel_id=1, source_target_pairs={{0,4},{4,8},{8,12},{12,0},{1,5},{5,9},{9,13},{13,1},{2,6},{6,10},{... | collective-permute-start | bytes 995336 | tf_op jit(solution)/shard_map/ppermute | solution.py:646
  37.3 35.0 %collective-permute-start.1 = (s32[16]{0:T(128)S(1)}, s32[16]{0:T(128)S(1)}, u32[]{:S(2)}, u32[]{:S(2)}) collective-permute-start(s32[16]{0:T(128)S(1)} %select_reduce_fusion.1), channel_id=1, source_target_pairs={{0,1},{1,0},{2,3},{3,2},{4,5},{5,4},{6,7},{7,6},{8,9},{9,8},{10,11... | collective-permute-start | bytes 200 | tf_op jit(solution)/shard_map/ppermute | solution.py:685
  58.8 77.5 %collective-permute-start.2 = (bf16[1024,768]{1,0:T(8,128)(2,1)}, bf16[1024,768]{1,0:T(8,128)(2,1)}, u32[]{:S(2)}, u32[]{:S(2)}) collective-permute-start(bf16[1024,768]{1,0:T(8,128)(2,1)} %collective-permute-done.t_own.tok), channel_id=1, source_target_pairs={{0,1},{1,0},{2,3},{3,2},{4,5},{5,4},{6,7},{7,6},{8,9},{9,8},{10,11... | collective-permute-start | bytes 4718600 | tf_op jit(solution)/shard_map/ppermute | solution.py:685
  58.9 13.0 %collective-permute-start.7 = (bf16[4,2,288]{2,1,0:T(2,128)(2,1)S(1)}, bf16[4,2,288]{2,1,0:T(2,128)(2,1)S(1)}, u32[]{:S(2)}, u32[]{:S(2)}) collective-permute-start(bf16[4,2,288]{2,1,0:T(2,128)(2,1)S(1)} %pad_maximum_fusion.11), channel_id=1, source_target_pairs={{0,16},{16,0},{1,17},{17,1},{2,18},{18,2},{3,19},{19,3},{4,20},{20... | collective-permute-start | bytes 13832 | tf_op jit(solution)/shard_map/ppermute | solution.py:646
  59.9 61.4 %collective-permute-start.21 = (bf16[4,432,384]{2,1,0:T(8,128)(2,1)S(1)}, bf16[4,432,384]{2,1,0:T(8,128)(2,1)S(1)}, u32[]{:S(2)}, u32[]{:S(2)}) collective-permute-start(bf16[4,432,384]{2,1,0:T(8,128)(2,1)S(1)} %pad_maximum_fusion.refs_0_), channel_id=1, source_target_pairs={{0,16},{16,0},{1,17},{17,1},{2,18},{18,2},{3,19},{19,3},{4,20},{20... | collective-permute-start | bytes 3981320 | tf_op jit(solution)/shard_map/ppermute | solution.py:646
  70.7 55.1 %collective-permute-start.20 = (bf16[4,432,384]{2,1,0:T(8,128)(2,1)S(1)}, bf16[4,432,384]{2,1,0:T(8,128)(2,1)}, u32[]{:S(2)}, u32[]{:S(2)}) collective-permute-start(bf16[4,432,384]{2,1,0:T(8,128)(2,1)S(1)} %pad_maximum_fusion.refs_0_), channel_id=1, source_target_pairs={{0,2},{2,0},{1,3},{3,1},{4,6},{6,4},{5,7},{7,5},{8,10},{10,8},{9,1... | collective-permute-start | bytes 3981320 | tf_op jit(solution)/shard_map/ppermute | solution.py:646
  72.0 27.8 %collective-permute-start.8 = (bf16[8,2,288]{2,1,0:T(2,128)(2,1)S(1)}, bf16[8,2,288]{2,1,0:T(2,128)(2,1)S(1)}, u32[]{:S(2)}, u32[]{:S(2)}) collective-permute-start(bf16[8,2,288]{2,1,0:T(2,128)(2,1)S(1)} %get-tuple-element.197), channel_id=1, source_target_pairs={{0,2},{2,0},{1,3},{3,1},{4,6},{6,4},{5,7},{7,5},{8,10},{10,8},{9,1... | collective-permute-start | bytes 27656 | tf_op jit(solution)/shard_map/ppermute | solution.py:646
  72.3 36.9 %collective-permute-start.14 = (bf16[4,144,384]{2,1,0:T(8,128)(2,1)S(1)}, bf16[4,144,384]{2,1,0:T(8,128)(2,1)}, u32[]{:S(2)}, u32[]{:S(2)}) collective-permute-start(bf16[4,144,384]{2,1,0:T(8,128)(2,1)S(1)} %pad_maximum_fusion.7.refs_0_), channel_id=1, source_target_pairs={{0,2},{2,0},{1,3},{3,1},{4,6},{6,4},{5,7},{7,5},{8,10},{10,8},{9,1... | collective-permute-start | bytes 1327112 | tf_op jit(solution)/shard_map/ppermute | solution.py:646
  110.2 26.0 %collective-permute-start.15 = (bf16[2,144,384]{2,1,0:T(8,128)(2,1)S(1)}, bf16[2,144,384]{2,1,0:T(8,128)(2,1)}, u32[]{:S(2)}, u32[]{:S(2)}) collective-permute-start(bf16[2,144,384]{2,1,0:T(8,128)(2,1)S(1)} %slice.480), channel_id=1, source_target_pairs={{0,16},{16,0},{1,17},{17,1},{2,18},{18,2},{3,19},{19,3},{4,20},{20... | collective-permute-start | bytes 663560 | tf_op jit(solution)/shard_map/ppermute | solution.py:646
  116.5 61.4 %collective-permute-start.26 = (bf16[4,432,384]{2,1,0:T(8,128)(2,1)S(1)}, bf16[4,432,384]{2,1,0:T(8,128)(2,1)S(1)}, u32[]{:S(2)}, u32[]{:S(2)}) collective-permute-start(bf16[4,432,384]{2,1,0:T(8,128)(2,1)S(1)} %pad_maximum_fusion.refs_0_), channel_id=1, source_target_pairs={{0,1},{1,0},{2,3},{3,2},{4,5},{5,4},{6,7},{7,6},{8,9},{9,8},{10,11... | collective-permute-start | bytes 3981320 | tf_op jit(solution)/shard_map/ppermute | solution.py:685
  121.4 72.8 %collective-permute-start.23 = (bf16[1024,768]{1,0:T(8,128)(2,1)}, bf16[1024,768]{1,0:T(8,128)(2,1)}, u32[]{:S(2)}, u32[]{:S(2)}) collective-permute-start(bf16[1024,768]{1,0:T(8,128)(2,1)} %bitcast.73), channel_id=1, source_target_pairs={{0,0},{1,16},{16,1},{17,17},{2,2},{3,18},{18,3},{19,19},{4,4},{5,2... | collective-permute-start | bytes 4718600 | tf_op jit(solution)/shard_map/ppermute | solution.py:689
  125.8 72.2 %collective-permute-start.27 = (bf16[4,432,384]{2,1,0:T(8,128)(2,1)S(1)}, bf16[4,432,384]{2,1,0:T(8,128)(2,1)}, u32[]{:S(2)}, u32[]{:S(2)}) collective-permute-start(bf16[4,432,384]{2,1,0:T(8,128)(2,1)S(1)} %collective-permute-done.21.refs_1_), channel_id=1, source_target_pairs={{0,1},{1,0},{2,3},{3,2},{4,5},{5,4},{6,7},{7,6},{8,9},{9,8},{10,11... | collective-permute-start | bytes 3981320 | tf_op jit(solution)/shard_map/ppermute | solution.py:685
  136.2 61.8 %collective-permute-start.28 = (bf16[4,432,384]{2,1,0:T(8,128)(2,1)}, bf16[4,432,384]{2,1,0:T(8,128)(2,1)}, u32[]{:S(2)}, u32[]{:S(2)}) collective-permute-start(bf16[4,432,384]{2,1,0:T(8,128)(2,1)} %collective-permute-done.20.refs_2_), channel_id=1, source_target_pairs={{0,1},{1,0},{2,3},{3,2},{4,5},{5,4},{6,7},{7,6},{8,9},{9,8},{10,11... | collective-permute-start | bytes 3981320 | tf_op jit(solution)/shard_map/ppermute | solution.py:685
  175.1 19.8 %collective-permute-start.24 = (bf16[2,432,384]{2,1,0:T(8,128)(2,1)S(1)}, bf16[2,432,384]{2,1,0:T(8,128)(2,1)}, u32[]{:S(2)}, u32[]{:S(2)}) collective-permute-start(bf16[2,432,384]{2,1,0:T(8,128)(2,1)S(1)} %slice.495), channel_id=1, source_target_pairs={{0,16},{16,0},{1,17},{17,1},{2,18},{18,2},{3,19},{19,3},{4,20},{20... | collective-permute-start | bytes 1990664 | tf_op jit(solution)/shard_map/ppermute | solution.py:646
  177.8 17.1 %collective-permute-start.25 = (bf16[2,432,384]{2,1,0:T(8,128)(2,1)S(1)}, bf16[2,432,384]{2,1,0:T(8,128)(2,1)S(1)}, u32[]{:S(2)}, u32[]{:S(2)}) collective-permute-start(bf16[2,432,384]{2,1,0:T(8,128)(2,1)S(1)} %slice.496), channel_id=1, source_target_pairs={{0,2},{2,0},{1,3},{3,1},{4,6},{6,4},{5,7},{7,5},{8,10},{10,8},{9,1... | collective-permute-start | bytes 1990664 | tf_op jit(solution)/shard_map/ppermute | solution.py:646
  259.7 40.6 %collective-permute-start.33 = (bf16[16,432,384]{2,1,0:T(8,128)(2,1)}, bf16[16,432,384]{2,1,0:T(8,128)(2,1)}, u32[]{:S(2)}, u32[]{:S(2)}) collective-permute-start(bf16[16,432,384]{2,1,0:T(8,128)(2,1)} %get-tuple-element.86), channel_id=1, source_target_pairs={{0,1},{1,0},{2,3},{3,2},{4,5},{5,4},{6,7},{7,6},{8,9},{9,8},{10,11... | collective-permute-start | bytes 15925256 | tf_op jit(solution)/shard_map/ppermute | solution.py:685
  303.0 29.3 %collective-permute-start.34 = (bf16[2,432,384]{2,1,0:T(8,128)(2,1)}, bf16[2,432,384]{2,1,0:T(8,128)(2,1)}, u32[]{:S(2)}, u32[]{:S(2)}) collective-permute-start(bf16[2,432,384]{2,1,0:T(8,128)(2,1)} %get-tuple-element.97), channel_id=1, source_target_pairs={{0,16},{16,0},{1,17},{17,1},{2,18},{18,2},{3,19},{19,3},{4,20},{20... | collective-permute-start | bytes 1990664 | tf_op jit(solution)/shard_map/ppermute | solution.py:646
  303.0 29.3 %collective-permute-start.35 = (bf16[2,432,384]{2,1,0:T(8,128)(2,1)S(1)}, bf16[2,432,384]{2,1,0:T(8,128)(2,1)}, u32[]{:S(2)}, u32[]{:S(2)}) collective-permute-start(bf16[2,432,384]{2,1,0:T(8,128)(2,1)S(1)} %get-tuple-element.98), channel_id=1, source_target_pairs={{0,2},{2,0},{1,3},{3,1},{4,6},{6,4},{5,7},{7,5},{8,10},{10,8},{9,1... | collective-permute-start | bytes 1990664 | tf_op jit(solution)/shard_map/ppermute | solution.py:646
  386.7 41.4 %collective-permute-start.46 = (bf16[4,432,384]{2,1,0:T(8,128)(2,1)}, bf16[4,432,384]{2,1,0:T(8,128)(2,1)}, u32[]{:S(2)}, u32[]{:S(2)}) collective-permute-start(bf16[4,432,384]{2,1,0:T(8,128)(2,1)} %pad_maximum_fusion.1), channel_id=1, source_target_pairs={{0,16},{16,0},{1,17},{17,1},{2,18},{18,2},{3,19},{19,3},{4,20},{20... | collective-permute-start | bytes 3981320 | tf_op jit(solution)/shard_map/ppermute | solution.py:646
  387.9 40.3 %collective-permute-start.47 = (bf16[4,432,384]{2,1,0:T(8,128)(2,1)}, bf16[4,432,384]{2,1,0:T(8,128)(2,1)}, u32[]{:S(2)}, u32[]{:S(2)}) collective-permute-start(bf16[4,432,384]{2,1,0:T(8,128)(2,1)} %pad_maximum_fusion.2), channel_id=1, source_target_pairs={{0,2},{2,0},{1,3},{3,1},{4,6},{6,4},{5,7},{7,5},{8,10},{10,8},{9,1... | collective-permute-start | bytes 3981320 | tf_op jit(solution)/shard_map/ppermute | solution.py:646
  398.1 17.6 %collective-permute-start.45 = (bf16[160,384]{1,0:T(8,128)(2,1)S(1)}, bf16[160,384]{1,0:T(8,128)(2,1)S(1)}, u32[]{:S(2)}, u32[]{:S(2)}) collective-permute-start(bf16[160,384]{1,0:T(8,128)(2,1)S(1)} %get-tuple-element.167), channel_id=1, source_target_pairs={{0,12},{4,0},{8,4},{12,8},{1,13},{5,1},{9,5},{13,9},{2,14},{6,2},{... | collective-permute-start | bytes 368648 | tf_op jit(solution)/shard_map/ppermute | solution.py:646
  401.6 25.5 %collective-permute-start.44 = (bf16[160,384]{1,0:T(8,128)(2,1)S(1)}, bf16[160,384]{1,0:T(8,128)(2,1)S(1)}, u32[]{:S(2)}, u32[]{:S(2)}) collective-permute-start(bf16[160,384]{1,0:T(8,128)(2,1)S(1)} %get-tuple-element.168), channel_id=1, source_target_pairs={{0,8},{4,12},{8,0},{12,4},{1,9},{5,13},{9,1},{13,5},{2,10},{6,14},... | collective-permute-start | bytes 368648 | tf_op jit(solution)/shard_map/ppermute | solution.py:646
  407.3 57.6 %collective-permute-start.31 = (bf16[1024,768]{1,0:T(8,128)(2,1)}, bf16[1024,768]{1,0:T(8,128)(2,1)}, u32[]{:S(2)}, u32[]{:S(2)}) collective-permute-start(bf16[1024,768]{1,0:T(8,128)(2,1)} %get-tuple-element.87), channel_id=1, source_target_pairs={{0,0},{1,16},{16,1},{17,17},{2,2},{3,18},{18,3},{19,19},{4,4},{5,2... | collective-permute-start | bytes 4718600 | tf_op jit(solution)/shard_map/ppermute | solution.py:689
  415.7 49.2 %collective-permute-start.36 = (bf16[1024,768]{1,0:T(8,128)(2,1)}, bf16[1024,768]{1,0:T(8,128)(2,1)}, u32[]{:S(2)}, u32[]{:S(2)}) collective-permute-start(bf16[1024,768]{1,0:T(8,128)(2,1)} %shard_map.369), channel_id=1, source_target_pairs={{0,1},{1,0},{2,3},{3,2},{4,5},{5,4},{6,7},{7,6},{8,9},{9,8},{10,11... | collective-permute-start | bytes 4718600 | tf_op jit(solution)/shard_map/ppermute | solution.py:685
  431.5 17.6 %collective-permute-start.50 = (bf16[432,384]{1,0:T(8,128)(2,1)S(1)}, bf16[432,384]{1,0:T(8,128)(2,1)S(1)}, u32[]{:S(2)}, u32[]{:S(2)}) collective-permute-start(bf16[432,384]{1,0:T(8,128)(2,1)S(1)} %get-tuple-element.134), channel_id=1, source_target_pairs={{0,12},{4,0},{8,4},{12,8},{1,13},{5,1},{9,5},{13,9},{2,14},{6,2},{... | collective-permute-start | bytes 995336 | tf_op jit(solution)/shard_map/ppermute | solution.py:646
  434.4 29.6 %collective-permute-start.49 = (bf16[432,384]{1,0:T(8,128)(2,1)S(1)}, bf16[432,384]{1,0:T(8,128)(2,1)S(1)}, u32[]{:S(2)}, u32[]{:S(2)}) collective-permute-start(bf16[432,384]{1,0:T(8,128)(2,1)S(1)} %get-tuple-element.135), channel_id=1, source_target_pairs={{0,8},{4,12},{8,0},{12,4},{1,9},{5,13},{9,1},{13,5},{2,10},{6,14},... | collective-permute-start | bytes 995336 | tf_op jit(solution)/shard_map/ppermute | solution.py:646
  471.9 21.9 %collective-permute-start.37 = (bf16[1024,768]{1,0:T(8,128)(2,1)}, bf16[1024,768]{1,0:T(8,128)(2,1)S(1)}, u32[]{:S(2)}, u32[]{:S(2)}) collective-permute-start(bf16[1024,768]{1,0:T(8,128)(2,1)} %shard_map.370), channel_id=1, source_target_pairs={{0,0},{1,16},{16,1},{17,17},{2,2},{3,18},{18,3},{19,19},{4,4},{5,2... | collective-permute-start | bytes 4718600 | tf_op jit(solution)/shard_map/ppermute | solution.py:689
  (31 other events, 435.2 us)

commit v3 on v2

--- a/solution.py
+++ b/solution.py
@@ -1,3 +1,5 @@
+import functools
+
 import jax
 import jax.numpy as jnp
 import numpy as np
@@ -232,6 +234,59 @@
         compiler_params=params(2),
         cost_estimate=cost(count * total * total * 5120, total * 128 * 2 * 12),
     )(segs, qkv, qkv, qkv, o_own, o_far, d_own, d_far, lse, *prev)
+
+
+def pack_body(info, qkv, w_out, w_in, w_down, small, mine, give):
+    me = info[0]
+    for half_at, dst in ((me, mine), (1 - me, give)):
+        slab = 0
+
+        def cols(base):
+            return pl.ds(pl.multiple_of(base + half_at * HALF, 128), HALF)
+
+        for j in range(3):
+            dst[slab] = qkv[:, cols(j * D)]
+            slab += 1
+        dst[slab] = jnp.zeros(dst.shape[1:], bf16)
+        dst[slab, :, 0:128] = small[...]
+        dst[slab + 1] = w_out[:, cols(0)]
+        slab += 2
+        for j in range(w_in.shape[1] // D):
+            dst[slab] = w_in[:, cols(j * D)]
+            slab += 1
+        for j in range(w_down.shape[0]):
+            dst[slab] = w_down[j, :, cols(0)]
+            slab += 1
+
+
+def combine_body(info, mine, got, unit1, unit2):
+    me = info[0]
+    n = unit2.shape[0] // 2
+    wide = n // 2
+    unit1[6] = jnp.zeros(unit1.shape[1:], bf16)
+    for at, src in ((me, mine), (1 - me, got)):
+        for j in range(3):
+            unit1[2 * j + at] = src[j]
+        for j in range(wide + 1):
+            unit2[2 * j + at] = src[4 + j]
+        for j in range(wide):
+            unit2[2 * (wide + 1) + at * wide + j] = src[5 + wide + j]
+    unit1[6, :, 0:128] = mine[3, :, 0:128]
+    unit1[6, :, 128:256] = got[3, :, 0:128]
+
+
+def whole_call(body, ins, outs, *args):
+    return pl.pallas_call(
+        body,
+        grid_spec=pltpu.PrefetchScalarGridSpec(
+            num_scalar_prefetch=1,
+            grid=(),
+            in_specs=[pl.BlockSpec(memory_space=pltpu.VMEM)] * ins,
+            out_specs=[pl.BlockSpec(memory_space=pltpu.VMEM)] * len(outs),
+        ),
+        out_shape=[shape(o) for o in outs],
+        cost_estimate=cost(0, 2 << 20),
+    )(*args)
 
 
 def each_slot(pieces):
@@ -436,40 +491,36 @@
     )(info, tok, o_own, o_got, back, vecs, bias_in, *pieces)
 
 
-def wgrad_body(info, act, ig, low, branch, o_own, o_got, attn_grad, keep, send, res_in, res_down, res_out, sems):
+def wgrad_body(own, info, act, ig, low, branch, o_own, o_got, attn_grad, dst, res_in, res_down, res_out, sems):
     j = pl.program_id(0)
     n = pl.num_programs(0)
     me = info[0]
     par = lax.rem(j, 2)
     down_rows = ROWS * n
     per_step = SLOTS // n
+    half_at = me if own else 1 - me
+    lane = pl.ds(pl.multiple_of(half_at * HALF, HALF), HALF)
 
     @pl.when(j == 0)
     def _():
-        for at, dst in ((0, send), (1, keep)):
-            half_at = me if at == 1 else 1 - me
-            lane = pl.ds(pl.multiple_of(half_at * HALF, HALF), HALF)
-            grad = attn_grad[:, lane]
-            for here, rows in ((me, o_own), (1 - me, o_got)):
-                spot = pl.ds(pl.multiple_of(here * HALF, HALF), HALF)
-                res_out[at, spot, :] = mxu(rows[...], grad, TN).astype(bf16)
-            for chip in range(SLOTS):
-                src = res_out.at[at, chip * ROWS : (chip + 1) * ROWS, :]
-                pltpu.make_async_copy(src, dst.at[info[1 + chip], 0:ROWS, :], sems.at[2]).start()
-
-    for at, dst in ((0, send), (1, keep)):
-        half_at = me if at == 1 else 1 - me
-        lane = pl.ds(pl.multiple_of(half_at * HALF, HALF), HALF)
-        res_in[par, at] = mxu(low[...], ig[:, lane], TN).astype(bf16)
+        grad = attn_grad[:, lane]
+        for here, rows in ((me, o_own), (1 - me, o_got)):
+            spot = pl.ds(pl.multiple_of(here * HALF, HALF), HALF)
+            res_out[spot, :] = mxu(rows[...], grad, TN).astype(bf16)
         for chip in range(SLOTS):
-            src = res_in.at[par, at, chip * ROWS : (chip + 1) * ROWS, :]
-            spot = pl.ds(pl.multiple_of((1 + j) * ROWS, ROWS), ROWS)
-            pltpu.make_async_copy(src, dst.at[info[1 + chip], spot, :], sems.at[par]).start()
-        res_down[par, at] = mxu(act[...], branch[:, lane], TN).astype(bf16)
-        for q in range(per_step):
-            src = res_down.at[par, at, q * down_rows : (q + 1) * down_rows, :]
-            slot = info[1 + j * per_step + q]
-            pltpu.make_async_copy(src, dst.at[slot, ROWS * (1 + n) : ROWS * (1 + 2 * n), :], sems.at[par]).start()
+            src = res_out.at[chip * ROWS : (chip + 1) * ROWS, :]
+            pltpu.make_async_copy(src, dst.at[info[1 + chip], 0:ROWS, :], sems.at[2]).start()
+
+    res_in[par] = mxu(low[...], ig[:, lane], TN).astype(bf16)
+    for chip in range(SLOTS):
+        src = res_in.at[par, chip * ROWS : (chip + 1) * ROWS, :]
+        spot = pl.ds(pl.multiple_of((1 + j) * ROWS, ROWS), ROWS)
+        pltpu.make_async_copy(src, dst.at[info[1 + chip], spot, :], sems.at[par]).start()
+    res_down[par] = mxu(act[...], branch[:, lane], TN).astype(bf16)
+    for q in range(per_step):
+        src = res_down.at[par, q * down_rows : (q + 1) * down_rows, :]
+        slot = info[1 + j * per_step + q]
+        pltpu.make_async_copy(src, dst.at[slot, ROWS * (1 + n) : ROWS * (1 + 2 * n), :], sems.at[par]).start()
 
     def settle(which):
         wait_for(res_in.at[which], sems.at[which])
@@ -485,29 +536,28 @@
         wait_for(res_out, sems.at[2])
 
 
-def weight_grads(info, act, ig, low, branch, o_own, o_got, attn_grad):
+def weight_grads(own, info, act, ig, low, branch, o_own, o_got, attn_grad):
     half, ff = act.shape
     n = ff // D
     strip = pl.BlockSpec((half, D), lambda j, *_: (0, j))
     fixed = lambda cols: pl.BlockSpec((half, cols), lambda j, *_: (0, 0))
-    size = (SLOTS, ROWS * (1 + 2 * n), HALF)
     return pl.pallas_call(
-        wgrad_body,
+        functools.partial(wgrad_body, own),
         grid_spec=pltpu.PrefetchScalarGridSpec(
             num_scalar_prefetch=1,
             grid=(n,),
             in_specs=[strip, strip, fixed(D), fixed(D), fixed(HALF), fixed(HALF), fixed(D)],
-            out_specs=[anyspec(), anyspec()],
+            out_specs=anyspec(),
             scratch_shapes=[
-                pltpu.VMEM((2, 2, D, HALF), bf16),
-                pltpu.VMEM((2, 2, D, HALF), bf16),
                 pltpu.VMEM((2, D, HALF), bf16),
+                pltpu.VMEM((2, D, HALF), bf16),
+                pltpu.VMEM((D, HALF), bf16),
                 pltpu.SemaphoreType.DMA((3,)),
             ],
         ),
-        out_shape=[shape(size), shape(size)],
+        out_shape=shape((SLOTS, ROWS * (1 + 2 * n), HALF)),
         compiler_params=params(),
-        cost_estimate=cost(half * D * (D + 2 * ff) * 2, half * ff * 8),
+        cost_estimate=cost(half * D * (D + 2 * ff), half * ff * 8),
     )(info, act, ig, low, branch, o_own, o_got, attn_grad)
 
 
@@ -685,8 +735,12 @@
     return lax.ppermute(x, "c", [(0, 1), (1, 0)])
 
 
-def relocate(x):
-    return lax.ppermute(x, ("s", "c"), [(0, 0), (1, 2), (2, 1), (3, 3)])
+def cross(x):
+    return lax.ppermute(x, ("s", "c"), [(1, 2), (2, 1)])
+
+
+def together(*values):
+    return lax.optimization_barrier(values)
 
 
 def half_of(x, at):
@@ -720,71 +774,102 @@
           norm1_gain, norm1_shift, in_weight, in_bias, down_weight, down_bias, norm2_gain, norm2_shift, cotangent):
     half = tokens.shape[1]
     me = plan.at(len(plan.dims) - 1)
+    stays = plan.at(0) == me
     rows_dev = qkv_weight.shape[0]
     ff_dev = down_weight.shape[0]
     ff_cols = in_weight.shape[1] // D
     me32 = me.astype(jnp.int32)
     pull = jnp.concatenate([me32[None], plan.chip_table(-1)])
     push = jnp.concatenate([me32[None], plan.slot_table(1)])
-
     sizes1 = [rows_dev] * 3
     sizes2 = [rows_dev] * (1 + ff_cols) + [ff_dev]
-    first = jnp.concatenate([qkv_weight[:, j * D : (j + 1) * D] for j in range(3)], axis=0)
-    second = jnp.concatenate([out_weight] + [in_weight[:, j * D : (j + 1) * D] for j in range(ff_cols)] + [down_weight], axis=0)
     smalls = (query_bias, value_bias, out_bias, norm1_gain, norm1_shift, in_bias, down_bias, norm2_gain, norm2_shift)
-    line = jnp.concatenate(smalls)
-    both = jnp.concatenate([first, second], axis=0)
-    got = swap_pair(half_of(both, 1 - me))
-    mine = half_of(both, me)
-    cut = 3 * rows_dev
-    unit1 = chip_units(me, mine[:cut], got[:cut], sizes1)
-    unit2 = chip_units(me, mine[cut:], got[cut:], sizes2)
-    line_got = swap_pair(line)
-    line_unit = jnp.stack([jnp.where(me == 0, line, line_got), jnp.where(me == 0, line_got, line)])
-
-    tok = relocate(tokens[0])
+    unit_rows = 2 * half // UNITS
+
+    def settle_rows(x, got):
+        return jnp.where(stays, x, got)
+
+    tok = settle_rows(tokens[0], cross(tokens[0]))
     if plan.direct:
+        counts = [(lengths[0] // unit_rows).astype(bf16), block_order[0].astype(bf16)]
+        lines = [jnp.pad(v, (0, 128 - v.shape[0])) for v in smalls + tuple(counts)]
+        lines += [jnp.zeros((128,), bf16)] * (rows_dev - len(lines))
+        slabs = 5 + 2 * ff_cols
+        slab = (slabs, rows_dev, HALF)
+        mine, give = whole_call(pack_body, 5, (slab, slab), pull, qkv_weight, out_weight, in_weight,
+                                down_weight.reshape(ff_cols, rows_dev, D), jnp.stack(lines))
+        got = swap_pair(give)
+        unit1, unit2 = whole_call(combine_body, 2, ((7, rows_dev, HALF), (2 + 4 * ff_cols, rows_dev, HALF)), pull, mine, got)
+        unit1 = unit1.reshape(7 * rows_dev, HALF)
+        unit2 = unit2.reshape(-1, HALF)
+        other = got[3, len(smalls) : len(smalls) + 2, :UNITS].astype(jnp.int32)
+        counts_here = jnp.where(stays, lengths[0] // unit_rows, other[0])
+        order_here = jnp.where(stays, block_order[0], other[1])
+
         z1 = gather_z(plan, unit1)
+        unit2, z1 = together(unit2, z1)
         x1, y1 = plan.send(z1, 0), plan.send(z1, 2)
-        pieces1 = [z1, x1, y1, plan.send(y1[0:2], 0), plan.send(x1[2:4], 2)]
-        z2 = gather_z(plan, tie(unit2, z1))
+        z2_parts = [unit2] + [plan.send(unit2, 1, k) for k in range(1, 4)]
+        cot, x1, y1 = together(cotangent[0], x1, y1)
+        d1a, d1b = plan.send(y1[0:2], 0), plan.send(x1[2:4], 2)
+        cot_got = cross(cot)
+        pieces1 = [z1, x1, y1, d1a, d1b]
+        tail_rows = [p[:, 6 * rows_dev : 6 * rows_dev + 16, 0:256] for p in pieces1]
+        table = jnp.take(jnp.concatenate(tail_rows, axis=0), plan.slot_table(-1), axis=0, mode="clip")
+        table = table.reshape(plan.chips, 16, 2, 128)
+        table = jnp.where(me == 0, table, table[:, :, ::-1])
+        vectors = [table[:, i, :, : v.shape[0]].reshape(-1).astype(f32) for i, v in enumerate(smalls)]
     else:
+        first = jnp.concatenate([qkv_weight[:, j * D : (j + 1) * D] for j in range(3)], axis=0)
+        second = jnp.concatenate([out_weight] + [in_weight[:, j * D : (j + 1) * D] for j in range(ff_cols)] + [down_weight], axis=0)
+        line = jnp.concatenate(smalls)
+        both = jnp.concatenate([first, second], axis=0)
+        got = swap_pair(half_of(both, 1 - me))
+        mine = half_of(both, me)
+        cut = 3 * rows_dev
+        unit1 = chip_units(me, mine[:cut], got[:cut], sizes1)
+        unit2 = chip_units(me, mine[cut:], got[cut:], sizes2)
+        line_got = swap_pair(line)
+        line_unit = jnp.stack([jnp.where(me == 0, line, line_got), jnp.where(me == 0, line_got, line)])
         pieces1 = [regroup(gather_chips(plan, unit1), [2 * r for r in sizes1], SLOTS)]
         pieces2 = [regroup(gather_chips(plan, unit2), [2 * r for r in sizes2], SLOTS)]
         far2 = [swap_pair(p) for p in pieces2]
-    lines = gather_chips(plan, line_unit).reshape(2 * plan.chips, line.shape[0])
-    vectors = []
-    at = 0
-    for piece in smalls:
-        size = piece.shape[0]
-        vectors.append(lines[:, at : at + size].reshape(2 * plan.chips * size).astype(f32))
-        at += size
+        lines = gather_chips(plan, line_unit).reshape(2 * plan.chips, line.shape[0])
+        vectors = []
+        at = 0
+        for piece in smalls:
+            size = piece.shape[0]
+            vectors.append(lines[:, at : at + size].reshape(2 * plan.chips * size).astype(f32))
+            at += size
+        counts_here = jnp.where(stays, lengths[0], swap_pair(lengths[0])) // unit_rows
+        order_here = jnp.where(stays, block_order[0], swap_pair(block_order[0]))
+        cot_got = cross(cotangent[0])
     bias_q, bias_v, bias_o, gain1, shift1, bias_in, bias_d, gain2, shift2 = vectors
     bias_qkv = jnp.concatenate([half_of(bias_q, me), jnp.zeros((HALF,), f32), half_of(bias_v, me)])[None]
     zero = jnp.zeros((D,), f32)
     vecs = jnp.stack([bias_o, gain1, shift1, bias_d, gain2, shift2, zero, zero])
 
-    ends = jnp.cumsum(lengths[0])
-    unit_rows = 2 * half // UNITS
-    seg_packed = jnp.sum((jnp.arange(UNITS)[:, None] * unit_rows >= ends[None, :]).astype(jnp.int32), axis=1)
-    hit = block_order[0][:, None] == jnp.arange(UNITS)[None, :]
-    seg_here = jnp.sum(jnp.where(hit, seg_packed[:, None], 0), axis=0)
-    segs = jnp.where(plan.at(0) == me, seg_here, swap_pair(seg_here))
+    spot = jnp.arange(UNITS)
+    ends = jnp.sum(jnp.where(spot[None, :] <= spot[:, None], counts_here[None, :], 0), axis=1)
+    seg_packed = jnp.sum((spot[:, None] >= ends[None, :]).astype(jnp.int32), axis=1)
+    hit = order_here[:, None] == spot[None, :]
+    segs = jnp.sum(jnp.where(hit, seg_packed[:, None], 0), axis=0)
     segs = jnp.where(me == 0, segs, jnp.roll(segs, UNITS // 2))
 
     tok_got = swap_pair(tok)
     qkv, w_qkv = project(pull, tok, tok_got, bias_qkv, pieces1)
-    back = relocate(tie(cotangent[0], pieces1[-1]))
     if plan.direct:
-        qkv = tie(qkv, z2)
+        *z2_parts, qkv = together(*z2_parts, qkv)
+        z2 = jnp.stack(z2_parts)
         x2, y2 = plan.send(z2, 0), plan.send(z2, 2)
         z2_far = swap_pair(z2)
-    att = attention(segs, qkv, 0, 2, None)
-    if plan.direct:
-        y2_cut, x2_cut = lax.optimization_barrier((y2[0:2], x2[2:4], att[0]))[:2]
-        d2a, d2b = plan.send(y2_cut, 0), plan.send(x2_cut, 2)
+        att = attention(segs, qkv, 0, 2, None)
+        x2, y2, cot_got, *att = together(x2, y2, cot_got, *att)
+        d2a, d2b = plan.send(y2[0:2], 0), plan.send(x2[2:4], 2)
         x2_far, y2_far = swap_pair(x2), swap_pair(y2)
-        att = lax.optimization_barrier(tuple(att) + (y2_cut, x2_cut))[:3]
+    else:
+        att = attention(segs, qkv, 0, 2, None)
+    back = settle_rows(cotangent[0], cot_got)
     o_own, o_far, lse = attention(segs, qkv, 2, PAIRS - 2, att)
     o_got = swap_pair(o_far)
     if plan.direct:
@@ -793,63 +878,71 @@
     (out_rows, act, ig, low, branch, attn_grad, resid1, d_own, d_far, sums) = middle(
         pull, tok, o_own, o_got, back, vecs, bias_in[None], pieces2, far2)
     d_got = swap_pair(d_far)
+    out_got = cross(out_rows)
     sum_got = swap_pair(half_of(sums, 1 - me))
-    small = half_of(sums, me) + sum_got
-    keep, give = weight_grads(push, act, ig, low, branch, o_own, o_got, attn_grad)
+    grad_args = (low, branch, o_own, o_got)
+    give = weight_grads(False, push, act, ig, *grad_args, attn_grad)
+    give, attn_grad = together(give, attn_grad)
+    got_g = swap_pair(give)
+    keep = weight_grads(True, push, act, ig, *grad_args, attn_grad)
     back_args = (o_own, o_far, d_own, d_got, lse)
     if plan.direct:
-        got_g = swap_pair(give)
-        g0 = attention_back(segs, tie(qkv, give), *back_args, 0, 1, None)
-        output = relocate(tie(out_rows, give))
 
         def both_sums(lo, hi):
             return keep[lo:hi].astype(f32) + got_g[lo:hi].astype(f32)
 
         step1 = both_sums(12, 16).astype(bf16)
-        sx, sy = lax.optimization_barrier((step1[:2], step1[2:], g0[0]))[:2]
+        sx, sy, qkv_back, out_got = together(step1[:2], step1[2:], qkv, out_got)
         rx, ry = plan.send(sx, 0), plan.send(sy, 2)
-        g0 = lax.optimization_barrier(tuple(g0) + (sx, sy))[:3]
-        g1 = attention_back(segs, qkv, *back_args, 1, 1, g0)
-        rx, ry = lax.optimization_barrier((rx, ry, g1[0]))[:2]
+        g = attention_back(segs, qkv_back, *back_args, 0, 1, None)
+        rx, ry, sum_got, *g = together(rx, ry, sum_got, *g)
         send_x = jnp.concatenate([both_sums(4, 6), both_sums(6, 8) + ry.astype(f32)], axis=0).astype(bf16)
         send_y = jnp.concatenate([both_sums(8, 10) + rx.astype(f32), both_sums(10, 12)], axis=0).astype(bf16)
+        send_x, send_y, *g = together(send_x, send_y, *g)
         px, py = plan.send(send_x, 0), plan.send(send_y, 2)
-        g1 = lax.optimization_barrier(tuple(g1) + (send_x, send_y))[:3]
-        dq, dk, dv = attention_back(segs, qkv, *back_args, 2, PAIRS - 2, g1)
-        px, py = lax.optimization_barrier((px, py, dq))[:2]
+        g = attention_back(segs, qkv_back, *back_args, 1, 1, g)
+        px, py, *g = together(px, py, *g)
         z_sum = both_sums(0, 4) + px.astype(f32) + py.astype(f32)
-        z_low = z_sum[1:].astype(bf16)
-        ffn = z_sum[0]
-        for k in range(1, 4):
-            ffn = ffn + plan.send(z_low[k - 1], 1, k).astype(f32)
-        dq = tie(dq, z_low)
+        z_low, ffn, *g = together(z_sum[1:].astype(bf16), z_sum[0], *g)
+        z_got = [plan.send(z_low[k - 1], 1, k) for k in range(1, 4)]
+        g = attention_back(segs, qkv_back, *back_args, 2, PAIRS - 2, g)
+        *z_got, dq, dk, dv = together(*z_got, *g)
+        for part in z_got:
+            ffn = ffn + part.astype(f32)
     else:
-        output = relocate(out_rows)
         dq, dk, dv = attention_back(segs, qkv, *back_args, 0, PAIRS, None)
-        summed = (keep.astype(f32) + swap_pair(give).astype(f32)).astype(bf16)
+        summed = (keep.astype(f32) + got_g.astype(f32)).astype(bf16)
         scale = plan.chips // SLOTS
         units = regroup_back(summed, [ROWS] * (1 + ff_cols) + [ROWS * ff_cols], scale)
         ffn = reduce_chips(plan, units)
+    output = settle_rows(out_rows, out_got)
+    small = half_of(sums, me) + sum_got
     tail = qkv_grads(push, small, tok, tok_got, dq, dk, dv)
     if plan.direct:
         rx, ry = plan.send(tail[12:14], 0), plan.send(tail[14:16], 2)
-        far_back = swap_pair(input_back(w_qkv, dq, dk, dv, True, ()))
+        far_back = input_back(w_qkv, dq, dk, dv, True, ())
+        rx, ry, far_back = together(rx, ry, far_back)
+        far_back = swap_pair(far_back)
         send_x = jnp.concatenate([tail[4:6], (tail[6:8].astype(f32) + ry.astype(f32)).astype(bf16)], axis=0)
         send_y = jnp.concatenate([(tail[8:10].astype(f32) + rx.astype(f32)).astype(bf16), tail[10:12]], axis=0)
         px, py = plan.send(send_x, 0), plan.send(send_y, 2)
         packed = input_back(w_qkv, dq, dk, dv, False, (resid1, far_back))
-        input_grad = relocate(packed)
+        px, py, packed = together(px, py, packed)
+        packed_got = cross(packed)
         z_sum = tail[0:4].astype(f32) + px.astype(f32) + py.astype(f32)
         z_low = z_sum[1:].astype(bf16)
         qkv_sum = z_sum[0]
-        for k in range(1, 4):
-            qkv_sum = qkv_sum + plan.send(z_low[k - 1], 1, k).astype(f32)
+        packed_got, *z_got = together(packed_got, *[plan.send(z_low[k - 1], 1, k) for k in range(1, 4)])
+        for part in z_got:
+            qkv_sum = qkv_sum + part.astype(f32)
     else:
         far_back = swap_pair(input_back(w_qkv, dq, dk, dv, True, ()))
-        input_grad = relocate(input_back(w_qkv, dq, dk, dv, False, (resid1, far_back)))
+        packed = input_back(w_qkv, dq, dk, dv, False, (resid1, far_back))
+        packed_got = cross(packed)
         units = regroup_back(tail[:, : 3 * ROWS], [ROWS] * 3, scale)
         extra = jnp.broadcast_to(tail[0:1, 3 * ROWS :], (plan.chips, 16, HALF))
         qkv_sum = reduce_chips(plan, jnp.concatenate([units, extra], axis=1))
+    input_grad = settle_rows(packed, packed_got)
 
     small_sum = qkv_sum[6 * rows_dev :]
     sizes = sizes1 + sizes2
@@ -869,12 +962,11 @@
     for a in range(1, len(plan.dims)):
         device = device * plan.dims[a] + plan.at(a)
     order = (14, 15, 0, 1, 2, 3, 3 + ff_cols, 4 + ff_cols, 5 + ff_cols)
-    outs = []
-    for piece, row in zip(smalls, order):
-        size = piece.shape[0]
-        span = small_full[row : row + size * 2 * plan.chips // D].reshape(-1)
-        outs.append(lax.dynamic_slice_in_dim(span, device * size, size))
-    s = outs
+    wide_row = 3
+    thin = lax.dynamic_slice_in_dim(small_full, device * rows_dev, rows_dev, axis=1)
+    span = small_full[wide_row : wide_row + ff_cols].reshape(-1)
+    s = [lax.dynamic_slice_in_dim(span, device * ff_dev, ff_dev) if row == wide_row and piece is in_bias else thin[row]
+         for piece, row in zip(smalls, order)]
     return (output[None], input_grad[None], out_qkv, s[0], s[1], out_out, s[2], s[3], s[4], out_in, s[5], out_down, s[6], s[7], s[8])
 
 

time: 505 us -> 389 us (0.77)
  starting transfers between devices: 111 us -> 45.3 us
  waiting for transfers between devices: 108 us -> 44.6 us
  Pallas kernels: 223 us -> 235 us
  other arithmetic: 25.1 us -> 35.5 us
  local copies, waits for them, and re-layouts: 29 us -> 23 us
    ppermute x33 -> x28, waiting for transfers between devices: 86.2 us -> 40.7 us  [send(): return lax.ppermute(x, self.names[a], shift(self.dims[a], k))]
    ppermute x15 -> x13, starting transfers between devices: 50.5 us -> 7.45 us  [swap_pair(): return lax.ppermute(x, 'c', [(0, 1), (1, 0)])]
    ppermute x33 -> x28, starting transfers between devices: 41.6 us -> 22.8 us  [send(): return lax.ppermute(x, self.names[a], shift(self.dims[a], k))]
    pallas_call x1 -> x4, Pallas kernels: 21.2 us -> 33.7 us  [the longest x2 28.6 us: weight_grads(): pl.pallas_call(functools.partial(wgrad_body, own), grid_spec=pltpu.Prefet...]
    ppermute x15 -> x13, waiting for transfers between devices: 10.2 us -> 0.03 us  [swap_pair(): return lax.ppermute(x, 'c', [(0, 1), (1, 0)])]
    ppermute x4, waiting for transfers between devices: 11.8 us -> 3.81 us  [cross(): return lax.ppermute(x, ('s', 'c'), [(1, 2), (2, 1)])]
    concatenate x6 -> x1, local copies, waits for them, and re-layouts: 7.08 us -> 0.01 us  [local(): jnp.concatenate(tail_rows, axis=0)]
    select_n x5, other arithmetic: 0.19 us -> 6.31 us  [the longest x2 5.44 us: settle_rows(): return jnp.where(stays, x, got)]
  transfers between devices with their start and end apart: 52 -> 45, of which waited for: 15 -> 13; matrix products, arithmetic and copies ran while one was open for 7% -> 8% of each run, Pallas kernels for 25% -> 44%
where the time goes in v3:
time: 389 us; the launch traced here: 386 us
  Pallas kernels  235 us (60%)
  starting transfers between devices  45.3 us (12%)
  waiting for transfers between devices  44.6 us (11%)
  other arithmetic  35.5 us (9%)
  local copies, waits for them, and re-layouts  23 us (6%)
    pallas_call x3, Pallas kernels, attention_back(): pl.pallas_call(attend_back_body, grid_spec=pltpu.PrefetchScalarGridSpec(n...  85.4 us
    pallas_call x2, Pallas kernels, attention(): pl.pallas_call(attend_body, grid_spec=pltpu.PrefetchScalarGridSpec(num_sc...  42.8 us
    ppermute x28, waiting for transfers between devices, send(): return lax.ppermute(x, self.names[a], shift(self.dims[a], k))  40.7 us
    pallas_call x1, Pallas kernels, middle(): pl.pallas_call(mid_body, grid_spec=pltpu.PrefetchScalarGridSpec(num_scala...  39.2 us
    pallas_call x2, Pallas kernels, weight_grads(): pl.pallas_call(functools.partial(wgrad_body, own), grid_spec=pltpu.Prefet...  28.6 us
    ppermute x28, starting transfers between devices, send(): return lax.ppermute(x, self.names[a], shift(self.dims[a], k))  22.8 us
    ppermute x4, starting transfers between devices, cross(): return lax.ppermute(x, ('s', 'c'), [(1, 2), (2, 1)])  15.1 us
    pallas_call x2, Pallas kernels, input_back(): pl.pallas_call(input_back_body, grid=(half // tile,), in_specs=[pl.BlockS...  13 us
  transfers between devices with their start and end apart: 45, of which 13 were waited for; matrix products, arithmetic and copies ran while one was open for 8% of the time, Pallas kernels for 44%

profile of v3, /device:TPU:1, one launch (start us, length us, event | category | flops | bytes accessed | tf_op | source)
XLA Modules:
  0.0 385.6 jit_solution(14947836272564325137)
XLA Ops:
  8.6 2.5 shard_map.361
  11.1 4.5 %collective-permute-start = (bf16[1024,768]{1,0:T(8,128)(2,1)}, bf16[1024,768]{1,0:T(8,128)(2,1)}, u32[]{:S(2)}, u32[]{:S(2)}) collective-permute-start(bf16[1024,768]{1,0:T(8,128)(2,1)} %bitcast.120), channel_id=1, source_target_pairs={{1,16},{16,1},{3,18},{18,3},{5,20},{20,5},{7,22},{22,7},{9,24},{24... | collective-permute-start | bytes 4718600 | tf_op jit(solution)/shard_map/ppermute | solution.py:739
  17.1 2.5 shard_map.362
  19.7 3.3 collective-permute-start.4
  26.6 7.6 %collective-permute-done.3 = bf16[168,384]{1,0:T(8,128)(2,1)S(1)} collective-permute-done((bf16[168,384]{1,0:T(8,128)(2,1)}, bf16[168,384]{1,0:T(8,128)(2,1)S(1)}, u32[]{:S(2)}, u32[]{:S(2)}) %collective-permute-start.3) | collective-permute-done | bytes 129056 | tf_op jit(solution)/shard_map/ppermute | solution.py:696
  36.5 2.7 broadcast_select_fusion.1.t_own.tok
  41.8 6.5 %collective-permute-done.10.refs_2_ = bf16[4,168,384]{2,1,0:T(8,128)(2,1)S(1)} collective-permute-done((bf16[4,168,384]{2,1,0:T(8,128)(2,1)S(1)}, bf16[4,168,384]{2,1,0:T(8,128)(2,1)S(1)}, u32[]{:S(2)}, u32[]{:S(2)}) %collective-permute-start.10) | collective-permute-done | bytes 516128 | tf_op jit(solution)/shard_map/ppermute | solution.py:696
  49.8 6.0 %collective-permute-done.11.refs_3_ = bf16[2,168,384]{2,1,0:T(8,128)(2,1)S(1)} collective-permute-done((bf16[2,168,384]{2,1,0:T(8,128)(2,1)S(1)}, bf16[2,168,384]{2,1,0:T(8,128)(2,1)S(1)}, u32[]{:S(2)}, u32[]{:S(2)}) %collective-permute-start.11) | collective-permute-done | bytes 258080 | tf_op jit(solution)/shard_map/ppermute | solution.py:696
  57.4 4.1 %collective-permute-start.15 = (bf16[1024,768]{1,0:T(8,128)(2,1)S(1)}, bf16[1024,768]{1,0:T(8,128)(2,1)S(1)}, u32[]{:S(2)}, u32[]{:S(2)}) collective-permute-start(bf16[1024,768]{1,0:T(8,128)(2,1)S(1)} %bitcast.121), channel_id=1, source_target_pairs={{1,16},{16,1},{3,18},{18,3},{5,20},{20,5},{7,22},{22,7},{9,24},{24... | collective-permute-start | bytes 4718600 | tf_op jit(solution)/shard_map/ppermute | solution.py:739
  64.1 11.1 %shard_map.363 = (bf16[2048,1152]{1,0:T(8,128)(2,1)}, bf16[768,1152]{1,0:T(8,128)(2,1)}) custom-call(s32[17]{0:T(128)} %pad_add_fusion.info, bf16[1024,768]{1,0:T(8,128)(2,1)} %broadcast_select_fusion.1.t_own.tok, bf16[1024,768]{1,0:T(8,128)(2,1)} %collective-permute-done.8.t_got, f32[1,1152]{1,0:T(1,128)} %broadcast_in_dim.86.bias, ...), custom_call_target="tpu_custom_call" | custom-call | flops 3623878656 | bytes 9437184 | tf_op jit(solution)/shard_map/pallas_call | solution.py:333
  77.2 27.7 %shard_map.364 = (bf16[1024,384]{1,0:T(8,128)(2,1)}, bf16[1024,384]{1,0:T(8,128)(2,1)}, f32[2048,384]{1,0:T(8,128)}) custom-call(s32[16]{0:T(128)} %broadcast_select_fusion.7.segs_ref, bf16[2048,1152]{1,0:T(8,128)(2,1)} %get-tuple-element.143.q_in.k_in.v_in, bf16[2048,1152]{1,0:T(8,128)(2,1)} %get-tuple-element.143.q_in.k_in.v_in, ...), custom_call_target="tpu_custom_call" | custom-call | flops 17179869184 | bytes 4194304 | tf_op jit(solution)/shard_map/pallas_call | solution.py:145
  104.9 2.3 collective-permute-done.14.refs_2_
  113.6 15.1 %shard_map.365 = (bf16[1024,384]{1,0:T(8,128)(2,1)}, bf16[1024,384]{1,0:T(8,128)(2,1)}, f32[2048,384]{1,0:T(8,128)}) custom-call(s32[16]{0:T(128)} %broadcast_select_fusion.7.segs_ref, bf16[2048,1152]{1,0:T(8,128)(2,1)} %get-tuple-element.143.q_in.k_in.v_in, ...), custom_call_target="tpu_custom_call", output_to_operand_aliasing={{0}: (4, {}), {1}: (5, {}), {2}: (6, {})} | custom-call | flops 8589934592 | bytes 4194304 | tf_op jit(solution)/shard_map/pallas_call | solution.py:145
  133.2 2.7 broadcast_select_fusion.back
  137.0 39.2 %shard_map.366 = (bf16[1024,768]{1,0:T(8,128)(2,1)}, bf16[1024,3072]{1,0:T(8,128)(2,1)}, bf16[1024,3072]{1,0:T(8,128)(2,1)}, bf16[1024,768]{1,0:T(8,128)(2,1)}, ...) custom-call(s32[17]{0:T(128)} %pad_add_fusion.info, ...), custom_call_target="tpu_custom_call" | custom-call | flops 21743271936 | bytes 31457280 | tf_op jit(solution)/shard_map/pallas_call | solution.py:462
  176.2 14.2 %shard_map.367 = bf16[16,432,384]{2,1,0:T(8,128)(2,1)} custom-call(s32[17]{0:T(128)} %pad_add_fusion.1.info, bf16[1024,3072]{1,0:T(8,128)(2,1)} %get-tuple-element.132.act, bf16[1024,3072]{1,0:T(8,128)(2,1)} %get-tuple-element.133.ig, bf16[1024,768]{1,0:T(8,128)(2,1)} %get-tuple-element.134.low, bf16[1024,768]{1,0:T(8,128)(2,1)} %get-tuple-element.135.branch, ...), custom_call_target="tpu_custom_call" | custom-call | flops 5435817984 | bytes 25165824 | tf_op jit(solution)/shard_map/pallas_call | solution.py:544
  190.5 3.0 collective-permute-start.25
  194.1 14.4 %shard_map.368 = bf16[16,432,384]{2,1,0:T(8,128)(2,1)} custom-call(s32[17]{0:T(128)} %pad_add_fusion.1.info, bf16[1024,3072]{1,0:T(8,128)(2,1)} %get-tuple-element.132.act, bf16[1024,3072]{1,0:T(8,128)(2,1)} %get-tuple-element.133.ig, bf16[1024,768]{1,0:T(8,128)(2,1)} %get-tuple-element.134.low, bf16[1024,768]{1,0:T(8,128)(2,1)} %get-tuple-element.135.branch, ...), custom_call_target="tpu_custom_call" | custom-call | flops 5435817984 | bytes 25165824 | tf_op jit(solution)/shard_map/pallas_call | solution.py:544
  214.3 28.7 %shard_map.369 = (bf16[2048,384]{1,0:T(8,128)(2,1)}, bf16[2048,384]{1,0:T(8,128)(2,1)}, bf16[2048,384]{1,0:T(8,128)(2,1)}) custom-call(s32[16]{0:T(128)} %broadcast_select_fusion.7.segs_ref, bf16[2048,1152]{1,0:T(8,128)(2,1)} %get-tuple-element.143.q_in.k_in.v_in, bf16[2048,1152]{1,0:T(8,128)(2,1)} %get-tuple-element.143.q_in.k_in.v_in, ...), custom_call_target="tpu_custom_call" | custom-call | flops 21474836480 | bytes 6291456 | tf_op jit(solution)/shard_map/pallas_call | solution.py:218
  243.6 2.7 add_convert_fusion.2
  250.6 28.4 %shard_map.370 = (bf16[2048,384]{1,0:T(8,128)(2,1)}, bf16[2048,384]{1,0:T(8,128)(2,1)}, bf16[2048,384]{1,0:T(8,128)(2,1)}) custom-call(s32[16]{0:T(128)} %broadcast_select_fusion.7.segs_ref, bf16[2048,1152]{1,0:T(8,128)(2,1)} %get-tuple-element.143.q_in.k_in.v_in, ...), custom_call_target="tpu_custom_call", output_to_operand_aliasing={{0}: (9, {}), {1}: (10, {}), {2}: (11, {})} | custom-call | flops 21474836480 | bytes 6291456 | tf_op jit(solution)/shard_map/pallas_call | solution.py:218
  280.6 2.7 convert_add_fusion
  287.4 28.4 %shard_map.371 = (bf16[2048,384]{1,0:T(8,128)(2,1)}, bf16[2048,384]{1,0:T(8,128)(2,1)}, bf16[2048,384]{1,0:T(8,128)(2,1)}) custom-call(s32[16]{0:T(128)} %broadcast_select_fusion.7.segs_ref, bf16[2048,1152]{1,0:T(8,128)(2,1)} %get-tuple-element.143.q_in.k_in.v_in, ...), custom_call_target="tpu_custom_call", output_to_operand_aliasing={{0}: (9, {}), {1}: (10, {}), {2}: (11, {})} | custom-call | flops 21474836480 | bytes 6291456 | tf_op jit(solution)/shard_map/pallas_call | solution.py:218
  315.8 10.2 %shard_map.372 = bf16[16,160,384]{2,1,0:T(8,128)(2,1)} custom-call(s32[17]{0:T(128)} %pad_add_fusion.1.info, f32[16,384]{1,0:T(8,128)} %dynamic-slice_add_fusion.small, bf16[1024,768]{1,0:T(8,128)(2,1)} %broadcast_select_fusion.1.t_own.tok, bf16[1024,768]{1,0:T(8,128)(2,1)} %collective-permute-done.8.t_got, bf16[2048,384]{1,0:T(8,128)(2,1)} %get-tuple-element.176.dq.refs_1_, ...), custom_call_target="tpu_custom_call" | custom-call | flops 3623878656 | bytes 7864320 | tf_op jit(solution)/shard_map/pallas_call | solution.py:593
  328.3 6.0 %shard_map.373 = bf16[1024,768]{1,0:T(8,128)(2,1)} custom-call(bf16[768,1152]{1,0:T(8,128)(2,1)} %get-tuple-element.179.refs_0_, bf16[2048,384]{1,0:T(8,128)(2,1)} %get-tuple-element.176.dq.refs_1_, bf16[2048,384]{1,0:T(8,128)(2,1)} %get-tuple-element.177.dk.refs_2_, bf16[2048,384]{1,0:T(8,128)(2,1)} %get-tuple-element.178.dv.refs_3_), custom_call_target="tpu_custom_call" | custom-call | flops 1811939328 | bytes 6291456 | tf_op jit(solution)/shard_map/pallas_call | solution.py:633
  334.3 3.1 collective-permute-start.39
  342.2 7.0 %shard_map.374 = bf16[1024,768]{1,0:T(8,128)(2,1)} custom-call(bf16[768,1152]{1,0:T(8,128)(2,1)} %get-tuple-element.179.refs_0_, bf16[2048,384]{1,0:T(8,128)(2,1)} %get-tuple-element.176.dq.refs_1_, bf16[2048,384]{1,0:T(8,128)(2,1)} %get-tuple-element.177.dk.refs_2_, bf16[2048,384]{1,0:T(8,128)(2,1)} %get-tuple-element.178.dv.refs_3_, ...), custom_call_target="tpu_custom_call" | custom-call | flops 1811939328 | bytes 6291456 | tf_op jit(solution)/shard_map/pallas_call | solution.py:633
  353.0 3.5 collective-permute-start.40
  360.5 2.6 collective-permute-done.43
  363.1 8.4 %collective-permute-done.42 = bf16[160,384]{1,0:T(8,128)(2,1)S(1)} collective-permute-done((bf16[160,384]{1,0:T(8,128)(2,1)S(1)}, bf16[160,384]{1,0:T(8,128)(2,1)S(1)}, u32[]{:S(2)}, u32[]{:S(2)}) %collective-permute-start.42) | collective-permute-done | bytes 122912 | tf_op jit(solution)/shard_map/ppermute | solution.py:696
  371.6 3.5 collective-permute-done.40
  378.4 2.8 select_bitcast_fusion
  (234 shorter events, 76.2 us)
Async XLA Ops:
  11.1 25.4 %collective-permute-start = (bf16[1024,768]{1,0:T(8,128)(2,1)}, bf16[1024,768]{1,0:T(8,128)(2,1)}, u32[]{:S(2)}, u32[]{:S(2)}) collective-permute-start(bf16[1024,768]{1,0:T(8,128)(2,1)} %bitcast.120), channel_id=1, source_target_pairs={{1,16},{16,1},{3,18},{18,3},{5,20},{20,5},{7,22},{22,7},{9,24},{24... | collective-permute-start | bytes 4718600 | tf_op jit(solution)/shard_map/ppermute | solution.py:739
  23.0 11.2 %collective-permute-start.3 = (bf16[168,384]{1,0:T(8,128)(2,1)}, bf16[168,384]{1,0:T(8,128)(2,1)S(1)}, u32[]{:S(2)}, u32[]{:S(2)}) collective-permute-start(bf16[168,384]{1,0:T(8,128)(2,1)} %bitcast.124), channel_id=1, source_target_pairs={{0,8},{4,12},{8,0},{12,4},{1,9},{5,13},{9,1},{13,5},{2,10},{6,14},... | collective-permute-start | bytes 387080 | tf_op jit(solution)/shard_map/ppermute | solution.py:696
  35.2 13.1 %collective-permute-start.10 = (bf16[4,168,384]{2,1,0:T(8,128)(2,1)S(1)}, bf16[4,168,384]{2,1,0:T(8,128)(2,1)S(1)}, u32[]{:S(2)}, u32[]{:S(2)}) collective-permute-start(bf16[4,168,384]{2,1,0:T(8,128)(2,1)S(1)} %pad_maximum_fusion.5.refs_0_), channel_id=1, source_target_pairs={{0,2},{2,0},{1,3},{3,1},{4,6},{6,4},{5,7},{7,5},{8,10},{10,8},{9,1... | collective-permute-start | bytes 1548296 | tf_op jit(solution)/shard_map/ppermute | solution.py:696
  36.5 12.7 %collective-permute-start.9 = (bf16[4,168,384]{2,1,0:T(8,128)(2,1)S(1)}, bf16[4,168,384]{2,1,0:T(8,128)(2,1)S(1)}, u32[]{:S(2)}, u32[]{:S(2)}) collective-permute-start(bf16[4,168,384]{2,1,0:T(8,128)(2,1)S(1)} %pad_maximum_fusion.5.refs_0_), channel_id=1, source_target_pairs={{0,16},{16,0},{1,17},{17,1},{2,18},{18,2},{3,19},{19,3},{4,20},{20... | collective-permute-start | bytes 1548296 | tf_op jit(solution)/shard_map/ppermute | solution.py:696
  39.3 24.8 %collective-permute-start.8 = (bf16[1024,768]{1,0:T(8,128)(2,1)}, bf16[1024,768]{1,0:T(8,128)(2,1)}, u32[]{:S(2)}, u32[]{:S(2)}) collective-permute-start(bf16[1024,768]{1,0:T(8,128)(2,1)} %broadcast_select_fusion.1.t_own.tok), channel_id=1, source_target_pairs={{0,1},{1,0},{2,3},{3,2},{4,5},{5,4},{6,7},{7,6},{8,9},{9,8},{10,11... | collective-permute-start | bytes 4718600 | tf_op jit(solution)/shard_map/ppermute | solution.py:735
  39.4 35.8 %collective-permute-start.7 = (bf16[432,384]{1,0:T(8,128)(2,1)}, bf16[432,384]{1,0:T(8,128)(2,1)}, u32[]{:S(2)}, u32[]{:S(2)}) collective-permute-start(bf16[432,384]{1,0:T(8,128)(2,1)} %bitcast.20), channel_id=1, source_target_pairs={{0,12},{4,0},{8,4},{12,8},{1,13},{5,1},{9,5},{13,9},{2,14},{6,2},{... | collective-permute-start | bytes 995336 | tf_op jit(solution)/shard_map/ppermute | solution.py:696
  40.8 34.4 %collective-permute-start.6 = (bf16[432,384]{1,0:T(8,128)(2,1)}, bf16[432,384]{1,0:T(8,128)(2,1)}, u32[]{:S(2)}, u32[]{:S(2)}) collective-permute-start(bf16[432,384]{1,0:T(8,128)(2,1)} %bitcast.20), channel_id=1, source_target_pairs={{0,8},{4,12},{8,0},{12,4},{1,9},{5,13},{9,1},{13,5},{2,10},{6,14},... | collective-permute-start | bytes 995336 | tf_op jit(solution)/shard_map/ppermute | solution.py:696
  55.8 19.4 %collective-permute-start.5 = (bf16[432,384]{1,0:T(8,128)(2,1)}, bf16[432,384]{1,0:T(8,128)(2,1)}, u32[]{:S(2)}, u32[]{:S(2)}) collective-permute-start(bf16[432,384]{1,0:T(8,128)(2,1)} %bitcast.20), channel_id=1, source_target_pairs={{0,4},{4,8},{8,12},{12,0},{1,5},{5,9},{9,13},{13,1},{2,6},{6,10},{... | collective-permute-start | bytes 995336 | tf_op jit(solution)/shard_map/ppermute | solution.py:696
  57.4 47.4 %collective-permute-start.15 = (bf16[1024,768]{1,0:T(8,128)(2,1)S(1)}, bf16[1024,768]{1,0:T(8,128)(2,1)S(1)}, u32[]{:S(2)}, u32[]{:S(2)}) collective-permute-start(bf16[1024,768]{1,0:T(8,128)(2,1)S(1)} %bitcast.121), channel_id=1, source_target_pairs={{1,16},{16,1},{3,18},{18,3},{5,20},{20,5},{7,22},{22,7},{9,24},{24... | collective-permute-start | bytes 4718600 | tf_op jit(solution)/shard_map/ppermute | solution.py:739
  76.7 52.1 %collective-permute-start.19 = (bf16[4,432,384]{2,1,0:T(8,128)(2,1)S(1)}, bf16[4,432,384]{2,1,0:T(8,128)(2,1)}, u32[]{:S(2)}, u32[]{:S(2)}) collective-permute-start(bf16[4,432,384]{2,1,0:T(8,128)(2,1)S(1)} %pad_maximum_fusion.refs_0_), channel_id=1, source_target_pairs={{0,1},{1,0},{2,3},{3,2},{4,5},{5,4},{6,7},{7,6},{8,9},{9,8},{10,11... | collective-permute-start | bytes 3981320 | tf_op jit(solution)/shard_map/ppermute | solution.py:735
  76.8 30.4 %collective-permute-start.14 = (bf16[4,432,384]{2,1,0:T(8,128)(2,1)S(1)}, bf16[4,432,384]{2,1,0:T(8,128)(2,1)}, u32[]{:S(2)}, u32[]{:S(2)}) collective-permute-start(bf16[4,432,384]{2,1,0:T(8,128)(2,1)S(1)} %pad_maximum_fusion.refs_0_), channel_id=1, source_target_pairs={{0,2},{2,0},{1,3},{3,1},{4,6},{6,4},{5,7},{7,5},{8,10},{10,8},{9,1... | collective-permute-start | bytes 3981320 | tf_op jit(solution)/shard_map/ppermute | solution.py:696
  77.1 30.1 %collective-permute-start.13 = (bf16[4,432,384]{2,1,0:T(8,128)(2,1)S(1)}, bf16[4,432,384]{2,1,0:T(8,128)(2,1)S(1)}, u32[]{:S(2)}, u32[]{:S(2)}) collective-permute-start(bf16[4,432,384]{2,1,0:T(8,128)(2,1)S(1)} %pad_maximum_fusion.refs_0_), channel_id=1, source_target_pairs={{0,16},{16,0},{1,17},{17,1},{2,18},{18,2},{3,19},{19,3},{4,20},{20... | collective-permute-start | bytes 3981320 | tf_op jit(solution)/shard_map/ppermute | solution.py:696
  109.4 26.5 %collective-permute-start.20 = (bf16[4,432,384]{2,1,0:T(8,128)(2,1)}, bf16[4,432,384]{2,1,0:T(8,128)(2,1)}, u32[]{:S(2)}, u32[]{:S(2)}) collective-permute-start(bf16[4,432,384]{2,1,0:T(8,128)(2,1)} %copy-done.17), channel_id=1, source_target_pairs={{0,1},{1,0},{2,3},{3,2},{4,5},{5,4},{6,7},{7,6},{8,9},{9,8},{10,11... | collective-permute-start | bytes 3981320 | tf_op jit(solution)/shard_map/ppermute | solution.py:735
  112.1 23.8 %collective-permute-start.21 = (bf16[4,432,384]{2,1,0:T(8,128)(2,1)}, bf16[4,432,384]{2,1,0:T(8,128)(2,1)}, u32[]{:S(2)}, u32[]{:S(2)}) collective-permute-start(bf16[4,432,384]{2,1,0:T(8,128)(2,1)} %collective-permute-done.14.refs_2_), channel_id=1, source_target_pairs={{0,1},{1,0},{2,3},{3,2},{4,5},{5,4},{6,7},{7,6},{8,9},{9,8},{10,11... | collective-permute-start | bytes 3981320 | tf_op jit(solution)/shard_map/ppermute | solution.py:735
  112.2 17.7 %collective-permute-start.17 = (bf16[2,432,384]{2,1,0:T(8,128)(2,1)S(1)}, bf16[2,432,384]{2,1,0:T(8,128)(2,1)}, u32[]{:S(2)}, u32[]{:S(2)}) collective-permute-start(bf16[2,432,384]{2,1,0:T(8,128)(2,1)S(1)} %slice.318), channel_id=1, source_target_pairs={{0,16},{16,0},{1,17},{17,1},{2,18},{18,2},{3,19},{19,3},{4,20},{20... | collective-permute-start | bytes 1990664 | tf_op jit(solution)/shard_map/ppermute | solution.py:696
  113.2 16.8 %collective-permute-start.18 = (bf16[2,432,384]{2,1,0:T(8,128)(2,1)S(1)}, bf16[2,432,384]{2,1,0:T(8,128)(2,1)}, u32[]{:S(2)}, u32[]{:S(2)}) collective-permute-start(bf16[2,432,384]{2,1,0:T(8,128)(2,1)S(1)} %slice.319), channel_id=1, source_target_pairs={{0,2},{2,0},{1,3},{3,1},{4,6},{6,4},{5,7},{7,5},{8,10},{10,8},{9,1... | collective-permute-start | bytes 1990664 | tf_op jit(solution)/shard_map/ppermute | solution.py:696
  190.4 18.2 %collective-permute-start.24 = (bf16[16,432,384]{2,1,0:T(8,128)(2,1)}, bf16[16,432,384]{2,1,0:T(8,128)(2,1)}, u32[]{:S(2)}, u32[]{:S(2)}) collective-permute-start(bf16[16,432,384]{2,1,0:T(8,128)(2,1)} %shard_map.367), channel_id=1, source_target_pairs={{0,1},{1,0},{2,3},{3,2},{4,5},{5,4},{6,7},{7,6},{8,9},{9,8},{10,11... | collective-permute-start | bytes 15925256 | tf_op jit(solution)/shard_map/ppermute | solution.py:735
  190.5 21.7 %collective-permute-start.25 = (bf16[1024,768]{1,0:T(8,128)(2,1)S(1)}, bf16[1024,768]{1,0:T(8,128)(2,1)S(1)}, u32[]{:S(2)}, u32[]{:S(2)}) collective-permute-start(bf16[1024,768]{1,0:T(8,128)(2,1)S(1)} %copy-done.5), channel_id=1, source_target_pairs={{1,16},{16,1},{3,18},{18,3},{5,20},{20,5},{7,22},{22,7},{9,24},{24... | collective-permute-start | bytes 4718600 | tf_op jit(solution)/shard_map/ppermute | solution.py:739
  193.5 49.4 %collective-permute-start.28 = (f32[16,384]{1,0:T(8,128)S(1)}, f32[16,384]{1,0:T(8,128)S(1)}, u32[]{:S(2)}, u32[]{:S(2)}) collective-permute-start(f32[16,384]{1,0:T(8,128)S(1)} %constant_dynamic-slice_fusion), channel_id=1, source_target_pairs={{0,1},{1,0},{2,3},{3,2},{4,5},{5,4},{6,7},{7,6},{8,9},{9,8},{10,11... | collective-permute-start | bytes 73736 | tf_op jit(solution)/shard_map/ppermute | solution.py:735
  193.6 19.4 %collective-permute-start.29 = (bf16[1024,384]{1,0:T(8,128)(2,1)}, bf16[1024,384]{1,0:T(8,128)(2,1)S(1)}, u32[]{:S(2)}, u32[]{:S(2)}) collective-permute-start(bf16[1024,384]{1,0:T(8,128)(2,1)} %get-tuple-element.145), channel_id=1, source_target_pairs={{0,1},{1,0},{2,3},{3,2},{4,5},{5,4},{6,7},{7,6},{8,9},{9,8},{10,11... | collective-permute-start | bytes 2359304 | tf_op jit(solution)/shard_map/ppermute | solution.py:735
  212.2 30.8 %collective-permute-start.26 = (bf16[2,432,384]{2,1,0:T(8,128)(2,1)}, bf16[2,432,384]{2,1,0:T(8,128)(2,1)S(1)}, u32[]{:S(2)}, u32[]{:S(2)}) collective-permute-start(bf16[2,432,384]{2,1,0:T(8,128)(2,1)} %get-tuple-element.141), channel_id=1, source_target_pairs={{0,16},{16,0},{1,17},{17,1},{2,18},{18,2},{3,19},{19,3},{4,20},{20... | collective-permute-start | bytes 1990664 | tf_op jit(solution)/shard_map/ppermute | solution.py:696
  212.2 30.8 %collective-permute-start.27 = (bf16[2,432,384]{2,1,0:T(8,128)(2,1)}, bf16[2,432,384]{2,1,0:T(8,128)(2,1)}, u32[]{:S(2)}, u32[]{:S(2)}) collective-permute-start(bf16[2,432,384]{2,1,0:T(8,128)(2,1)} %get-tuple-element.142), channel_id=1, source_target_pairs={{0,2},{2,0},{1,3},{3,1},{4,6},{6,4},{5,7},{7,5},{8,10},{10,8},{9,1... | collective-permute-start | bytes 1990664 | tf_op jit(solution)/shard_map/ppermute | solution.py:696
  248.8 30.2 %collective-permute-start.30 = (bf16[4,432,384]{2,1,0:T(8,128)(2,1)}, bf16[4,432,384]{2,1,0:T(8,128)(2,1)}, u32[]{:S(2)}, u32[]{:S(2)}) collective-permute-start(bf16[4,432,384]{2,1,0:T(8,128)(2,1)} %pad_maximum_fusion.1), channel_id=1, source_target_pairs={{0,16},{16,0},{1,17},{17,1},{2,18},{18,2},{3,19},{19,3},{4,20},{20... | collective-permute-start | bytes 3981320 | tf_op jit(solution)/shard_map/ppermute | solution.py:696
  250.0 30.6 %collective-permute-start.31 = (bf16[4,432,384]{2,1,0:T(8,128)(2,1)}, bf16[4,432,384]{2,1,0:T(8,128)(2,1)}, u32[]{:S(2)}, u32[]{:S(2)}) collective-permute-start(bf16[4,432,384]{2,1,0:T(8,128)(2,1)} %pad_maximum_fusion.2), channel_id=1, source_target_pairs={{0,2},{2,0},{1,3},{3,1},{4,6},{6,4},{5,7},{7,5},{8,10},{10,8},{9,1... | collective-permute-start | bytes 3981320 | tf_op jit(solution)/shard_map/ppermute | solution.py:696
  283.6 32.2 %collective-permute-start.34 = (bf16[432,384]{1,0:T(8,128)(2,1)S(1)}, bf16[432,384]{1,0:T(8,128)(2,1)S(1)}, u32[]{:S(2)}, u32[]{:S(2)}) collective-permute-start(bf16[432,384]{1,0:T(8,128)(2,1)S(1)} %get-tuple-element.209), channel_id=1, source_target_pairs={{0,12},{4,0},{8,4},{12,8},{1,13},{5,1},{9,5},{13,9},{2,14},{6,2},{... | collective-permute-start | bytes 995336 | tf_op jit(solution)/shard_map/ppermute | solution.py:696
  285.6 30.2 %collective-permute-start.33 = (bf16[432,384]{1,0:T(8,128)(2,1)S(1)}, bf16[432,384]{1,0:T(8,128)(2,1)S(1)}, u32[]{:S(2)}, u32[]{:S(2)}) collective-permute-start(bf16[432,384]{1,0:T(8,128)(2,1)S(1)} %get-tuple-element.210), channel_id=1, source_target_pairs={{0,8},{4,12},{8,0},{12,4},{1,9},{5,13},{9,1},{13,5},{2,10},{6,14},... | collective-permute-start | bytes 995336 | tf_op jit(solution)/shard_map/ppermute | solution.py:696
  286.2 29.6 %collective-permute-start.32 = (bf16[432,384]{1,0:T(8,128)(2,1)S(1)}, bf16[432,384]{1,0:T(8,128)(2,1)S(1)}, u32[]{:S(2)}, u32[]{:S(2)}) collective-permute-start(bf16[432,384]{1,0:T(8,128)(2,1)S(1)} %get-tuple-element.211), channel_id=1, source_target_pairs={{0,4},{4,8},{8,12},{12,0},{1,5},{5,9},{9,13},{13,1},{2,6},{6,10},{... | collective-permute-start | bytes 995336 | tf_op jit(solution)/shard_map/ppermute | solution.py:696
  338.4 13.1 %collective-permute-start.37 = (bf16[4,160,384]{2,1,0:T(8,128)(2,1)}, bf16[4,160,384]{2,1,0:T(8,128)(2,1)S(1)}, u32[]{:S(2)}, u32[]{:S(2)}) collective-permute-start(bf16[4,160,384]{2,1,0:T(8,128)(2,1)} %pad_maximum_fusion.6), channel_id=1, source_target_pairs={{0,16},{16,0},{1,17},{17,1},{2,18},{18,2},{3,19},{19,3},{4,20},{20... | collective-permute-start | bytes 1474568 | tf_op jit(solution)/shard_map/ppermute | solution.py:696
  340.2 12.8 %collective-permute-start.38 = (bf16[4,160,384]{2,1,0:T(8,128)(2,1)}, bf16[4,160,384]{2,1,0:T(8,128)(2,1)}, u32[]{:S(2)}, u32[]{:S(2)}) collective-permute-start(bf16[4,160,384]{2,1,0:T(8,128)(2,1)} %pad_maximum_fusion.7), channel_id=1, source_target_pairs={{0,2},{2,0},{1,3},{3,1},{4,6},{6,4},{5,7},{7,5},{8,10},{10,8},{9,1... | collective-permute-start | bytes 1474568 | tf_op jit(solution)/shard_map/ppermute | solution.py:696
  353.0 22.0 %collective-permute-start.40 = (bf16[1024,768]{1,0:T(8,128)(2,1)}, bf16[1024,768]{1,0:T(8,128)(2,1)}, u32[]{:S(2)}, u32[]{:S(2)}) collective-permute-start(bf16[1024,768]{1,0:T(8,128)(2,1)} %shard_map.374), channel_id=1, source_target_pairs={{1,16},{16,1},{3,18},{18,3},{5,20},{20,5},{7,22},{22,7},{9,24},{24... | collective-permute-start | bytes 4718600 | tf_op jit(solution)/shard_map/ppermute | solution.py:739
  359.9 11.6 %collective-permute-start.42 = (bf16[160,384]{1,0:T(8,128)(2,1)S(1)}, bf16[160,384]{1,0:T(8,128)(2,1)S(1)}, u32[]{:S(2)}, u32[]{:S(2)}) collective-permute-start(bf16[160,384]{1,0:T(8,128)(2,1)S(1)} %get-tuple-element.229), channel_id=1, source_target_pairs={{0,8},{4,12},{8,0},{12,4},{1,9},{5,13},{9,1},{13,5},{2,10},{6,14},... | collective-permute-start | bytes 368648 | tf_op jit(solution)/shard_map/ppermute | solution.py:696
  359.9 11.6 %collective-permute-start.41 = (bf16[160,384]{1,0:T(8,128)(2,1)S(1)}, bf16[160,384]{1,0:T(8,128)(2,1)S(1)}, u32[]{:S(2)}, u32[]{:S(2)}) collective-permute-start(bf16[160,384]{1,0:T(8,128)(2,1)S(1)} %get-tuple-element.230), channel_id=1, source_target_pairs={{0,4},{4,8},{8,12},{12,0},{1,5},{5,9},{9,13},{13,1},{2,6},{6,10},{... | collective-permute-start | bytes 368648 | tf_op jit(solution)/shard_map/ppermute | solution.py:696
  (41 other events, 374.4 us)
